TPU v7x, 128 devices: a whole 4x4x4 slice. The times are simulated.
128 devices in a mesh: rows: 128 (over z, y, x, core).
Axes of the slice: x: 4, y: 4, z: 4, core: 2. Of those that a mesh axis runs over, the one named last changes fastest.
Arguments:
- right_sides: float32 [8, 128, 128, 64], P(None, 'rows'), may hold values from -6 to 6
- lower_tiles: bfloat16 [8, 128, 16, 128, 128], P(None, 'rows'), may hold values from -0.0625 to 0.0625
- diag_inverse: bfloat16 [8, 128, 128, 128], P(None, 'rows'), may hold values from -1.5 to 1.5, as said below
- tile_columns: int32 [8, 128, 16], P(None, 'rows'), may hold values from 0 to 1023, as said below
- tile_counts: int32 [8, 128], P(None, 'rows'), may hold values from 0 to 16, as said below
- level_sets: int32 [8, 128], replicated, may hold values from 0 to 15, as said below
Outputs:
- solution: bfloat16 [8, 128, 128, 64], P(None, 'rows')
Inputs may be any that keep to these rules, and one draw needn't show every extreme that they name: `level_sets`: the block rows of one device (one index d) have pairwise different levels; every level from 0 to 15 has block rows. For k < tile_counts of block row g, tile_columns names a block row of a lower level than g's, and slot 0 names one of level exactly one lower; slots from tile_counts on name arbitrary block rows. `tile_counts`: zero exactly for the block rows of level 0. `diag_inverse`: each tile is the inverse of a diagonal tile of the factor.
All inputs are finite; a program needn't handle non-finite values.
Results may differ from a plain program's by a relative error of at most 0.0053.
Values may be sent and summed in bfloat16 or wider, within the bound.
No kernel may reach another device: no remote copies, remote signals or barrier semaphores. Data moves between devices by JAX's collectives and lax.ppermute only.
A program may use at most 64 MiB of HBM per device.

v0:
```python
import jax
import jax.numpy as jnp
from jax import lax
from jax.sharding import Mesh
from jax.sharding import PartitionSpec as P

LEVELS = 16
ROWS = ("rows_0", "rows_1", "rows_2", "rows_3")


def copy_for_each(value, axis):
    length = lax.axis_size(axis)
    return lax.all_to_all(
        jnp.broadcast_to(value[None], (length, *value.shape)), axis, 0, 0, tiled=True
    )


def laid_out(tiles, dim):
    tiles = jnp.moveaxis(tiles, 0, dim)
    lengths = tiles.shape
    return tiles.reshape(*lengths[:dim], lengths[dim] * lengths[dim + 1], *lengths[dim + 2 :])


def gathered_by_axis(value, axes, dim):
    far, near = axes
    tiles = copy_for_each(copy_for_each(value, far), near)
    return laid_out(tiles.swapaxes(0, 1).reshape(-1, *value.shape), dim)


def select_blocks(received, col_owner, col_level, in_use, level_now):
    needed = in_use & (col_level == level_now)
    fetched = received[col_owner]
    fetched = jnp.where(needed[..., None, None], fetched, jnp.zeros_like(fetched))
    return (needed, fetched)


def local(right_sides, lower_tiles, diag_inverse, tile_columns, tile_counts, level_sets):
    owners = lax.axis_size(ROWS)
    own_index = lax.axis_index(ROWS)
    rhs_local = right_sides[:, 0]
    tiles_local = lower_tiles[:, 0]
    inverse_local = diag_inverse[:, 0]
    columns_local = tile_columns[:, 0]
    counts_local = tile_counts[:, 0]
    width_k = columns_local.shape[1]
    flat_levels = level_sets.reshape(-1)
    own_levels = lax.dynamic_slice_in_dim(level_sets, own_index, 1, 1)[:, 0]
    col_level = flat_levels[columns_local]
    col_owner = columns_local % owners
    slot_range = jnp.arange(width_k, dtype=jnp.int32)
    in_use = slot_range[None, :] < counts_local[:, None]
    solution = jnp.zeros(rhs_local.shape, jnp.bfloat16)
    store = jnp.zeros(rhs_local.shape, jnp.float32)

    def row_update(held, slot):
        return held[slot]

    def absorb(held, fetched):
        return held + jnp.einsum(
            "skab,skbr->sar", tiles_local, fetched, preferred_element_type=jnp.float32
        )

    def finish(level_now, held, solution):
        chosen = own_levels == level_now
        slot = jnp.argmax(chosen.astype(jnp.int32))
        update = row_update(held, slot)
        rounded = (rhs_local[slot] - update).astype(jnp.bfloat16)
        solved = jnp.dot(inverse_local[slot], rounded, preferred_element_type=jnp.float32).astype(
            jnp.bfloat16
        )
        solution = jnp.where(chosen[:, None, None], solved[None], solution)
        present = jnp.any(chosen)
        solved_piece = jnp.where(present, solved, jnp.zeros_like(solved))
        block_id = slot * owners + own_index
        return (solution, solved_piece, block_id, present)

    def advance(level_now, carry):
        held, solution = carry
        solution, solved_piece, block_id, present = finish(level_now, held, solution)
        received = gathered_by_axis(
            solved_piece[None], (("rows_0", "rows_1", "rows_2"), "rows_3"), 0
        )
        needed, fetched = select_blocks(received, col_owner, col_level, in_use, level_now)
        return (absorb(held, fetched), solution)

    held, solution = lax.fori_loop(0, LEVELS - 1, advance, (store, solution))
    solution, unused, unused_id, unused_flag = finish(LEVELS - 1, held, solution)
    return solution[:, None]


def solution(mesh):
    finer = Mesh(mesh.devices.reshape(4, 4, 4, 2), ("rows_0", "rows_1", "rows_2", "rows_3"))
    return jax.shard_map(
        local,
        mesh=finer,
        in_specs=(
            P(None, ROWS, None, None),
            P(None, ROWS, None, None, None),
            P(None, ROWS, None, None),
            P(None, ROWS, None),
            P(None, ROWS),
            P(),
        ),
        out_specs=P(None, ROWS, None, None),
        check_vma=False,
    )
```

profile of v0, /device:TPU:1, one launch (start us, length us, event | category | flops | bytes accessed | tf_op | source)
XLA Modules:
  0.0 656.0 jit_solution(10785920177373101226)
XLA Ops:
  5.2 649.0 %while.16 = (s32[]{:T(128)}, f32[8,128,64]{1,2,0:T(8,128)S(1)}, bf16[8,128,64]{2,1,0:T(8,128)(2,1)S(1)}, s32[8,16]{1,0:T(8,128)S(1)}, s32[8]{0:T(128)S(1)}, /*in...) while((s32[]{:T(128)}, f32[8,128,64]{1,2,0:T(8,128)S(1)}, ...), condition=%wide.region_4.5_spmd.clone, body=%wide.region_1.4_spmd.clone.sunk | while | flops 271877952 | bytes 27731512 | solution.py:86
  11.1 12.0 %all-to-all-start = ((bf16[64,1,128,64]{2,3,1,0:T(8,128)(2,1)}), bf16[64,1,128,64]{2,3,1,0:T(8,128)(2,1)S(1)}, u32[]{:S(2)}, u32[]{:S(2)}) async-start(bf16[64,1,128,64]{2,3,1,0:T(8,128)(2,1)} %broadcast_in_dim.152), calls=%async_computation | async-start | bytes 2097152 | tf_op jit(solution)/shard_map/while/body/eval_jaxpr/all_to_all | solution.py:13
  23.5 17.3 %all-to-all-done = bf16[64,1,128,64]{2,3,1,0:T(8,128)(2,1)S(1)} async-done(((bf16[64,1,128,64]{2,3,1,0:T(8,128)(2,1)}), bf16[64,1,128,64]{2,3,1,0:T(8,128)(2,1)S(1)}, u32[]{:S(2)}, u32[]{:S(2)}) %all-to-all-start) | async-done | bytes 1048608 | tf_op jit(solution)/shard_map/while/body/eval_jaxpr/all_to_all | solution.py:13
  41.3 7.2 %all_to_all.22 = bf16[2,64,1,128,64]{3,4,2,1,0:T(8,128)(2,1)S(1)} all-to-all(bf16[2,64,1,128,64]{3,4,2,1,0:T(8,128)(2,1)S(1)} %broadcast_in_dim.153), channel_id=1, replica_groups=mesh['rows_0'=4,'rows_1'=4,'rows_2'=4,'rows_3'=2] {'rows_3'}, dimensions={0} | all-to-all | bytes 4194304 | tf_op jit(solution)/shard_map/while/body/eval_jaxpr/all_to_all | solution.py:13
  50.8 4.5 fusion.37
  61.2 4.7 all-to-all-start
  66.3 17.7 %all-to-all-done = bf16[64,1,128,64]{2,3,1,0:T(8,128)(2,1)S(1)} async-done(((bf16[64,1,128,64]{2,3,1,0:T(8,128)(2,1)}), bf16[64,1,128,64]{2,3,1,0:T(8,128)(2,1)S(1)}, u32[]{:S(2)}, u32[]{:S(2)}) %all-to-all-start) | async-done | bytes 1048608 | tf_op jit(solution)/shard_map/while/body/eval_jaxpr/all_to_all | solution.py:13
  84.5 6.7 %all_to_all.22 = bf16[2,64,1,128,64]{3,4,2,1,0:T(8,128)(2,1)S(1)} all-to-all(bf16[2,64,1,128,64]{3,4,2,1,0:T(8,128)(2,1)S(1)} %broadcast_in_dim.153), channel_id=1, replica_groups=mesh['rows_0'=4,'rows_1'=4,'rows_2'=4,'rows_3'=2] {'rows_3'}, dimensions={0} | all-to-all | bytes 4194304 | tf_op jit(solution)/shard_map/while/body/eval_jaxpr/all_to_all | solution.py:13
  93.6 4.5 fusion.37
  104.0 4.7 all-to-all-start
  109.0 17.7 %all-to-all-done = bf16[64,1,128,64]{2,3,1,0:T(8,128)(2,1)S(1)} async-done(((bf16[64,1,128,64]{2,3,1,0:T(8,128)(2,1)}), bf16[64,1,128,64]{2,3,1,0:T(8,128)(2,1)S(1)}, u32[]{:S(2)}, u32[]{:S(2)}) %all-to-all-start) | async-done | bytes 1048608 | tf_op jit(solution)/shard_map/while/body/eval_jaxpr/all_to_all | solution.py:13
  127.3 6.7 %all_to_all.22 = bf16[2,64,1,128,64]{3,4,2,1,0:T(8,128)(2,1)S(1)} all-to-all(bf16[2,64,1,128,64]{3,4,2,1,0:T(8,128)(2,1)S(1)} %broadcast_in_dim.153), channel_id=1, replica_groups=mesh['rows_0'=4,'rows_1'=4,'rows_2'=4,'rows_3'=2] {'rows_3'}, dimensions={0} | all-to-all | bytes 4194304 | tf_op jit(solution)/shard_map/while/body/eval_jaxpr/all_to_all | solution.py:13
  146.7 4.7 all-to-all-start
  151.8 17.7 %all-to-all-done = bf16[64,1,128,64]{2,3,1,0:T(8,128)(2,1)S(1)} async-done(((bf16[64,1,128,64]{2,3,1,0:T(8,128)(2,1)}), bf16[64,1,128,64]{2,3,1,0:T(8,128)(2,1)S(1)}, u32[]{:S(2)}, u32[]{:S(2)}) %all-to-all-start) | async-done | bytes 1048608 | tf_op jit(solution)/shard_map/while/body/eval_jaxpr/all_to_all | solution.py:13
  170.1 6.7 %all_to_all.22 = bf16[2,64,1,128,64]{3,4,2,1,0:T(8,128)(2,1)S(1)} all-to-all(bf16[2,64,1,128,64]{3,4,2,1,0:T(8,128)(2,1)S(1)} %broadcast_in_dim.153), channel_id=1, replica_groups=mesh['rows_0'=4,'rows_1'=4,'rows_2'=4,'rows_3'=2] {'rows_3'}, dimensions={0} | all-to-all | bytes 4194304 | tf_op jit(solution)/shard_map/while/body/eval_jaxpr/all_to_all | solution.py:13
  189.5 4.7 all-to-all-start
  194.6 17.7 %all-to-all-done = bf16[64,1,128,64]{2,3,1,0:T(8,128)(2,1)S(1)} async-done(((bf16[64,1,128,64]{2,3,1,0:T(8,128)(2,1)}), bf16[64,1,128,64]{2,3,1,0:T(8,128)(2,1)S(1)}, u32[]{:S(2)}, u32[]{:S(2)}) %all-to-all-start) | async-done | bytes 1048608 | tf_op jit(solution)/shard_map/while/body/eval_jaxpr/all_to_all | solution.py:13
  212.9 6.7 %all_to_all.22 = bf16[2,64,1,128,64]{3,4,2,1,0:T(8,128)(2,1)S(1)} all-to-all(bf16[2,64,1,128,64]{3,4,2,1,0:T(8,128)(2,1)S(1)} %broadcast_in_dim.153), channel_id=1, replica_groups=mesh['rows_0'=4,'rows_1'=4,'rows_2'=4,'rows_3'=2] {'rows_3'}, dimensions={0} | all-to-all | bytes 4194304 | tf_op jit(solution)/shard_map/while/body/eval_jaxpr/all_to_all | solution.py:13
  232.3 4.7 all-to-all-start
  237.4 17.7 %all-to-all-done = bf16[64,1,128,64]{2,3,1,0:T(8,128)(2,1)S(1)} async-done(((bf16[64,1,128,64]{2,3,1,0:T(8,128)(2,1)}), bf16[64,1,128,64]{2,3,1,0:T(8,128)(2,1)S(1)}, u32[]{:S(2)}, u32[]{:S(2)}) %all-to-all-start) | async-done | bytes 1048608 | tf_op jit(solution)/shard_map/while/body/eval_jaxpr/all_to_all | solution.py:13
  255.6 6.7 %all_to_all.22 = bf16[2,64,1,128,64]{3,4,2,1,0:T(8,128)(2,1)S(1)} all-to-all(bf16[2,64,1,128,64]{3,4,2,1,0:T(8,128)(2,1)S(1)} %broadcast_in_dim.153), channel_id=1, replica_groups=mesh['rows_0'=4,'rows_1'=4,'rows_2'=4,'rows_3'=2] {'rows_3'}, dimensions={0} | all-to-all | bytes 4194304 | tf_op jit(solution)/shard_map/while/body/eval_jaxpr/all_to_all | solution.py:13
  275.1 4.7 all-to-all-start
  280.2 17.7 %all-to-all-done = bf16[64,1,128,64]{2,3,1,0:T(8,128)(2,1)S(1)} async-done(((bf16[64,1,128,64]{2,3,1,0:T(8,128)(2,1)}), bf16[64,1,128,64]{2,3,1,0:T(8,128)(2,1)S(1)}, u32[]{:S(2)}, u32[]{:S(2)}) %all-to-all-start) | async-done | bytes 1048608 | tf_op jit(solution)/shard_map/while/body/eval_jaxpr/all_to_all | solution.py:13
  298.4 6.7 %all_to_all.22 = bf16[2,64,1,128,64]{3,4,2,1,0:T(8,128)(2,1)S(1)} all-to-all(bf16[2,64,1,128,64]{3,4,2,1,0:T(8,128)(2,1)S(1)} %broadcast_in_dim.153), channel_id=1, replica_groups=mesh['rows_0'=4,'rows_1'=4,'rows_2'=4,'rows_3'=2] {'rows_3'}, dimensions={0} | all-to-all | bytes 4194304 | tf_op jit(solution)/shard_map/while/body/eval_jaxpr/all_to_all | solution.py:13
  317.9 4.7 all-to-all-start
  322.9 17.7 %all-to-all-done = bf16[64,1,128,64]{2,3,1,0:T(8,128)(2,1)S(1)} async-done(((bf16[64,1,128,64]{2,3,1,0:T(8,128)(2,1)}), bf16[64,1,128,64]{2,3,1,0:T(8,128)(2,1)S(1)}, u32[]{:S(2)}, u32[]{:S(2)}) %all-to-all-start) | async-done | bytes 1048608 | tf_op jit(solution)/shard_map/while/body/eval_jaxpr/all_to_all | solution.py:13
  341.2 6.7 %all_to_all.22 = bf16[2,64,1,128,64]{3,4,2,1,0:T(8,128)(2,1)S(1)} all-to-all(bf16[2,64,1,128,64]{3,4,2,1,0:T(8,128)(2,1)S(1)} %broadcast_in_dim.153), channel_id=1, replica_groups=mesh['rows_0'=4,'rows_1'=4,'rows_2'=4,'rows_3'=2] {'rows_3'}, dimensions={0} | all-to-all | bytes 4194304 | tf_op jit(solution)/shard_map/while/body/eval_jaxpr/all_to_all | solution.py:13
  360.6 4.7 all-to-all-start
  365.7 17.7 %all-to-all-done = bf16[64,1,128,64]{2,3,1,0:T(8,128)(2,1)S(1)} async-done(((bf16[64,1,128,64]{2,3,1,0:T(8,128)(2,1)}), bf16[64,1,128,64]{2,3,1,0:T(8,128)(2,1)S(1)}, u32[]{:S(2)}, u32[]{:S(2)}) %all-to-all-start) | async-done | bytes 1048608 | tf_op jit(solution)/shard_map/while/body/eval_jaxpr/all_to_all | solution.py:13
  384.0 6.7 %all_to_all.22 = bf16[2,64,1,128,64]{3,4,2,1,0:T(8,128)(2,1)S(1)} all-to-all(bf16[2,64,1,128,64]{3,4,2,1,0:T(8,128)(2,1)S(1)} %broadcast_in_dim.153), channel_id=1, replica_groups=mesh['rows_0'=4,'rows_1'=4,'rows_2'=4,'rows_3'=2] {'rows_3'}, dimensions={0} | all-to-all | bytes 4194304 | tf_op jit(solution)/shard_map/while/body/eval_jaxpr/all_to_all | solution.py:13
  403.4 4.7 all-to-all-start
  408.5 17.7 %all-to-all-done = bf16[64,1,128,64]{2,3,1,0:T(8,128)(2,1)S(1)} async-done(((bf16[64,1,128,64]{2,3,1,0:T(8,128)(2,1)}), bf16[64,1,128,64]{2,3,1,0:T(8,128)(2,1)S(1)}, u32[]{:S(2)}, u32[]{:S(2)}) %all-to-all-start) | async-done | bytes 1048608 | tf_op jit(solution)/shard_map/while/body/eval_jaxpr/all_to_all | solution.py:13
  426.8 6.7 %all_to_all.22 = bf16[2,64,1,128,64]{3,4,2,1,0:T(8,128)(2,1)S(1)} all-to-all(bf16[2,64,1,128,64]{3,4,2,1,0:T(8,128)(2,1)S(1)} %broadcast_in_dim.153), channel_id=1, replica_groups=mesh['rows_0'=4,'rows_1'=4,'rows_2'=4,'rows_3'=2] {'rows_3'}, dimensions={0} | all-to-all | bytes 4194304 | tf_op jit(solution)/shard_map/while/body/eval_jaxpr/all_to_all | solution.py:13
  446.2 4.7 all-to-all-start
  451.3 17.7 %all-to-all-done = bf16[64,1,128,64]{2,3,1,0:T(8,128)(2,1)S(1)} async-done(((bf16[64,1,128,64]{2,3,1,0:T(8,128)(2,1)}), bf16[64,1,128,64]{2,3,1,0:T(8,128)(2,1)S(1)}, u32[]{:S(2)}, u32[]{:S(2)}) %all-to-all-start) | async-done | bytes 1048608 | tf_op jit(solution)/shard_map/while/body/eval_jaxpr/all_to_all | solution.py:13
  469.5 6.7 %all_to_all.22 = bf16[2,64,1,128,64]{3,4,2,1,0:T(8,128)(2,1)S(1)} all-to-all(bf16[2,64,1,128,64]{3,4,2,1,0:T(8,128)(2,1)S(1)} %broadcast_in_dim.153), channel_id=1, replica_groups=mesh['rows_0'=4,'rows_1'=4,'rows_2'=4,'rows_3'=2] {'rows_3'}, dimensions={0} | all-to-all | bytes 4194304 | tf_op jit(solution)/shard_map/while/body/eval_jaxpr/all_to_all | solution.py:13
  489.0 4.7 all-to-all-start
  494.1 17.7 %all-to-all-done = bf16[64,1,128,64]{2,3,1,0:T(8,128)(2,1)S(1)} async-done(((bf16[64,1,128,64]{2,3,1,0:T(8,128)(2,1)}), bf16[64,1,128,64]{2,3,1,0:T(8,128)(2,1)S(1)}, u32[]{:S(2)}, u32[]{:S(2)}) %all-to-all-start) | async-done | bytes 1048608 | tf_op jit(solution)/shard_map/while/body/eval_jaxpr/all_to_all | solution.py:13
  512.3 6.7 %all_to_all.22 = bf16[2,64,1,128,64]{3,4,2,1,0:T(8,128)(2,1)S(1)} all-to-all(bf16[2,64,1,128,64]{3,4,2,1,0:T(8,128)(2,1)S(1)} %broadcast_in_dim.153), channel_id=1, replica_groups=mesh['rows_0'=4,'rows_1'=4,'rows_2'=4,'rows_3'=2] {'rows_3'}, dimensions={0} | all-to-all | bytes 4194304 | tf_op jit(solution)/shard_map/while/body/eval_jaxpr/all_to_all | solution.py:13
  531.8 4.7 all-to-all-start
  536.8 17.7 %all-to-all-done = bf16[64,1,128,64]{2,3,1,0:T(8,128)(2,1)S(1)} async-done(((bf16[64,1,128,64]{2,3,1,0:T(8,128)(2,1)}), bf16[64,1,128,64]{2,3,1,0:T(8,128)(2,1)S(1)}, u32[]{:S(2)}, u32[]{:S(2)}) %all-to-all-start) | async-done | bytes 1048608 | tf_op jit(solution)/shard_map/while/body/eval_jaxpr/all_to_all | solution.py:13
  555.1 6.7 %all_to_all.22 = bf16[2,64,1,128,64]{3,4,2,1,0:T(8,128)(2,1)S(1)} all-to-all(bf16[2,64,1,128,64]{3,4,2,1,0:T(8,128)(2,1)S(1)} %broadcast_in_dim.153), channel_id=1, replica_groups=mesh['rows_0'=4,'rows_1'=4,'rows_2'=4,'rows_3'=2] {'rows_3'}, dimensions={0} | all-to-all | bytes 4194304 | tf_op jit(solution)/shard_map/while/body/eval_jaxpr/all_to_all | solution.py:13
  574.5 4.7 all-to-all-start
  579.6 17.7 %all-to-all-done = bf16[64,1,128,64]{2,3,1,0:T(8,128)(2,1)S(1)} async-done(((bf16[64,1,128,64]{2,3,1,0:T(8,128)(2,1)}), bf16[64,1,128,64]{2,3,1,0:T(8,128)(2,1)S(1)}, u32[]{:S(2)}, u32[]{:S(2)}) %all-to-all-start) | async-done | bytes 1048608 | tf_op jit(solution)/shard_map/while/body/eval_jaxpr/all_to_all | solution.py:13
  597.9 6.7 %all_to_all.22 = bf16[2,64,1,128,64]{3,4,2,1,0:T(8,128)(2,1)S(1)} all-to-all(bf16[2,64,1,128,64]{3,4,2,1,0:T(8,128)(2,1)S(1)} %broadcast_in_dim.153), channel_id=1, replica_groups=mesh['rows_0'=4,'rows_1'=4,'rows_2'=4,'rows_3'=2] {'rows_3'}, dimensions={0} | all-to-all | bytes 4194304 | tf_op jit(solution)/shard_map/while/body/eval_jaxpr/all_to_all | solution.py:13
  617.3 4.7 all-to-all-start
  622.4 17.7 %all-to-all-done = bf16[64,1,128,64]{2,3,1,0:T(8,128)(2,1)S(1)} async-done(((bf16[64,1,128,64]{2,3,1,0:T(8,128)(2,1)}), bf16[64,1,128,64]{2,3,1,0:T(8,128)(2,1)S(1)}, u32[]{:S(2)}, u32[]{:S(2)}) %all-to-all-start) | async-done | bytes 1048608 | tf_op jit(solution)/shard_map/while/body/eval_jaxpr/all_to_all | solution.py:13
  640.6 6.7 %all_to_all.22 = bf16[2,64,1,128,64]{3,4,2,1,0:T(8,128)(2,1)S(1)} all-to-all(bf16[2,64,1,128,64]{3,4,2,1,0:T(8,128)(2,1)S(1)} %broadcast_in_dim.153), channel_id=1, replica_groups=mesh['rows_0'=4,'rows_1'=4,'rows_2'=4,'rows_3'=2] {'rows_3'}, dimensions={0} | all-to-all | bytes 4194304 | tf_op jit(solution)/shard_map/while/body/eval_jaxpr/all_to_all | solution.py:13
  (243 shorter events, 174.8 us)
Async XLA Ops:
  0.0 0.7 copy-start
  4.1 1.1 copy-start.1
  4.1 1.1 copy-start.2
  11.1 29.7 %all-to-all-start = ((bf16[64,1,128,64]{2,3,1,0:T(8,128)(2,1)}), bf16[64,1,128,64]{2,3,1,0:T(8,128)(2,1)S(1)}, u32[]{:S(2)}, u32[]{:S(2)}) async-start(bf16[64,1,128,64]{2,3,1,0:T(8,128)(2,1)} %broadcast_in_dim.152), calls=%async_computation | async-start | bytes 2097152 | tf_op jit(solution)/shard_map/while/body/eval_jaxpr/all_to_all | solution.py:13
  61.2 22.8 %all-to-all-start = ((bf16[64,1,128,64]{2,3,1,0:T(8,128)(2,1)}), bf16[64,1,128,64]{2,3,1,0:T(8,128)(2,1)S(1)}, u32[]{:S(2)}, u32[]{:S(2)}) async-start(bf16[64,1,128,64]{2,3,1,0:T(8,128)(2,1)} %broadcast_in_dim.152), calls=%async_computation | async-start | bytes 2097152 | tf_op jit(solution)/shard_map/while/body/eval_jaxpr/all_to_all | solution.py:13
  104.0 22.8 %all-to-all-start = ((bf16[64,1,128,64]{2,3,1,0:T(8,128)(2,1)}), bf16[64,1,128,64]{2,3,1,0:T(8,128)(2,1)S(1)}, u32[]{:S(2)}, u32[]{:S(2)}) async-start(bf16[64,1,128,64]{2,3,1,0:T(8,128)(2,1)} %broadcast_in_dim.152), calls=%async_computation | async-start | bytes 2097152 | tf_op jit(solution)/shard_map/while/body/eval_jaxpr/all_to_all | solution.py:13
  146.7 22.8 %all-to-all-start = ((bf16[64,1,128,64]{2,3,1,0:T(8,128)(2,1)}), bf16[64,1,128,64]{2,3,1,0:T(8,128)(2,1)S(1)}, u32[]{:S(2)}, u32[]{:S(2)}) async-start(bf16[64,1,128,64]{2,3,1,0:T(8,128)(2,1)} %broadcast_in_dim.152), calls=%async_computation | async-start | bytes 2097152 | tf_op jit(solution)/shard_map/while/body/eval_jaxpr/all_to_all | solution.py:13
  189.5 22.8 %all-to-all-start = ((bf16[64,1,128,64]{2,3,1,0:T(8,128)(2,1)}), bf16[64,1,128,64]{2,3,1,0:T(8,128)(2,1)S(1)}, u32[]{:S(2)}, u32[]{:S(2)}) async-start(bf16[64,1,128,64]{2,3,1,0:T(8,128)(2,1)} %broadcast_in_dim.152), calls=%async_computation | async-start | bytes 2097152 | tf_op jit(solution)/shard_map/while/body/eval_jaxpr/all_to_all | solution.py:13
  232.3 22.8 %all-to-all-start = ((bf16[64,1,128,64]{2,3,1,0:T(8,128)(2,1)}), bf16[64,1,128,64]{2,3,1,0:T(8,128)(2,1)S(1)}, u32[]{:S(2)}, u32[]{:S(2)}) async-start(bf16[64,1,128,64]{2,3,1,0:T(8,128)(2,1)} %broadcast_in_dim.152), calls=%async_computation | async-start | bytes 2097152 | tf_op jit(solution)/shard_map/while/body/eval_jaxpr/all_to_all | solution.py:13
  275.1 22.8 %all-to-all-start = ((bf16[64,1,128,64]{2,3,1,0:T(8,128)(2,1)}), bf16[64,1,128,64]{2,3,1,0:T(8,128)(2,1)S(1)}, u32[]{:S(2)}, u32[]{:S(2)}) async-start(bf16[64,1,128,64]{2,3,1,0:T(8,128)(2,1)} %broadcast_in_dim.152), calls=%async_computation | async-start | bytes 2097152 | tf_op jit(solution)/shard_map/while/body/eval_jaxpr/all_to_all | solution.py:13
  317.9 22.8 %all-to-all-start = ((bf16[64,1,128,64]{2,3,1,0:T(8,128)(2,1)}), bf16[64,1,128,64]{2,3,1,0:T(8,128)(2,1)S(1)}, u32[]{:S(2)}, u32[]{:S(2)}) async-start(bf16[64,1,128,64]{2,3,1,0:T(8,128)(2,1)} %broadcast_in_dim.152), calls=%async_computation | async-start | bytes 2097152 | tf_op jit(solution)/shard_map/while/body/eval_jaxpr/all_to_all | solution.py:13
  360.6 22.8 %all-to-all-start = ((bf16[64,1,128,64]{2,3,1,0:T(8,128)(2,1)}), bf16[64,1,128,64]{2,3,1,0:T(8,128)(2,1)S(1)}, u32[]{:S(2)}, u32[]{:S(2)}) async-start(bf16[64,1,128,64]{2,3,1,0:T(8,128)(2,1)} %broadcast_in_dim.152), calls=%async_computation | async-start | bytes 2097152 | tf_op jit(solution)/shard_map/while/body/eval_jaxpr/all_to_all | solution.py:13
  403.4 22.8 %all-to-all-start = ((bf16[64,1,128,64]{2,3,1,0:T(8,128)(2,1)}), bf16[64,1,128,64]{2,3,1,0:T(8,128)(2,1)S(1)}, u32[]{:S(2)}, u32[]{:S(2)}) async-start(bf16[64,1,128,64]{2,3,1,0:T(8,128)(2,1)} %broadcast_in_dim.152), calls=%async_computation | async-start | bytes 2097152 | tf_op jit(solution)/shard_map/while/body/eval_jaxpr/all_to_all | solution.py:13
  446.2 22.8 %all-to-all-start = ((bf16[64,1,128,64]{2,3,1,0:T(8,128)(2,1)}), bf16[64,1,128,64]{2,3,1,0:T(8,128)(2,1)S(1)}, u32[]{:S(2)}, u32[]{:S(2)}) async-start(bf16[64,1,128,64]{2,3,1,0:T(8,128)(2,1)} %broadcast_in_dim.152), calls=%async_computation | async-start | bytes 2097152 | tf_op jit(solution)/shard_map/while/body/eval_jaxpr/all_to_all | solution.py:13
  489.0 22.8 %all-to-all-start = ((bf16[64,1,128,64]{2,3,1,0:T(8,128)(2,1)}), bf16[64,1,128,64]{2,3,1,0:T(8,128)(2,1)S(1)}, u32[]{:S(2)}, u32[]{:S(2)}) async-start(bf16[64,1,128,64]{2,3,1,0:T(8,128)(2,1)} %broadcast_in_dim.152), calls=%async_computation | async-start | bytes 2097152 | tf_op jit(solution)/shard_map/while/body/eval_jaxpr/all_to_all | solution.py:13
  531.8 22.8 %all-to-all-start = ((bf16[64,1,128,64]{2,3,1,0:T(8,128)(2,1)}), bf16[64,1,128,64]{2,3,1,0:T(8,128)(2,1)S(1)}, u32[]{:S(2)}, u32[]{:S(2)}) async-start(bf16[64,1,128,64]{2,3,1,0:T(8,128)(2,1)} %broadcast_in_dim.152), calls=%async_computation | async-start | bytes 2097152 | tf_op jit(solution)/shard_map/while/body/eval_jaxpr/all_to_all | solution.py:13
  574.5 22.8 %all-to-all-start = ((bf16[64,1,128,64]{2,3,1,0:T(8,128)(2,1)}), bf16[64,1,128,64]{2,3,1,0:T(8,128)(2,1)S(1)}, u32[]{:S(2)}, u32[]{:S(2)}) async-start(bf16[64,1,128,64]{2,3,1,0:T(8,128)(2,1)} %broadcast_in_dim.152), calls=%async_computation | async-start | bytes 2097152 | tf_op jit(solution)/shard_map/while/body/eval_jaxpr/all_to_all | solution.py:13
  617.3 22.8 %all-to-all-start = ((bf16[64,1,128,64]{2,3,1,0:T(8,128)(2,1)}), bf16[64,1,128,64]{2,3,1,0:T(8,128)(2,1)S(1)}, u32[]{:S(2)}, u32[]{:S(2)}) async-start(bf16[64,1,128,64]{2,3,1,0:T(8,128)(2,1)} %broadcast_in_dim.152), calls=%async_computation | async-start | bytes 2097152 | tf_op jit(solution)/shard_map/while/body/eval_jaxpr/all_to_all | solution.py:13
where the time goes:
time: 660 us; the launch traced here: 656 us
  waiting for transfers between devices  266 us (40%)
  blocking collectives  102 us (15%)
  matrix products  91 us (14%)
  starting transfers between devices  77.1 us (12%)
  local copies, waits for them, and re-layouts  66.8 us (10%)
  loops' own time  26.4 us (4%)
  other arithmetic  25.9 us (4%)
    all_to_all x15, waiting for transfers between devices, copy_for_each(): lax.all_to_all(jnp.broadcast_to(value[None], (length, *value.shape)), axi...  266 us
    all_to_all x15, blocking collectives, copy_for_each(): lax.all_to_all(jnp.broadcast_to(value[None], (length, *value.shape)), axi...  102 us
    all_to_all x15, starting transfers between devices, copy_for_each(): lax.all_to_all(jnp.broadcast_to(value[None], (length, *value.shape)), axi...  77.1 us
    dot_general x15, matrix products, absorb(): jnp.einsum('skab,skbr->sar', tiles_local, fetched, preferred_element_type...  66.8 us
    gather x15, local copies, waits for them, and re-layouts, select_blocks(): fetched = received[col_owner]  32.5 us
    broadcast_in_dim x30, local copies, waits for them, and re-layouts, copy_for_each(): jnp.broadcast_to(value[None], (length, *value.shape))  26.7 us
    another operation x1, loops' own time, local(): held, solution = lax.fori_loop(0, LEVELS - 1, advance, (store, solution))  26.4 us
    dot_general x16, matrix products, finish(): jnp.dot(inverse_local[slot], rounded, preferred_element_type=jnp.float32)  24.2 us
  transfers between devices with their start and end apart: 15, of which 15 were waited for; matrix products, arithmetic and copies ran while one was open for 1% of the time, Pallas kernels for 0%

commit v1 on v0

v1 whole, which is shorter than its diff:
```python
import functools

import jax
import jax.numpy as jnp
from jax import lax
from jax.experimental import pallas as pl
from jax.experimental.pallas import tpu as pltpu
from jax.sharding import Mesh
from jax.sharding import PartitionSpec as P

LEVELS = 16
ROWS = ("rows_0", "rows_1", "rows_2", "rows_3")
CHIPS = ("rows_0", "rows_1", "rows_2")
CORE = "rows_3"
SWAP = ((0, 1), (1, 0))
MEMBERS = 2
KEYS = LEVELS * 2 * MEMBERS
RING = 8


def smem():
    return pl.BlockSpec(memory_space=pltpu.SMEM)


def vmem():
    return pl.BlockSpec(memory_space=pltpu.VMEM)


def anywhere():
    return pl.BlockSpec(memory_space=pl.ANY)


def bucket(level, urgent, member):
    return (level * 2 + (0 if urgent else 1)) * MEMBERS + member


def times_transposed(rows, tile):
    return lax.dot_general(
        rows, tile, (((1,), (1,)), ((), ())), preferred_element_type=jnp.float32
    )


def list_edges(owners, columns, counts, row_levels, levels, edges, starts, fill):
    members_rows = counts.shape[0] // MEMBERS
    width_k = columns.shape[0] // counts.shape[0]

    def clear(key, unused):
        fill[key] = 0
        return unused

    lax.fori_loop(0, KEYS, clear, 0)

    def key_of(row, slot):
        col = columns[row * width_k + slot]
        level = levels[col]
        late = jnp.where(row_levels[row] == level + 1, 0, 1)
        return col, (level * 2 + late) * MEMBERS + row // members_rows

    def count_row(row, unused):
        def count(slot, unused):
            col, key = key_of(row, slot)
            fill[key] = fill[key] + 1
            return unused

        return lax.fori_loop(0, counts[row], count, unused)

    lax.fori_loop(0, counts.shape[0], count_row, 0)

    def prefix(key, total):
        starts[key] = total
        here = fill[key]
        fill[key] = total
        return total + here

    starts[KEYS] = lax.fori_loop(0, KEYS, prefix, 0)

    def place_row(row, unused):
        def place(slot, unused):
            col, key = key_of(row, slot)
            at = fill[key]
            edges[at] = (row * width_k + slot) * owners + col % owners
            fill[key] = at + 1
            return unused

        return lax.fori_loop(0, counts[row], place, unused)

    lax.fori_loop(0, counts.shape[0], place_row, 0)


def solve_level(level, rows, width_k, owners, core, row_levels, *refs):
    if level:
        edges, starts, received, held, *refs = refs
    else:
        held, *refs = refs
    tiles, inverses = refs[:MEMBERS], refs[MEMBERS : 2 * MEMBERS]
    piece, tile_buf, inverse_buf, tile_sem, inverse_sem = refs[2 * MEMBERS :]

    picked = []
    for member in range(MEMBERS):
        row = jnp.int32(-1)
        for s in range(rows):
            row = jnp.where(row_levels[member * rows + s] == level, s, row)
        picked.append(row)

    def inverse_copy(member):
        return pltpu.make_async_copy(
            inverses[member].at[jnp.maximum(picked[member], 0)],
            inverse_buf.at[member],
            inverse_sem.at[member],
        )

    def tile_copy(member, first, i):
        code = edges[first + i] // owners - member * rows * width_k
        return pltpu.make_async_copy(
            tiles[member].at[code // width_k, code % width_k],
            tile_buf.at[member * width_k + i],
            tile_sem.at[member * width_k + i],
        )

    spans = []
    for member in range(MEMBERS):
        if level:
            first = starts[bucket(level - 1, True, member)]
            spans.append((first, starts[bucket(level - 1, True, member) + 1] - first))

            def begin(i, unused, member=member, first=first):
                tile_copy(member, first, i).start()
                return unused

            lax.fori_loop(0, spans[member][1], begin, 0)

        @pl.when(picked[member] >= 0)
        def _(member=member):
            inverse_copy(member).start()

    for member in range(MEMBERS):
        at = core[0] if member == 0 else 1 - core[0]

        @pl.when(picked[member] < 0)
        def _(at=at):
            piece[at] = jnp.zeros(piece.shape[1:], piece.dtype)

        @pl.when(picked[member] >= 0)
        def _(member=member, at=at):
            total = held[member * rows + picked[member]]
            if level:
                first, many = spans[member]

                def absorb(i, total):
                    tile_copy(member, first, i).wait()
                    block = received[edges[first + i] % owners]
                    return total - times_transposed(block, tile_buf[member * width_k + i])

                total = lax.fori_loop(0, many, absorb, total)
            inverse_copy(member).wait()
            solved = times_transposed(total.astype(jnp.bfloat16), inverse_buf[member])
            piece[at] = solved.astype(jnp.bfloat16)


def absorb_level(level, rows, width_k, owners, edges, starts, received, held_in, *refs):
    tiles, (held, tile_buf, tile_sem) = refs[:MEMBERS], refs[MEMBERS:]
    held[...] = held_in[...]
    for member in range(MEMBERS):
        first = starts[bucket(level - 1, False, member)]
        many = starts[bucket(level - 1, False, member) + 1] - first

        def tile_copy(i, member=member, first=first):
            code = edges[first + i] // owners - member * rows * width_k
            at = lax.rem(i, RING)
            return pltpu.make_async_copy(
                tiles[member].at[code // width_k, code % width_k],
                tile_buf.at[at],
                tile_sem.at[at],
            )

        def begin(i, unused, tile_copy=tile_copy):
            tile_copy(i).start()
            return unused

        lax.fori_loop(0, jnp.minimum(many, RING), begin, 0)

        def absorb(i, unused, tile_copy=tile_copy, first=first, many=many):
            tile_copy(i).wait()
            code = edges[first + i]
            row = code // (owners * width_k)
            given = times_transposed(received[code % owners], tile_buf[lax.rem(i, RING)])
            held[row] = held[row] - given

            @pl.when(i + RING < many)
            def _():
                tile_copy(i + RING).start()

            return unused

        lax.fori_loop(0, many, absorb, 0)


def local(right_sides, lower_tiles, diag_inverse, tile_columns, tile_counts, level_sets):
    owners = lax.axis_size(ROWS)
    chips = lax.axis_size(CHIPS)
    own_index = lax.axis_index(ROWS)
    core = lax.axis_index(CORE)
    rows, unused_one, width_k = tile_columns.shape
    part = right_sides.shape[3] // MEMBERS
    lanes = right_sides.shape[2]

    def swapped(value):
        return lax.ppermute(value, CORE, SWAP)

    rhs = jnp.swapaxes(right_sides[:, 0], 1, 2)
    rhs_mine = lax.dynamic_slice_in_dim(rhs, core * part, part, 1)
    rhs_theirs = swapped(lax.dynamic_slice_in_dim(rhs, (1 - core) * part, part, 1))
    held = jnp.concatenate([rhs_mine, rhs_theirs])
    inverses = (diag_inverse[:, 0], swapped(diag_inverse[:, 0]))
    tiles = (lower_tiles[:, 0], swapped(lower_tiles[:, 0]))
    columns = jnp.concatenate([tile_columns[:, 0].reshape(-1), swapped(tile_columns[:, 0]).reshape(-1)])
    counts = jnp.concatenate([tile_counts[:, 0], swapped(tile_counts[:, 0])])
    levels_of = lambda device: lax.dynamic_slice_in_dim(level_sets, device, 1, 1)[:, 0]
    row_levels = jnp.concatenate(
        [levels_of(own_index), levels_of(own_index + 1 - 2 * core)]
    )
    core_id = core.reshape(1).astype(jnp.int32)

    edges, starts = pl.pallas_call(
        functools.partial(list_edges, owners),
        out_shape=(
            jax.ShapeDtypeStruct((columns.size,), jnp.int32),
            jax.ShapeDtypeStruct((KEYS + 1,), jnp.int32),
        ),
        in_specs=[smem()] * 4,
        out_specs=(smem(), smem()),
        scratch_shapes=[pltpu.SMEM((KEYS,), jnp.int32)],
        name="list_edges",
    )(columns, counts, row_levels, level_sets.reshape(-1))

    block = (part, lanes)
    tile = lower_tiles.shape[3:]

    def solve(level, received, held):
        lists = ((edges, starts, received) if level else ()) + (held,)
        return pl.pallas_call(
            functools.partial(solve_level, level, rows, width_k, owners),
            out_shape=jax.ShapeDtypeStruct((MEMBERS, *block), jnp.bfloat16),
            in_specs=[smem(), smem()]
            + ([smem(), smem(), vmem()] if level else [])
            + [vmem()]
            + [anywhere()] * (2 * MEMBERS),
            out_specs=vmem(),
            scratch_shapes=[
                pltpu.VMEM((MEMBERS * width_k, *tile), jnp.bfloat16),
                pltpu.VMEM((MEMBERS, *tile), jnp.bfloat16),
                pltpu.SemaphoreType.DMA((MEMBERS * width_k,)),
                pltpu.SemaphoreType.DMA((MEMBERS,)),
            ],
            compiler_params=pltpu.CompilerParams(vmem_limit_bytes=8 << 20),
            cost_estimate=pl.CostEstimate(flops=4 << 20, bytes_accessed=1 << 18, transcendentals=0),
            name=f"solve_{level}",
        )(core_id, row_levels, *lists, *tiles, *inverses)

    def absorb(level, received, held):
        return pl.pallas_call(
            functools.partial(absorb_level, level, rows, width_k, owners),
            out_shape=jax.ShapeDtypeStruct(held.shape, held.dtype),
            in_specs=[smem(), smem(), vmem(), vmem()] + [anywhere()] * MEMBERS,
            out_specs=vmem(),
            scratch_shapes=[
                pltpu.VMEM((RING, *tile), jnp.bfloat16),
                pltpu.SemaphoreType.DMA((RING,)),
            ],
            compiler_params=pltpu.CompilerParams(vmem_limit_bytes=8 << 20),
            cost_estimate=pl.CostEstimate(flops=32 << 20, bytes_accessed=1 << 20, transcendentals=0),
            name=f"absorb_{level}",
        )(edges, starts, received, held, *tiles)

    received = None
    pieces = []
    for level in range(LEVELS):
        piece = solve(level, received, held)
        pieces.append(piece)
        if level == LEVELS - 1:
            break
        arriving = lax.all_to_all(
            jnp.broadcast_to(piece[None], (chips, *piece.shape)), CHIPS, 0, 0, tiled=True
        )
        if level:
            held = absorb(level, received, held)
        received = arriving.reshape(owners, *block)

    pieces = jnp.stack(pieces)
    mine = pieces[row_levels[:rows], core]
    theirs = swapped(pieces[row_levels[rows:], 1 - core])
    both = jnp.concatenate([mine, theirs], 1)
    crossed = jnp.concatenate([theirs, mine], 1)
    return jnp.swapaxes(jnp.where(core == 0, both, crossed), 1, 2)[:, None]


def solution(mesh):
    finer = Mesh(mesh.devices.reshape(4, 4, 4, 2), ROWS)
    return jax.shard_map(
        local,
        mesh=finer,
        in_specs=(
            P(None, ROWS, None, None),
            P(None, ROWS, None, None, None),
            P(None, ROWS, None, None),
            P(None, ROWS, None),
            P(None, ROWS),
            P(),
        ),
        out_specs=P(None, ROWS, None, None),
        check_vma=False,
    )
```

time: 660 us -> 425 us (0.64)
  waiting for transfers between devices: 266 us -> 140 us
  blocking collectives: 102 us -> 0 us
  matrix products: 91 us -> 0 us
  Pallas kernels: 0 us -> 64.9 us
  local copies, waits for them, and re-layouts: 66.8 us -> 102 us
  starting transfers between devices: 77.1 us -> 109 us
  loops' own time: 26.4 us -> 0 us
  other arithmetic: 25.9 us -> 3.67 us
    all_to_all x15, waiting for transfers between devices: 266 us -> 135 us  [local(): lax.all_to_all(jnp.broadcast_to(piece[None], (chips, *piece.shape)), CHIP...]
    all_to_all x15 -> x0, blocking collectives: 102 us -> none  [copy_for_each(): lax.all_to_all(jnp.broadcast_to(value[None], (length, *value.shape)), axi...]
    dot_general x31 -> x0, matrix products: 91 us -> none  [the longest x15 66.8 us: absorb(): jnp.einsum('skab,skbr->sar', tiles_local, fetched, preferred_element_type...]
    unnamed x6 -> x98, local copies, waits for them, and re-layouts: 0.7 us -> 78 us
    pallas_call x0 -> x31, Pallas kernels: none -> 64.9 us  [the longest x14 31.3 us: absorb(): pl.pallas_call(functools.partial(absorb_level, level, rows, width_k, owne...]
    gather x17 -> x2, local copies, waits for them, and re-layouts: 33.6 us -> 3.06 us  [the longest x1 1.53 us: local(): mine = pieces[row_levels[:rows], core]]
    another operation x1 -> x0, loops' own time: 26.4 us -> none  [local(): held, solution = lax.fori_loop(0, LEVELS - 1, advance, (store, solution))]
    ppermute x0 -> x6, starting transfers between devices: none -> 22.5 us  [swapped(): return lax.ppermute(value, CORE, SWAP)]
  transfers between devices with their start and end apart: 15 -> 21, of which waited for: 15 -> 16; matrix products, arithmetic and copies ran while one was open for 1% -> 4% of each run, Pallas kernels for 0% -> 9%
where the time goes in v1:
time: 425 us; the launch traced here: 419 us
  waiting for transfers between devices  140 us (33%)
  starting transfers between devices  109 us (26%)
  local copies, waits for them, and re-layouts  102 us (24%)
  Pallas kernels  64.9 us (15%)
    all_to_all x15, waiting for transfers between devices, local(): lax.all_to_all(jnp.broadcast_to(piece[None], (chips, *piece.shape)), CHIP...  135 us
    all_to_all x15, starting transfers between devices, local(): lax.all_to_all(jnp.broadcast_to(piece[None], (chips, *piece.shape)), CHIP...  86.1 us
    unnamed x98, local copies, waits for them, and re-layouts  78 us
    pallas_call x14, Pallas kernels, absorb(): pl.pallas_call(functools.partial(absorb_level, level, rows, width_k, owne...  31.3 us
    pallas_call x16, Pallas kernels, solve(): pl.pallas_call(functools.partial(solve_level, level, rows, width_k, owner...  27.4 us
    ppermute x6, starting transfers between devices, swapped(): return lax.ppermute(value, CORE, SWAP)  22.5 us
    broadcast_in_dim x15, local copies, waits for them, and re-layouts, local(): jnp.broadcast_to(piece[None], (chips, *piece.shape))  18.9 us
  transfers between devices with their start and end apart: 21, of which 16 were waited for; matrix products, arithmetic and copies ran while one was open for 4% of the time, Pallas kernels for 9%

profile of v1, /device:TPU:1, one launch (start us, length us, event | category | flops | bytes accessed | tf_op | source)
XLA Modules:
  0.0 419.1 jit_solution(12517935398333554114)
XLA Ops:
  4.0 4.9 %collective-permute-done = f32[8,32,128]{2,1,0:T(8,128)S(1)} collective-permute-done((f32[8,32,128]{2,1,0:T(8,128)S(1)}, f32[8,32,128]{2,1,0:T(8,128)S(1)}, u32[]{:S(2)}, u32[]{:S(2)}) %collective-permute-start) | collective-permute-done | bytes 131104 | tf_op jit(solution)/shard_map/ppermute | solution.py:208
  14.5 11.4 %all-to-all-start = ((bf16[64,2,32,128]{3,2,1,0:T(8,128)(2,1)}), bf16[64,2,32,128]{3,2,1,0:T(8,128)(2,1)S(1)}, u32[]{:S(2)}, u32[]{:S(2)}) async-start(bf16[64,2,32,128]{3,2,1,0:T(8,128)(2,1)} %broadcast_in_dim.32), calls=%async_computation | async-start | bytes 2097152 | tf_op jit(solution)/shard_map/all_to_all | solution.py:282
  29.4 6.3 %list_edges.1 = (s32[256]{0:T(256)}, s32[65]{0:T(128)}) custom-call(s32[256]{0:T(256)} %pad_add_fusion.columns, s32[16]{0:T(128)} %pad_add_fusion.2.counts, s32[16]{0:T(128)} %copy-done.36, s32[1024]{0:T(1024)} %bitcast.144), custom_call_target="tpu_custom_call" | custom-call | tf_op jit(solution)/shard_map/list_edges/pallas_call | solution.py:224
  35.6 8.4 %all-to-all-done = bf16[64,2,32,128]{3,2,1,0:T(8,128)(2,1)S(1)} async-done(((bf16[64,2,32,128]{3,2,1,0:T(8,128)(2,1)}), bf16[64,2,32,128]{3,2,1,0:T(8,128)(2,1)S(1)}, u32[]{:S(2)}, u32[]{:S(2)}) %all-to-all-start) | async-done | bytes 1048608 | tf_op jit(solution)/shard_map/all_to_all | solution.py:282
  44.0 2.2 copy-done.1
  48.1 2.4 solve_1.1
  51.8 7.0 %all-to-all-start.1 = ((bf16[64,2,32,128]{3,2,1,0:T(8,128)(2,1)}), bf16[64,2,32,128]{3,2,1,0:T(8,128)(2,1)S(1)}, u32[]{:S(2)}, u32[]{:S(2)}) async-start(bf16[64,2,32,128]{3,2,1,0:T(8,128)(2,1)} %broadcast_in_dim.33), calls=%async_computation.1 | async-start | bytes 2097152 | tf_op jit(solution)/shard_map/all_to_all | solution.py:282
  61.0 3.5 absorb_1.1.refs_3_.held_in
  64.5 11.0 %all-to-all-done.1 = bf16[64,2,32,128]{3,2,1,0:T(8,128)(2,1)S(1)} async-done(((bf16[64,2,32,128]{3,2,1,0:T(8,128)(2,1)}), bf16[64,2,32,128]{3,2,1,0:T(8,128)(2,1)S(1)}, u32[]{:S(2)}, u32[]{:S(2)}) %all-to-all-start.1) | async-done | bytes 1048608 | tf_op jit(solution)/shard_map/all_to_all | solution.py:282
  75.5 2.2 copy-done.3
  81.1 5.4 %all-to-all-start.2 = ((bf16[64,2,32,128]{3,2,1,0:T(8,128)(2,1)}), bf16[64,2,32,128]{3,2,1,0:T(8,128)(2,1)S(1)}, u32[]{:S(2)}, u32[]{:S(2)}) async-start(bf16[64,2,32,128]{3,2,1,0:T(8,128)(2,1)} %broadcast_in_dim.34), calls=%async_computation.2 | async-start | bytes 2097152 | tf_op jit(solution)/shard_map/all_to_all | solution.py:282
  88.7 4.1 absorb_2.1.refs_3_.held_in
  92.7 9.3 %all-to-all-done.2 = bf16[64,2,32,128]{3,2,1,0:T(8,128)(2,1)S(1)} async-done(((bf16[64,2,32,128]{3,2,1,0:T(8,128)(2,1)}), bf16[64,2,32,128]{3,2,1,0:T(8,128)(2,1)S(1)}, u32[]{:S(2)}, u32[]{:S(2)}) %all-to-all-start.2) | async-done | bytes 1048608 | tf_op jit(solution)/shard_map/all_to_all | solution.py:282
  104.2 2.7 solve_3.1
  108.2 4.7 %all-to-all-start.3 = ((bf16[64,2,32,128]{3,2,1,0:T(8,128)(2,1)}), bf16[64,2,32,128]{3,2,1,0:T(8,128)(2,1)S(1)}, u32[]{:S(2)}, u32[]{:S(2)}) async-start(bf16[64,2,32,128]{3,2,1,0:T(8,128)(2,1)} %broadcast_in_dim.35), calls=%async_computation.3 | async-start | bytes 2097152 | tf_op jit(solution)/shard_map/all_to_all | solution.py:282
  115.0 3.0 absorb_3.1.refs_3_.held_in
  118.0 9.6 %all-to-all-done.3 = bf16[64,2,32,128]{3,2,1,0:T(8,128)(2,1)S(1)} async-done(((bf16[64,2,32,128]{3,2,1,0:T(8,128)(2,1)}), bf16[64,2,32,128]{3,2,1,0:T(8,128)(2,1)S(1)}, u32[]{:S(2)}, u32[]{:S(2)}) %all-to-all-start.3) | async-done | bytes 1048608 | tf_op jit(solution)/shard_map/all_to_all | solution.py:282
  132.0 6.7 %all-to-all-start.4 = ((bf16[64,2,32,128]{3,2,1,0:T(8,128)(2,1)}), bf16[64,2,32,128]{3,2,1,0:T(8,128)(2,1)S(1)}, u32[]{:S(2)}, u32[]{:S(2)}) async-start(bf16[64,2,32,128]{3,2,1,0:T(8,128)(2,1)} %broadcast_in_dim.36), calls=%async_computation.4 | async-start | bytes 2097152 | tf_op jit(solution)/shard_map/all_to_all | solution.py:282
  140.9 2.7 absorb_4.1.refs_3_.held_in
  143.7 9.8 %all-to-all-done.4 = bf16[64,2,32,128]{3,2,1,0:T(8,128)(2,1)S(1)} async-done(((bf16[64,2,32,128]{3,2,1,0:T(8,128)(2,1)}), bf16[64,2,32,128]{3,2,1,0:T(8,128)(2,1)S(1)}, u32[]{:S(2)}, u32[]{:S(2)}) %all-to-all-start.4) | async-done | bytes 1048608 | tf_op jit(solution)/shard_map/all_to_all | solution.py:282
  157.8 5.2 %all-to-all-start.5 = ((bf16[64,2,32,128]{3,2,1,0:T(8,128)(2,1)}), bf16[64,2,32,128]{3,2,1,0:T(8,128)(2,1)S(1)}, u32[]{:S(2)}, u32[]{:S(2)}) async-start(bf16[64,2,32,128]{3,2,1,0:T(8,128)(2,1)} %broadcast_in_dim.37), calls=%async_computation.5 | async-start | bytes 2097152 | tf_op jit(solution)/shard_map/all_to_all | solution.py:282
  165.2 3.5 absorb_5.1.refs_3_.held_in
  168.8 8.2 %all-to-all-done.5 = bf16[64,2,32,128]{3,2,1,0:T(8,128)(2,1)S(1)} async-done(((bf16[64,2,32,128]{3,2,1,0:T(8,128)(2,1)}), bf16[64,2,32,128]{3,2,1,0:T(8,128)(2,1)S(1)}, u32[]{:S(2)}, u32[]{:S(2)}) %all-to-all-start.5) | async-done | bytes 1048608 | tf_op jit(solution)/shard_map/all_to_all | solution.py:282
  182.4 4.8 %all-to-all-start.6 = ((bf16[64,2,32,128]{3,2,1,0:T(8,128)(2,1)}), bf16[64,2,32,128]{3,2,1,0:T(8,128)(2,1)S(1)}, u32[]{:S(2)}, u32[]{:S(2)}) async-start(bf16[64,2,32,128]{3,2,1,0:T(8,128)(2,1)} %broadcast_in_dim.38), calls=%async_computation.6 | async-start | bytes 2097152 | tf_op jit(solution)/shard_map/all_to_all | solution.py:282
  189.4 3.5 absorb_6.1.refs_3_.held_in
  192.9 8.0 %all-to-all-done.6 = bf16[64,2,32,128]{3,2,1,0:T(8,128)(2,1)S(1)} async-done(((bf16[64,2,32,128]{3,2,1,0:T(8,128)(2,1)}), bf16[64,2,32,128]{3,2,1,0:T(8,128)(2,1)S(1)}, u32[]{:S(2)}, u32[]{:S(2)}) %all-to-all-start.6) | async-done | bytes 1048608 | tf_op jit(solution)/shard_map/all_to_all | solution.py:282
  203.0 2.3 solve_7.1
  206.6 4.7 %all-to-all-start.7 = ((bf16[64,2,32,128]{3,2,1,0:T(8,128)(2,1)}), bf16[64,2,32,128]{3,2,1,0:T(8,128)(2,1)S(1)}, u32[]{:S(2)}, u32[]{:S(2)}) async-start(bf16[64,2,32,128]{3,2,1,0:T(8,128)(2,1)} %broadcast_in_dim.39), calls=%async_computation.7 | async-start | bytes 2097152 | tf_op jit(solution)/shard_map/all_to_all | solution.py:282
  215.5 9.3 %all-to-all-done.7 = bf16[64,2,32,128]{3,2,1,0:T(8,128)(2,1)S(1)} async-done(((bf16[64,2,32,128]{3,2,1,0:T(8,128)(2,1)}), bf16[64,2,32,128]{3,2,1,0:T(8,128)(2,1)S(1)}, u32[]{:S(2)}, u32[]{:S(2)}) %all-to-all-start.7) | async-done | bytes 1048608 | tf_op jit(solution)/shard_map/all_to_all | solution.py:282
  229.2 5.4 %all-to-all-start.8 = ((bf16[64,2,32,128]{3,2,1,0:T(8,128)(2,1)}), bf16[64,2,32,128]{3,2,1,0:T(8,128)(2,1)S(1)}, u32[]{:S(2)}, u32[]{:S(2)}) async-start(bf16[64,2,32,128]{3,2,1,0:T(8,128)(2,1)} %broadcast_in_dim.40), calls=%async_computation.8 | async-start | bytes 2097152 | tf_op jit(solution)/shard_map/all_to_all | solution.py:282
  236.8 2.5 absorb_8.1.refs_3_.held_in
  239.3 8.8 %all-to-all-done.8 = bf16[64,2,32,128]{3,2,1,0:T(8,128)(2,1)S(1)} async-done(((bf16[64,2,32,128]{3,2,1,0:T(8,128)(2,1)}), bf16[64,2,32,128]{3,2,1,0:T(8,128)(2,1)S(1)}, u32[]{:S(2)}, u32[]{:S(2)}) %all-to-all-start.8) | async-done | bytes 1048608 | tf_op jit(solution)/shard_map/all_to_all | solution.py:282
  250.3 2.5 solve_9.1
  254.1 4.7 %all-to-all-start.9 = ((bf16[64,2,32,128]{3,2,1,0:T(8,128)(2,1)}), bf16[64,2,32,128]{3,2,1,0:T(8,128)(2,1)S(1)}, u32[]{:S(2)}, u32[]{:S(2)}) async-start(bf16[64,2,32,128]{3,2,1,0:T(8,128)(2,1)} %broadcast_in_dim.41), calls=%async_computation.9 | async-start | bytes 2097152 | tf_op jit(solution)/shard_map/all_to_all | solution.py:282
  262.8 9.5 %all-to-all-done.9 = bf16[64,2,32,128]{3,2,1,0:T(8,128)(2,1)S(1)} async-done(((bf16[64,2,32,128]{3,2,1,0:T(8,128)(2,1)}), bf16[64,2,32,128]{3,2,1,0:T(8,128)(2,1)S(1)}, u32[]{:S(2)}, u32[]{:S(2)}) %all-to-all-start.9) | async-done | bytes 1048608 | tf_op jit(solution)/shard_map/all_to_all | solution.py:282
  274.5 2.2 solve_10.1
  278.0 4.7 %all-to-all-start.10 = ((bf16[64,2,32,128]{3,2,1,0:T(8,128)(2,1)}), bf16[64,2,32,128]{3,2,1,0:T(8,128)(2,1)S(1)}, u32[]{:S(2)}, u32[]{:S(2)}) async-start(bf16[64,2,32,128]{3,2,1,0:T(8,128)(2,1)} %broadcast_in_dim.42), calls=%async_computation.10 | async-start | bytes 2097152 | tf_op jit(solution)/shard_map/all_to_all | solution.py:282
  286.6 9.6 %all-to-all-done.10 = bf16[64,2,32,128]{3,2,1,0:T(8,128)(2,1)S(1)} async-done(((bf16[64,2,32,128]{3,2,1,0:T(8,128)(2,1)}), bf16[64,2,32,128]{3,2,1,0:T(8,128)(2,1)S(1)}, u32[]{:S(2)}, u32[]{:S(2)}) %all-to-all-start.10) | async-done | bytes 1048608 | tf_op jit(solution)/shard_map/all_to_all | solution.py:282
  300.6 5.5 %all-to-all-start.11 = ((bf16[64,2,32,128]{3,2,1,0:T(8,128)(2,1)}), bf16[64,2,32,128]{3,2,1,0:T(8,128)(2,1)S(1)}, u32[]{:S(2)}, u32[]{:S(2)}) async-start(bf16[64,2,32,128]{3,2,1,0:T(8,128)(2,1)} %broadcast_in_dim.43), calls=%async_computation.11 | async-start | bytes 2097152 | tf_op jit(solution)/shard_map/all_to_all | solution.py:282
  308.9 10.7 %all-to-all-done.11 = bf16[64,2,32,128]{3,2,1,0:T(8,128)(2,1)S(1)} async-done(((bf16[64,2,32,128]{3,2,1,0:T(8,128)(2,1)}), bf16[64,2,32,128]{3,2,1,0:T(8,128)(2,1)S(1)}, u32[]{:S(2)}, u32[]{:S(2)}) %all-to-all-start.11) | async-done | bytes 1048608 | tf_op jit(solution)/shard_map/all_to_all | solution.py:282
  324.3 5.5 %all-to-all-start.12 = ((bf16[64,2,32,128]{3,2,1,0:T(8,128)(2,1)}), bf16[64,2,32,128]{3,2,1,0:T(8,128)(2,1)S(1)}, u32[]{:S(2)}, u32[]{:S(2)}) async-start(bf16[64,2,32,128]{3,2,1,0:T(8,128)(2,1)} %broadcast_in_dim.44), calls=%async_computation.12 | async-start | bytes 2097152 | tf_op jit(solution)/shard_map/all_to_all | solution.py:282
  335.9 7.5 %all-to-all-done.12 = bf16[64,2,32,128]{3,2,1,0:T(8,128)(2,1)S(1)} async-done(((bf16[64,2,32,128]{3,2,1,0:T(8,128)(2,1)}), bf16[64,2,32,128]{3,2,1,0:T(8,128)(2,1)S(1)}, u32[]{:S(2)}, u32[]{:S(2)}) %all-to-all-start.12) | async-done | bytes 1048608 | tf_op jit(solution)/shard_map/all_to_all | solution.py:282
  348.8 4.9 %all-to-all-start.13 = ((bf16[64,2,32,128]{3,2,1,0:T(8,128)(2,1)}), bf16[64,2,32,128]{3,2,1,0:T(8,128)(2,1)S(1)}, u32[]{:S(2)}, u32[]{:S(2)}) async-start(bf16[64,2,32,128]{3,2,1,0:T(8,128)(2,1)} %broadcast_in_dim.45), calls=%async_computation.13 | async-start | bytes 2097152 | tf_op jit(solution)/shard_map/all_to_all | solution.py:282
  359.6 7.5 %all-to-all-done.13 = bf16[64,2,32,128]{3,2,1,0:T(8,128)(2,1)S(1)} async-done(((bf16[64,2,32,128]{3,2,1,0:T(8,128)(2,1)}), bf16[64,2,32,128]{3,2,1,0:T(8,128)(2,1)S(1)}, u32[]{:S(2)}, u32[]{:S(2)}) %all-to-all-start.13) | async-done | bytes 1048608 | tf_op jit(solution)/shard_map/all_to_all | solution.py:282
  371.4 5.7 %all-to-all-start.14 = ((bf16[64,2,32,128]{3,2,1,0:T(8,128)(2,1)}), bf16[64,2,32,128]{3,2,1,0:T(8,128)(2,1)S(1)}, u32[]{:S(2)}, u32[]{:S(2)}) async-start(bf16[64,2,32,128]{3,2,1,0:T(8,128)(2,1)} %broadcast_in_dim.46), calls=%async_computation.14 | async-start | bytes 2097152 | tf_op jit(solution)/shard_map/all_to_all | solution.py:282
  382.9 7.7 %all-to-all-done.14 = bf16[64,2,32,128]{3,2,1,0:T(8,128)(2,1)S(1)} async-done(((bf16[64,2,32,128]{3,2,1,0:T(8,128)(2,1)}), bf16[64,2,32,128]{3,2,1,0:T(8,128)(2,1)S(1)}, u32[]{:S(2)}, u32[]{:S(2)}) %all-to-all-start.14) | async-done | bytes 1048608 | tf_op jit(solution)/shard_map/all_to_all | solution.py:282
  392.8 2.2 solve_15.1
  397.2 19.7 %collective-permute-start.5 = (bf16[8,32,128]{2,1,0:T(8,128)(2,1)S(1)}, bf16[8,32,128]{2,1,0:T(8,128)(2,1)S(1)}, u32[]{:S(2)}, u32[]{:S(2)}) collective-permute-start(bf16[8,32,128]{2,1,0:T(8,128)(2,1)S(1)} %gather_fusion.1), channel_id=1, source_target_pairs={{0,1},{1,0},{2,3},{3,2},{4,5},{5,4},{6,7},{7,6},{8,9},{9,8},{10,11... | collective-permute-start | bytes 196616 | tf_op jit(solution)/shard_map/ppermute | solution.py:208
  (151 shorter events, 125.4 us)
Async XLA Ops:
  0.0 9.0 %collective-permute-start.1 = (bf16[8,16,128,128]{3,2,1,0:T(8,128)(2,1)}, bf16[8,16,128,128]{3,2,1,0:T(8,128)(2,1)}, u32[]{:S(2)}, u32[]{:S(2)}) collective-permute-start(bf16[8,16,128,128]{3,2,1,0:T(8,128)(2,1)} %bitcast.67), channel_id=1, source_target_pairs={{0,1},{1,0},{2,3},{3,2},{4,5},{5,4},{6,7},{7,6},{8,9},{9,8},{10,11... | collective-permute-start | bytes 12582920 | tf_op jit(solution)/shard_map/ppermute | solution.py:208
  1.4 7.6 %collective-permute-start.2 = (bf16[8,128,128]{2,1,0:T(8,128)(2,1)}, bf16[8,128,128]{2,1,0:T(8,128)(2,1)S(1)}, u32[]{:S(2)}, u32[]{:S(2)}) collective-permute-start(bf16[8,128,128]{2,1,0:T(8,128)(2,1)} %bitcast.98), channel_id=1, source_target_pairs={{0,1},{1,0},{2,3},{3,2},{4,5},{5,4},{6,7},{7,6},{8,9},{9,8},{10,11... | collective-permute-start | bytes 786440 | tf_op jit(solution)/shard_map/ppermute | solution.py:208
  2.4 6.6 %collective-permute-start = (f32[8,32,128]{2,1,0:T(8,128)S(1)}, f32[8,32,128]{2,1,0:T(8,128)S(1)}, u32[]{:S(2)}, u32[]{:S(2)}) collective-permute-start(f32[8,32,128]{2,1,0:T(8,128)S(1)} %get-tuple-element.14), channel_id=1, source_target_pairs={{0,1},{1,0},{2,3},{3,2},{4,5},{5,4},{6,7},{7,6},{8,9},{9,8},{10,11... | collective-permute-start | bytes 393224 | tf_op jit(solution)/shard_map/ppermute | solution.py:208
  4.0 9.2 %copy-start.36 = (s32[16]{0:T(128)}, s32[16]{0:T(128)S(1)}, u32[]{:S(2)}) copy-start(s32[16]{0:T(128)S(1)} %pad_add_fusion.1.row_levels) | copy-start | bytes 196
  9.0 2.2 copy-start
  12.1 13.8 %copy-start.40 = (s32[8,1]{0,1:T(1,128)S(1)}, s32[8,1]{0,1:T(1,128)}, u32[]{:S(2)}) copy-start(s32[8,1]{0,1:T(1,128)} %param.10) | copy-start | bytes 100
  12.1 14.5 %copy-start.39 = (s32[8,1,16]{2,1,0:T(1,128)S(1)}, s32[8,1,16]{2,1,0:T(1,128)}, u32[]{:S(2)}) copy-start(s32[8,1,16]{2,1,0:T(1,128)} %param.9) | copy-start | bytes 1540
  12.1 31.9 %copy-start.31 = (bf16[8,1,128,128]{3,2,1,0:T(8,128)(2,1)S(1)}, bf16[8,1,128,128]{3,2,1,0:T(8,128)(2,1)}, u32[]{:S(2)}) copy-start(bf16[8,1,128,128]{3,2,1,0:T(8,128)(2,1)} %param.8) | copy-start | bytes 786436
  14.5 29.5 %all-to-all-start = ((bf16[64,2,32,128]{3,2,1,0:T(8,128)(2,1)}), bf16[64,2,32,128]{3,2,1,0:T(8,128)(2,1)S(1)}, u32[]{:S(2)}, u32[]{:S(2)}) async-start(bf16[64,2,32,128]{3,2,1,0:T(8,128)(2,1)} %broadcast_in_dim.32), calls=%async_computation | async-start | bytes 2097152 | tf_op jit(solution)/shard_map/all_to_all | solution.py:282
  25.9 2.1 collective-permute-start.4
  26.7 2.0 collective-permute-start.3
  44.0 2.2 copy-start.1
  48.1 10.7 %copy-start.33 = (s32[256]{0:T(256)S(1)}, s32[256]{0:T(256)}, u32[]{:S(2)}) copy-start(s32[256]{0:T(256)} %get-tuple-element.7.refs_0_.edges) | copy-start | bytes 3076
  48.1 10.7 %copy-start.35 = (s32[65]{0:T(128)S(1)}, s32[65]{0:T(128)}, u32[]{:S(2)}) copy-start(s32[65]{0:T(128)} %get-tuple-element.8.refs_1_.starts) | copy-start | bytes 784
  51.8 23.7 %all-to-all-start.1 = ((bf16[64,2,32,128]{3,2,1,0:T(8,128)(2,1)}), bf16[64,2,32,128]{3,2,1,0:T(8,128)(2,1)S(1)}, u32[]{:S(2)}, u32[]{:S(2)}) async-start(bf16[64,2,32,128]{3,2,1,0:T(8,128)(2,1)} %broadcast_in_dim.33), calls=%async_computation.1 | async-start | bytes 2097152 | tf_op jit(solution)/shard_map/all_to_all | solution.py:282
  58.8 2.2 copy-start.2
  61.0 14.5 %copy-start.38 = (s32[16]{0:T(128)S(1)}, s32[16]{0:T(128)}, u32[]{:S(2)}) copy-start(s32[16]{0:T(128)} %copy-done.36) | copy-start | bytes 196
  75.5 2.2 copy-start.3
  81.1 20.9 %all-to-all-start.2 = ((bf16[64,2,32,128]{3,2,1,0:T(8,128)(2,1)}), bf16[64,2,32,128]{3,2,1,0:T(8,128)(2,1)S(1)}, u32[]{:S(2)}, u32[]{:S(2)}) async-start(bf16[64,2,32,128]{3,2,1,0:T(8,128)(2,1)} %broadcast_in_dim.34), calls=%async_computation.2 | async-start | bytes 2097152 | tf_op jit(solution)/shard_map/all_to_all | solution.py:282
  86.5 2.2 copy-start.4
  102.0 2.2 copy-start.5
  108.2 19.4 %all-to-all-start.3 = ((bf16[64,2,32,128]{3,2,1,0:T(8,128)(2,1)}), bf16[64,2,32,128]{3,2,1,0:T(8,128)(2,1)S(1)}, u32[]{:S(2)}, u32[]{:S(2)}) async-start(bf16[64,2,32,128]{3,2,1,0:T(8,128)(2,1)} %broadcast_in_dim.35), calls=%async_computation.3 | async-start | bytes 2097152 | tf_op jit(solution)/shard_map/all_to_all | solution.py:282
  112.8 2.2 copy-start.6
  127.6 2.2 copy-start.7
  132.0 21.4 %all-to-all-start.4 = ((bf16[64,2,32,128]{3,2,1,0:T(8,128)(2,1)}), bf16[64,2,32,128]{3,2,1,0:T(8,128)(2,1)S(1)}, u32[]{:S(2)}, u32[]{:S(2)}) async-start(bf16[64,2,32,128]{3,2,1,0:T(8,128)(2,1)} %broadcast_in_dim.36), calls=%async_computation.4 | async-start | bytes 2097152 | tf_op jit(solution)/shard_map/all_to_all | solution.py:282
  138.7 2.2 copy-start.8
  153.4 2.2 copy-start.9
  157.8 19.1 %all-to-all-start.5 = ((bf16[64,2,32,128]{3,2,1,0:T(8,128)(2,1)}), bf16[64,2,32,128]{3,2,1,0:T(8,128)(2,1)S(1)}, u32[]{:S(2)}, u32[]{:S(2)}) async-start(bf16[64,2,32,128]{3,2,1,0:T(8,128)(2,1)} %broadcast_in_dim.37), calls=%async_computation.5 | async-start | bytes 2097152 | tf_op jit(solution)/shard_map/all_to_all | solution.py:282
  163.0 2.2 copy-start.10
  177.0 2.2 copy-start.11
  182.4 18.5 %all-to-all-start.6 = ((bf16[64,2,32,128]{3,2,1,0:T(8,128)(2,1)}), bf16[64,2,32,128]{3,2,1,0:T(8,128)(2,1)S(1)}, u32[]{:S(2)}, u32[]{:S(2)}) async-start(bf16[64,2,32,128]{3,2,1,0:T(8,128)(2,1)} %broadcast_in_dim.38), calls=%async_computation.6 | async-start | bytes 2097152 | tf_op jit(solution)/shard_map/all_to_all | solution.py:282
  187.2 2.2 copy-start.12
  206.6 18.3 %all-to-all-start.7 = ((bf16[64,2,32,128]{3,2,1,0:T(8,128)(2,1)}), bf16[64,2,32,128]{3,2,1,0:T(8,128)(2,1)S(1)}, u32[]{:S(2)}, u32[]{:S(2)}) async-start(bf16[64,2,32,128]{3,2,1,0:T(8,128)(2,1)} %broadcast_in_dim.39), calls=%async_computation.7 | async-start | bytes 2097152 | tf_op jit(solution)/shard_map/all_to_all | solution.py:282
  211.3 2.2 copy-start.14
  229.2 18.9 %all-to-all-start.8 = ((bf16[64,2,32,128]{3,2,1,0:T(8,128)(2,1)}), bf16[64,2,32,128]{3,2,1,0:T(8,128)(2,1)S(1)}, u32[]{:S(2)}, u32[]{:S(2)}) async-start(bf16[64,2,32,128]{3,2,1,0:T(8,128)(2,1)} %broadcast_in_dim.40), calls=%async_computation.8 | async-start | bytes 2097152 | tf_op jit(solution)/shard_map/all_to_all | solution.py:282
  234.6 2.2 copy-start.16
  248.1 2.2 copy-start.17
  254.1 18.2 %all-to-all-start.9 = ((bf16[64,2,32,128]{3,2,1,0:T(8,128)(2,1)}), bf16[64,2,32,128]{3,2,1,0:T(8,128)(2,1)S(1)}, u32[]{:S(2)}, u32[]{:S(2)}) async-start(bf16[64,2,32,128]{3,2,1,0:T(8,128)(2,1)} %broadcast_in_dim.41), calls=%async_computation.9 | async-start | bytes 2097152 | tf_op jit(solution)/shard_map/all_to_all | solution.py:282
  258.8 2.2 copy-start.18
  272.3 2.2 copy-start.19
  278.0 18.2 %all-to-all-start.10 = ((bf16[64,2,32,128]{3,2,1,0:T(8,128)(2,1)}), bf16[64,2,32,128]{3,2,1,0:T(8,128)(2,1)S(1)}, u32[]{:S(2)}, u32[]{:S(2)}) async-start(bf16[64,2,32,128]{3,2,1,0:T(8,128)(2,1)} %broadcast_in_dim.42), calls=%async_computation.10 | async-start | bytes 2097152 | tf_op jit(solution)/shard_map/all_to_all | solution.py:282
  282.6 2.2 copy-start.20
  300.6 19.0 %all-to-all-start.11 = ((bf16[64,2,32,128]{3,2,1,0:T(8,128)(2,1)}), bf16[64,2,32,128]{3,2,1,0:T(8,128)(2,1)S(1)}, u32[]{:S(2)}, u32[]{:S(2)}) async-start(bf16[64,2,32,128]{3,2,1,0:T(8,128)(2,1)} %broadcast_in_dim.43), calls=%async_computation.11 | async-start | bytes 2097152 | tf_op jit(solution)/shard_map/all_to_all | solution.py:282
  306.0 2.2 copy-start.22
  324.3 19.1 %all-to-all-start.12 = ((bf16[64,2,32,128]{3,2,1,0:T(8,128)(2,1)}), bf16[64,2,32,128]{3,2,1,0:T(8,128)(2,1)S(1)}, u32[]{:S(2)}, u32[]{:S(2)}) async-start(bf16[64,2,32,128]{3,2,1,0:T(8,128)(2,1)} %broadcast_in_dim.44), calls=%async_computation.12 | async-start | bytes 2097152 | tf_op jit(solution)/shard_map/all_to_all | solution.py:282
  348.8 18.2 %all-to-all-start.13 = ((bf16[64,2,32,128]{3,2,1,0:T(8,128)(2,1)}), bf16[64,2,32,128]{3,2,1,0:T(8,128)(2,1)S(1)}, u32[]{:S(2)}, u32[]{:S(2)}) async-start(bf16[64,2,32,128]{3,2,1,0:T(8,128)(2,1)} %broadcast_in_dim.45), calls=%async_computation.13 | async-start | bytes 2097152 | tf_op jit(solution)/shard_map/all_to_all | solution.py:282
  371.4 19.2 %all-to-all-start.14 = ((bf16[64,2,32,128]{3,2,1,0:T(8,128)(2,1)}), bf16[64,2,32,128]{3,2,1,0:T(8,128)(2,1)S(1)}, u32[]{:S(2)}, u32[]{:S(2)}) async-start(bf16[64,2,32,128]{3,2,1,0:T(8,128)(2,1)} %broadcast_in_dim.46), calls=%async_computation.14 | async-start | bytes 2097152 | tf_op jit(solution)/shard_map/all_to_all | solution.py:282
  397.2 21.2 %collective-permute-start.5 = (bf16[8,32,128]{2,1,0:T(8,128)(2,1)S(1)}, bf16[8,32,128]{2,1,0:T(8,128)(2,1)S(1)}, u32[]{:S(2)}, u32[]{:S(2)}) collective-permute-start(bf16[8,32,128]{2,1,0:T(8,128)(2,1)S(1)} %gather_fusion.1), channel_id=1, source_target_pairs={{0,1},{1,0},{2,3},{3,2},{4,5},{5,4},{6,7},{7,6},{8,9},{9,8},{10,11... | collective-permute-start | bytes 196616 | tf_op jit(solution)/shard_map/ppermute | solution.py:208
  (14 other events, 24.7 us)

commit v2 on v1

--- a/solution.py
+++ b/solution.py
@@ -27,7 +27,7 @@
 
 
 def anywhere():
-    return pl.BlockSpec(memory_space=pl.ANY)
+    return pl.BlockSpec(memory_space=pltpu.HBM)
 
 
 def bucket(level, urgent, member):
@@ -193,6 +193,18 @@
             return unused
 
         lax.fori_loop(0, many, absorb, 0)
+
+
+def collect_rows(rows, core, row_levels, *refs):
+    pieces, outs = refs[:LEVELS], refs[LEVELS:]
+    for level in range(LEVELS):
+        for member in range(MEMBERS):
+            at = core[0] if member == 0 else 1 - core[0]
+            for s in range(rows):
+
+                @pl.when(row_levels[member * rows + s] == level)
+                def _(level=level, member=member, at=at, s=s):
+                    outs[member][s] = pieces[level][at]
 
 
 def local(right_sides, lower_tiles, diag_inverse, tile_columns, tile_counts, level_sets):
@@ -252,7 +264,7 @@
                 pltpu.SemaphoreType.DMA((MEMBERS * width_k,)),
                 pltpu.SemaphoreType.DMA((MEMBERS,)),
             ],
-            compiler_params=pltpu.CompilerParams(vmem_limit_bytes=8 << 20),
+            compiler_params=pltpu.CompilerParams(vmem_limit_bytes=52 << 20),
             cost_estimate=pl.CostEstimate(flops=4 << 20, bytes_accessed=1 << 18, transcendentals=0),
             name=f"solve_{level}",
         )(core_id, row_levels, *lists, *tiles, *inverses)
@@ -267,7 +279,7 @@
                 pltpu.VMEM((RING, *tile), jnp.bfloat16),
                 pltpu.SemaphoreType.DMA((RING,)),
             ],
-            compiler_params=pltpu.CompilerParams(vmem_limit_bytes=8 << 20),
+            compiler_params=pltpu.CompilerParams(vmem_limit_bytes=52 << 20),
             cost_estimate=pl.CostEstimate(flops=32 << 20, bytes_accessed=1 << 20, transcendentals=0),
             name=f"absorb_{level}",
         )(edges, starts, received, held, *tiles)
@@ -286,9 +298,15 @@
             held = absorb(level, received, held)
         received = arriving.reshape(owners, *block)
 
-    pieces = jnp.stack(pieces)
-    mine = pieces[row_levels[:rows], core]
-    theirs = swapped(pieces[row_levels[rows:], 1 - core])
+    mine, theirs = pl.pallas_call(
+        functools.partial(collect_rows, rows),
+        out_shape=(jax.ShapeDtypeStruct((rows, *block), jnp.bfloat16),) * MEMBERS,
+        in_specs=[smem(), smem()] + [vmem()] * LEVELS,
+        out_specs=(vmem(),) * MEMBERS,
+        compiler_params=pltpu.CompilerParams(vmem_limit_bytes=52 << 20),
+        name="collect_rows",
+    )(core_id, row_levels, *pieces)
+    theirs = swapped(theirs)
     both = jnp.concatenate([mine, theirs], 1)
     crossed = jnp.concatenate([theirs, mine], 1)
     return jnp.swapaxes(jnp.where(core == 0, both, crossed), 1, 2)[:, None]

time: 425 us -> 392 us (0.922)
  local copies, waits for them, and re-layouts: 102 us -> 24.5 us
  waiting for transfers between devices: 140 us -> 183 us
  Pallas kernels: 64.9 us -> 71.4 us
    unnamed x98 -> x23, local copies, waits for them, and re-layouts: 78 us -> 3.32 us
    all_to_all x15, waiting for transfers between devices: 135 us -> 177 us  [local(): lax.all_to_all(jnp.broadcast_to(piece[None], (chips, *piece.shape)), CHIP...]
    pallas_call x16, Pallas kernels: 27.4 us -> 31.9 us  [solve(): pl.pallas_call(functools.partial(solve_level, level, rows, width_k, owner...]
  transfers between devices with their start and end apart: 21 -> 21, of which waited for: 16 -> 17; matrix products, arithmetic and copies ran while one was open for 4% -> 1% of each run, Pallas kernels for 9% -> 9%
where the time goes in v2:
time: 392 us; the launch traced here: 389 us
  waiting for transfers between devices  183 us (47%)
  starting transfers between devices  107 us (27%)
  Pallas kernels  71.4 us (18%)
  local copies, waits for them, and re-layouts  24.5 us (6%)
    all_to_all x15, waiting for transfers between devices, local(): lax.all_to_all(jnp.broadcast_to(piece[None], (chips, *piece.shape)), CHIP...  177 us
    all_to_all x15, starting transfers between devices, local(): lax.all_to_all(jnp.broadcast_to(piece[None], (chips, *piece.shape)), CHIP...  83.3 us
    pallas_call x16, Pallas kernels, solve(): pl.pallas_call(functools.partial(solve_level, level, rows, width_k, owner...  31.9 us
    pallas_call x14, Pallas kernels, absorb(): pl.pallas_call(functools.partial(absorb_level, level, rows, width_k, owne...  31 us
    ppermute x6, starting transfers between devices, swapped(): return lax.ppermute(value, CORE, SWAP)  23.5 us
    broadcast_in_dim x15, local copies, waits for them, and re-layouts, local(): jnp.broadcast_to(piece[None], (chips, *piece.shape))  19 us
  transfers between devices with their start and end apart: 21, of which 17 were waited for; matrix products, arithmetic and copies ran while one was open for 1% of the time, Pallas kernels for 9%

profile of v2, /device:TPU:1, one launch (start us, length us, event | category | flops | bytes accessed | tf_op | source)
XLA Modules:
  0.0 388.7 jit_solution(12820758816983440204)
XLA Ops:
  4.0 4.9 %collective-permute-done = f32[8,32,128]{2,1,0:T(8,128)S(1)} collective-permute-done((f32[8,32,128]{2,1,0:T(8,128)S(1)}, f32[8,32,128]{2,1,0:T(8,128)S(1)}, u32[]{:S(2)}, u32[]{:S(2)}) %collective-permute-start) | collective-permute-done | bytes 131104 | tf_op jit(solution)/shard_map/ppermute | solution.py:220
  12.5 11.1 %all-to-all-start = ((bf16[64,2,32,128]{3,2,1,0:T(8,128)(2,1)}), bf16[64,2,32,128]{3,2,1,0:T(8,128)(2,1)S(1)}, u32[]{:S(2)}, u32[]{:S(2)}) async-start(bf16[64,2,32,128]{3,2,1,0:T(8,128)(2,1)} %broadcast_in_dim.32), calls=%async_computation | async-start | bytes 2097152 | tf_op jit(solution)/shard_map/all_to_all | solution.py:294
  27.0 5.7 %list_edges.1 = (s32[256]{0:T(256)}, s32[65]{0:T(128)}) custom-call(s32[256]{0:T(256)} %pad_add_fusion.columns, s32[16]{0:T(128)} %pad_add_fusion.2.counts, s32[16]{0:T(128)} %copy-done.6, s32[1024]{0:T(1024)} %bitcast.112), custom_call_target="tpu_custom_call" | custom-call | tf_op jit(solution)/shard_map/list_edges/pallas_call | solution.py:236
  32.7 9.0 %all-to-all-done = bf16[64,2,32,128]{3,2,1,0:T(8,128)(2,1)S(1)} async-done(((bf16[64,2,32,128]{3,2,1,0:T(8,128)(2,1)}), bf16[64,2,32,128]{3,2,1,0:T(8,128)(2,1)S(1)}, u32[]{:S(2)}, u32[]{:S(2)}) %all-to-all-start) | async-done | bytes 1048608 | tf_op jit(solution)/shard_map/all_to_all | solution.py:294
  43.5 5.0 %solve_1.1.refs_1_ = bf16[2,32,128]{2,1,0:T(8,128)(2,1)S(1)} custom-call(s32[1]{0:T(128)} %bitcast.core, s32[16]{0:T(128)S(1)} %copy-done.7, s32[256]{0:T(256)S(1)} %copy-done.2, s32[65]{0:T(128)S(1)} %copy-done.4, bf16[128,32,128]{2,1,0:T(8,128)(2,1)S(1)} %bitcast.52, f32[16,32,128]{2,1,0:T(8,128)S(1)} %pad_maximum_fusion.refs_0_.refs_3_.held_in, ...), custom_call_target="tpu_custom_call" | custom-call | flops 4194304 | bytes 262144 | tf_op jit(solution)/shard_map/solve_1/pallas_call | solution.py:253
  49.8 4.8 %all-to-all-start.1 = ((bf16[64,2,32,128]{3,2,1,0:T(8,128)(2,1)}), bf16[64,2,32,128]{3,2,1,0:T(8,128)(2,1)S(1)}, u32[]{:S(2)}, u32[]{:S(2)}) async-start(bf16[64,2,32,128]{3,2,1,0:T(8,128)(2,1)} %broadcast_in_dim.33), calls=%async_computation.1 | async-start | bytes 2097152 | tf_op jit(solution)/shard_map/all_to_all | solution.py:294
  54.7 3.7 absorb_1.1.refs_3_.held_in
  58.4 13.1 %all-to-all-done.1 = bf16[64,2,32,128]{3,2,1,0:T(8,128)(2,1)S(1)} async-done(((bf16[64,2,32,128]{3,2,1,0:T(8,128)(2,1)}), bf16[64,2,32,128]{3,2,1,0:T(8,128)(2,1)S(1)}, u32[]{:S(2)}, u32[]{:S(2)}) %all-to-all-start.1) | async-done | bytes 1048608 | tf_op jit(solution)/shard_map/all_to_all | solution.py:294
  71.5 3.2 solve_2.1.refs_2_
  75.9 4.8 %all-to-all-start.2 = ((bf16[64,2,32,128]{3,2,1,0:T(8,128)(2,1)}), bf16[64,2,32,128]{3,2,1,0:T(8,128)(2,1)S(1)}, u32[]{:S(2)}, u32[]{:S(2)}) async-start(bf16[64,2,32,128]{3,2,1,0:T(8,128)(2,1)} %broadcast_in_dim.34), calls=%async_computation.2 | async-start | bytes 2097152 | tf_op jit(solution)/shard_map/all_to_all | solution.py:294
  80.8 2.2 absorb_2.1.refs_3_.held_in
  83.0 13.6 %all-to-all-done.2 = bf16[64,2,32,128]{3,2,1,0:T(8,128)(2,1)S(1)} async-done(((bf16[64,2,32,128]{3,2,1,0:T(8,128)(2,1)}), bf16[64,2,32,128]{3,2,1,0:T(8,128)(2,1)S(1)}, u32[]{:S(2)}, u32[]{:S(2)}) %all-to-all-start.2) | async-done | bytes 1048608 | tf_op jit(solution)/shard_map/all_to_all | solution.py:294
  98.7 6.4 %all-to-all-start.3 = ((bf16[64,2,32,128]{3,2,1,0:T(8,128)(2,1)}), bf16[64,2,32,128]{3,2,1,0:T(8,128)(2,1)S(1)}, u32[]{:S(2)}, u32[]{:S(2)}) async-start(bf16[64,2,32,128]{3,2,1,0:T(8,128)(2,1)} %broadcast_in_dim.35), calls=%async_computation.3 | async-start | bytes 2097152 | tf_op jit(solution)/shard_map/all_to_all | solution.py:294
  105.1 4.1 %absorb_3.1.refs_3_.held_in = f32[16,32,128]{2,1,0:T(8,128)S(1)} custom-call(s32[256]{0:T(256)S(1)} %copy-done.3, s32[65]{0:T(128)S(1)} %copy-done.5, bf16[128,32,128]{2,1,0:T(8,128)(2,1)S(1)} %bitcast.57, f32[16,32,128]{2,1,0:T(8,128)S(1)} %absorb_2.1.refs_3_.held_in, bf16[8,16,128,128]{3,2,1,0:T(8,128)(2,1)} %bitcast.88, ...), custom_call_target="tpu_custom_call" | custom-call | flops 33554432 | bytes 1048576 | tf_op jit(solution)/shard_map/absorb_3/pallas_call | solution.py:273
  109.3 10.5 %all-to-all-done.3 = bf16[64,2,32,128]{3,2,1,0:T(8,128)(2,1)S(1)} async-done(((bf16[64,2,32,128]{3,2,1,0:T(8,128)(2,1)}), bf16[64,2,32,128]{3,2,1,0:T(8,128)(2,1)S(1)}, u32[]{:S(2)}, u32[]{:S(2)}) %all-to-all-start.3) | async-done | bytes 1048608 | tf_op jit(solution)/shard_map/all_to_all | solution.py:294
  123.2 4.8 %all-to-all-start.4 = ((bf16[64,2,32,128]{3,2,1,0:T(8,128)(2,1)}), bf16[64,2,32,128]{3,2,1,0:T(8,128)(2,1)S(1)}, u32[]{:S(2)}, u32[]{:S(2)}) async-start(bf16[64,2,32,128]{3,2,1,0:T(8,128)(2,1)} %broadcast_in_dim.36), calls=%async_computation.4 | async-start | bytes 2097152 | tf_op jit(solution)/shard_map/all_to_all | solution.py:294
  128.0 3.5 absorb_4.1.refs_3_.held_in
  131.5 10.4 %all-to-all-done.4 = bf16[64,2,32,128]{3,2,1,0:T(8,128)(2,1)S(1)} async-done(((bf16[64,2,32,128]{3,2,1,0:T(8,128)(2,1)}), bf16[64,2,32,128]{3,2,1,0:T(8,128)(2,1)S(1)}, u32[]{:S(2)}, u32[]{:S(2)}) %all-to-all-start.4) | async-done | bytes 1048608 | tf_op jit(solution)/shard_map/all_to_all | solution.py:294
  144.1 5.5 %all-to-all-start.5 = ((bf16[64,2,32,128]{3,2,1,0:T(8,128)(2,1)}), bf16[64,2,32,128]{3,2,1,0:T(8,128)(2,1)S(1)}, u32[]{:S(2)}, u32[]{:S(2)}) async-start(bf16[64,2,32,128]{3,2,1,0:T(8,128)(2,1)} %broadcast_in_dim.37), calls=%async_computation.5 | async-start | bytes 2097152 | tf_op jit(solution)/shard_map/all_to_all | solution.py:294
  149.6 2.6 absorb_5.1.refs_3_.held_in
  152.3 11.1 %all-to-all-done.5 = bf16[64,2,32,128]{3,2,1,0:T(8,128)(2,1)S(1)} async-done(((bf16[64,2,32,128]{3,2,1,0:T(8,128)(2,1)}), bf16[64,2,32,128]{3,2,1,0:T(8,128)(2,1)S(1)}, u32[]{:S(2)}, u32[]{:S(2)}) %all-to-all-start.5) | async-done | bytes 1048608 | tf_op jit(solution)/shard_map/all_to_all | solution.py:294
  166.6 4.9 %all-to-all-start.6 = ((bf16[64,2,32,128]{3,2,1,0:T(8,128)(2,1)}), bf16[64,2,32,128]{3,2,1,0:T(8,128)(2,1)S(1)}, u32[]{:S(2)}, u32[]{:S(2)}) async-start(bf16[64,2,32,128]{3,2,1,0:T(8,128)(2,1)} %broadcast_in_dim.38), calls=%async_computation.6 | async-start | bytes 2097152 | tf_op jit(solution)/shard_map/all_to_all | solution.py:294
  171.5 2.8 absorb_6.1.refs_3_.held_in
  174.3 10.9 %all-to-all-done.6 = bf16[64,2,32,128]{3,2,1,0:T(8,128)(2,1)S(1)} async-done(((bf16[64,2,32,128]{3,2,1,0:T(8,128)(2,1)}), bf16[64,2,32,128]{3,2,1,0:T(8,128)(2,1)S(1)}, u32[]{:S(2)}, u32[]{:S(2)}) %all-to-all-start.6) | async-done | bytes 1048608 | tf_op jit(solution)/shard_map/all_to_all | solution.py:294
  188.5 4.8 %all-to-all-start.7 = ((bf16[64,2,32,128]{3,2,1,0:T(8,128)(2,1)}), bf16[64,2,32,128]{3,2,1,0:T(8,128)(2,1)S(1)}, u32[]{:S(2)}, u32[]{:S(2)}) async-start(bf16[64,2,32,128]{3,2,1,0:T(8,128)(2,1)} %broadcast_in_dim.39), calls=%async_computation.7 | async-start | bytes 2097152 | tf_op jit(solution)/shard_map/all_to_all | solution.py:294
  193.3 2.6 absorb_7.1.refs_3_.held_in
  195.9 11.0 %all-to-all-done.7 = bf16[64,2,32,128]{3,2,1,0:T(8,128)(2,1)S(1)} async-done(((bf16[64,2,32,128]{3,2,1,0:T(8,128)(2,1)}), bf16[64,2,32,128]{3,2,1,0:T(8,128)(2,1)S(1)}, u32[]{:S(2)}, u32[]{:S(2)}) %all-to-all-start.7) | async-done | bytes 1048608 | tf_op jit(solution)/shard_map/all_to_all | solution.py:294
  209.1 5.9 %all-to-all-start.8 = ((bf16[64,2,32,128]{3,2,1,0:T(8,128)(2,1)}), bf16[64,2,32,128]{3,2,1,0:T(8,128)(2,1)S(1)}, u32[]{:S(2)}, u32[]{:S(2)}) async-start(bf16[64,2,32,128]{3,2,1,0:T(8,128)(2,1)} %broadcast_in_dim.40), calls=%async_computation.8 | async-start | bytes 2097152 | tf_op jit(solution)/shard_map/all_to_all | solution.py:294
  215.0 2.8 absorb_8.1.refs_3_.held_in
  217.8 10.8 %all-to-all-done.8 = bf16[64,2,32,128]{3,2,1,0:T(8,128)(2,1)S(1)} async-done(((bf16[64,2,32,128]{3,2,1,0:T(8,128)(2,1)}), bf16[64,2,32,128]{3,2,1,0:T(8,128)(2,1)S(1)}, u32[]{:S(2)}, u32[]{:S(2)}) %all-to-all-start.8) | async-done | bytes 1048608 | tf_op jit(solution)/shard_map/all_to_all | solution.py:294
  228.5 2.6 solve_9.1.refs_9_
  232.4 4.7 %all-to-all-start.9 = ((bf16[64,2,32,128]{3,2,1,0:T(8,128)(2,1)}), bf16[64,2,32,128]{3,2,1,0:T(8,128)(2,1)S(1)}, u32[]{:S(2)}, u32[]{:S(2)}) async-start(bf16[64,2,32,128]{3,2,1,0:T(8,128)(2,1)} %broadcast_in_dim.41), calls=%async_computation.9 | async-start | bytes 2097152 | tf_op jit(solution)/shard_map/all_to_all | solution.py:294
  237.7 12.9 %all-to-all-done.9 = bf16[64,2,32,128]{3,2,1,0:T(8,128)(2,1)S(1)} async-done(((bf16[64,2,32,128]{3,2,1,0:T(8,128)(2,1)}), bf16[64,2,32,128]{3,2,1,0:T(8,128)(2,1)S(1)}, u32[]{:S(2)}, u32[]{:S(2)}) %all-to-all-start.9) | async-done | bytes 1048608 | tf_op jit(solution)/shard_map/all_to_all | solution.py:294
  252.8 6.0 %all-to-all-start.10 = ((bf16[64,2,32,128]{3,2,1,0:T(8,128)(2,1)}), bf16[64,2,32,128]{3,2,1,0:T(8,128)(2,1)S(1)}, u32[]{:S(2)}, u32[]{:S(2)}) async-start(bf16[64,2,32,128]{3,2,1,0:T(8,128)(2,1)} %broadcast_in_dim.42), calls=%async_computation.10 | async-start | bytes 2097152 | tf_op jit(solution)/shard_map/all_to_all | solution.py:294
  260.4 12.0 %all-to-all-done.10 = bf16[64,2,32,128]{3,2,1,0:T(8,128)(2,1)S(1)} async-done(((bf16[64,2,32,128]{3,2,1,0:T(8,128)(2,1)}), bf16[64,2,32,128]{3,2,1,0:T(8,128)(2,1)S(1)}, u32[]{:S(2)}, u32[]{:S(2)}) %all-to-all-start.10) | async-done | bytes 1048608 | tf_op jit(solution)/shard_map/all_to_all | solution.py:294
  272.3 2.3 solve_11.1.refs_11_
  275.9 4.7 %all-to-all-start.11 = ((bf16[64,2,32,128]{3,2,1,0:T(8,128)(2,1)}), bf16[64,2,32,128]{3,2,1,0:T(8,128)(2,1)S(1)}, u32[]{:S(2)}, u32[]{:S(2)}) async-start(bf16[64,2,32,128]{3,2,1,0:T(8,128)(2,1)} %broadcast_in_dim.43), calls=%async_computation.11 | async-start | bytes 2097152 | tf_op jit(solution)/shard_map/all_to_all | solution.py:294
  282.1 12.0 %all-to-all-done.11 = bf16[64,2,32,128]{3,2,1,0:T(8,128)(2,1)S(1)} async-done(((bf16[64,2,32,128]{3,2,1,0:T(8,128)(2,1)}), bf16[64,2,32,128]{3,2,1,0:T(8,128)(2,1)S(1)}, u32[]{:S(2)}, u32[]{:S(2)}) %all-to-all-start.11) | async-done | bytes 1048608 | tf_op jit(solution)/shard_map/all_to_all | solution.py:294
  297.5 4.7 %all-to-all-start.12 = ((bf16[64,2,32,128]{3,2,1,0:T(8,128)(2,1)}), bf16[64,2,32,128]{3,2,1,0:T(8,128)(2,1)S(1)}, u32[]{:S(2)}, u32[]{:S(2)}) async-start(bf16[64,2,32,128]{3,2,1,0:T(8,128)(2,1)} %broadcast_in_dim.44), calls=%async_computation.12 | async-start | bytes 2097152 | tf_op jit(solution)/shard_map/all_to_all | solution.py:294
  302.9 12.9 %all-to-all-done.12 = bf16[64,2,32,128]{3,2,1,0:T(8,128)(2,1)S(1)} async-done(((bf16[64,2,32,128]{3,2,1,0:T(8,128)(2,1)}), bf16[64,2,32,128]{3,2,1,0:T(8,128)(2,1)S(1)}, u32[]{:S(2)}, u32[]{:S(2)}) %all-to-all-start.12) | async-done | bytes 1048608 | tf_op jit(solution)/shard_map/all_to_all | solution.py:294
  315.8 2.4 solve_13.1.refs_13_
  319.5 4.7 %all-to-all-start.13 = ((bf16[64,2,32,128]{3,2,1,0:T(8,128)(2,1)}), bf16[64,2,32,128]{3,2,1,0:T(8,128)(2,1)S(1)}, u32[]{:S(2)}, u32[]{:S(2)}) async-start(bf16[64,2,32,128]{3,2,1,0:T(8,128)(2,1)} %broadcast_in_dim.45), calls=%async_computation.13 | async-start | bytes 2097152 | tf_op jit(solution)/shard_map/all_to_all | solution.py:294
  324.8 12.9 %all-to-all-done.13 = bf16[64,2,32,128]{3,2,1,0:T(8,128)(2,1)S(1)} async-done(((bf16[64,2,32,128]{3,2,1,0:T(8,128)(2,1)}), bf16[64,2,32,128]{3,2,1,0:T(8,128)(2,1)S(1)}, u32[]{:S(2)}, u32[]{:S(2)}) %all-to-all-start.13) | async-done | bytes 1048608 | tf_op jit(solution)/shard_map/all_to_all | solution.py:294
  340.1 5.5 %all-to-all-start.14 = ((bf16[64,2,32,128]{3,2,1,0:T(8,128)(2,1)}), bf16[64,2,32,128]{3,2,1,0:T(8,128)(2,1)S(1)}, u32[]{:S(2)}, u32[]{:S(2)}) async-start(bf16[64,2,32,128]{3,2,1,0:T(8,128)(2,1)} %broadcast_in_dim.46), calls=%async_computation.14 | async-start | bytes 2097152 | tf_op jit(solution)/shard_map/all_to_all | solution.py:294
  347.2 14.2 %all-to-all-done.14 = bf16[64,2,32,128]{3,2,1,0:T(8,128)(2,1)S(1)} async-done(((bf16[64,2,32,128]{3,2,1,0:T(8,128)(2,1)}), bf16[64,2,32,128]{3,2,1,0:T(8,128)(2,1)S(1)}, u32[]{:S(2)}, u32[]{:S(2)}) %all-to-all-start.14) | async-done | bytes 1048608 | tf_op jit(solution)/shard_map/all_to_all | solution.py:294
  361.4 2.3 solve_15.1.refs_15_
  363.7 2.7 collect_rows.1
  366.4 20.7 %collective-permute-start.5 = (bf16[8,32,128]{2,1,0:T(8,128)(2,1)S(1)}, bf16[8,32,128]{2,1,0:T(8,128)(2,1)S(1)}, u32[]{:S(2)}, u32[]{:S(2)}) collective-permute-start(bf16[8,32,128]{2,1,0:T(8,128)(2,1)S(1)} %get-tuple-element.12), channel_id=1, source_target_pairs={{0,1},{1,0},{2,3},{3,2},{4,5},{5,4},{6,7},{7,6},{8,9},{9,8},{10,11... | collective-permute-start | bytes 196616 | tf_op jit(solution)/shard_map/ppermute | solution.py:220
  (74 shorter events, 51.7 us)
Async XLA Ops:
  0.0 9.0 %collective-permute-start.1 = (bf16[8,16,128,128]{3,2,1,0:T(8,128)(2,1)}, bf16[8,16,128,128]{3,2,1,0:T(8,128)(2,1)}, u32[]{:S(2)}, u32[]{:S(2)}) collective-permute-start(bf16[8,16,128,128]{3,2,1,0:T(8,128)(2,1)} %bitcast.81), channel_id=1, source_target_pairs={{0,1},{1,0},{2,3},{3,2},{4,5},{5,4},{6,7},{7,6},{8,9},{9,8},{10,11... | collective-permute-start | bytes 12582920 | tf_op jit(solution)/shard_map/ppermute | solution.py:220
  1.4 7.6 %collective-permute-start.2 = (bf16[8,128,128]{2,1,0:T(8,128)(2,1)}, bf16[8,128,128]{2,1,0:T(8,128)(2,1)S(1)}, u32[]{:S(2)}, u32[]{:S(2)}) collective-permute-start(bf16[8,128,128]{2,1,0:T(8,128)(2,1)} %bitcast.35), channel_id=1, source_target_pairs={{0,1},{1,0},{2,3},{3,2},{4,5},{5,4},{6,7},{7,6},{8,9},{9,8},{10,11... | collective-permute-start | bytes 786440 | tf_op jit(solution)/shard_map/ppermute | solution.py:220
  2.4 6.6 %collective-permute-start = (f32[8,32,128]{2,1,0:T(8,128)S(1)}, f32[8,32,128]{2,1,0:T(8,128)S(1)}, u32[]{:S(2)}, u32[]{:S(2)}) collective-permute-start(f32[8,32,128]{2,1,0:T(8,128)S(1)} %get-tuple-element.16), channel_id=1, source_target_pairs={{0,1},{1,0},{2,3},{3,2},{4,5},{5,4},{6,7},{7,6},{8,9},{9,8},{10,11... | collective-permute-start | bytes 393224 | tf_op jit(solution)/shard_map/ppermute | solution.py:220
  4.0 7.2 %copy-start.6 = (s32[16]{0:T(128)}, s32[16]{0:T(128)S(1)}, u32[]{:S(2)}) copy-start(s32[16]{0:T(128)S(1)} %pad_add_fusion.1.row_levels) | copy-start | bytes 196
  9.0 1.0 copy-start
  9.9 13.6 %copy-start.10 = (s32[8,1]{0,1:T(1,128)S(1)}, s32[8,1]{0,1:T(1,128)}, u32[]{:S(2)}) copy-start(s32[8,1]{0,1:T(1,128)} %param.10) | copy-start | bytes 100
  9.9 14.4 %copy-start.9 = (s32[8,1,16]{2,1,0:T(1,128)S(1)}, s32[8,1,16]{2,1,0:T(1,128)}, u32[]{:S(2)}) copy-start(s32[8,1,16]{2,1,0:T(1,128)} %param.9) | copy-start | bytes 1540
  9.9 31.7 %copy-start.1 = (bf16[8,1,128,128]{3,2,1,0:T(8,128)(2,1)S(1)}, bf16[8,1,128,128]{3,2,1,0:T(8,128)(2,1)}, u32[]{:S(2)}) copy-start(bf16[8,1,128,128]{3,2,1,0:T(8,128)(2,1)} %param.8) | copy-start | bytes 786436
  12.5 29.2 %all-to-all-start = ((bf16[64,2,32,128]{3,2,1,0:T(8,128)(2,1)}), bf16[64,2,32,128]{3,2,1,0:T(8,128)(2,1)S(1)}, u32[]{:S(2)}, u32[]{:S(2)}) async-start(bf16[64,2,32,128]{3,2,1,0:T(8,128)(2,1)} %broadcast_in_dim.32), calls=%async_computation | async-start | bytes 2097152 | tf_op jit(solution)/shard_map/all_to_all | solution.py:294
  23.6 2.1 collective-permute-start.4
  24.3 2.0 collective-permute-start.3
  41.7 0.6 copy-start.2
  42.3 0.6 copy-start.4
  42.9 0.6 copy-start.7
  43.5 11.1 %copy-start.3 = (s32[256]{0:T(256)S(1)}, s32[256]{0:T(256)}, u32[]{:S(2)}) copy-start(s32[256]{0:T(256)} %get-tuple-element.9.refs_0_.edges) | copy-start | bytes 3076
  43.5 11.1 %copy-start.5 = (s32[65]{0:T(128)S(1)}, s32[65]{0:T(128)}, u32[]{:S(2)}) copy-start(s32[65]{0:T(128)} %get-tuple-element.10.refs_1_.starts) | copy-start | bytes 784
  49.8 21.7 %all-to-all-start.1 = ((bf16[64,2,32,128]{3,2,1,0:T(8,128)(2,1)}), bf16[64,2,32,128]{3,2,1,0:T(8,128)(2,1)S(1)}, u32[]{:S(2)}, u32[]{:S(2)}) async-start(bf16[64,2,32,128]{3,2,1,0:T(8,128)(2,1)} %broadcast_in_dim.33), calls=%async_computation.1 | async-start | bytes 2097152 | tf_op jit(solution)/shard_map/all_to_all | solution.py:294
  54.7 16.8 %copy-start.8 = (s32[16]{0:T(128)S(1)}, s32[16]{0:T(128)}, u32[]{:S(2)}) copy-start(s32[16]{0:T(128)} %copy-done.6) | copy-start | bytes 196
  75.9 20.6 %all-to-all-start.2 = ((bf16[64,2,32,128]{3,2,1,0:T(8,128)(2,1)}), bf16[64,2,32,128]{3,2,1,0:T(8,128)(2,1)S(1)}, u32[]{:S(2)}, u32[]{:S(2)}) async-start(bf16[64,2,32,128]{3,2,1,0:T(8,128)(2,1)} %broadcast_in_dim.34), calls=%async_computation.2 | async-start | bytes 2097152 | tf_op jit(solution)/shard_map/all_to_all | solution.py:294
  98.7 21.1 %all-to-all-start.3 = ((bf16[64,2,32,128]{3,2,1,0:T(8,128)(2,1)}), bf16[64,2,32,128]{3,2,1,0:T(8,128)(2,1)S(1)}, u32[]{:S(2)}, u32[]{:S(2)}) async-start(bf16[64,2,32,128]{3,2,1,0:T(8,128)(2,1)} %broadcast_in_dim.35), calls=%async_computation.3 | async-start | bytes 2097152 | tf_op jit(solution)/shard_map/all_to_all | solution.py:294
  123.2 18.7 %all-to-all-start.4 = ((bf16[64,2,32,128]{3,2,1,0:T(8,128)(2,1)}), bf16[64,2,32,128]{3,2,1,0:T(8,128)(2,1)S(1)}, u32[]{:S(2)}, u32[]{:S(2)}) async-start(bf16[64,2,32,128]{3,2,1,0:T(8,128)(2,1)} %broadcast_in_dim.36), calls=%async_computation.4 | async-start | bytes 2097152 | tf_op jit(solution)/shard_map/all_to_all | solution.py:294
  144.1 19.3 %all-to-all-start.5 = ((bf16[64,2,32,128]{3,2,1,0:T(8,128)(2,1)}), bf16[64,2,32,128]{3,2,1,0:T(8,128)(2,1)S(1)}, u32[]{:S(2)}, u32[]{:S(2)}) async-start(bf16[64,2,32,128]{3,2,1,0:T(8,128)(2,1)} %broadcast_in_dim.37), calls=%async_computation.5 | async-start | bytes 2097152 | tf_op jit(solution)/shard_map/all_to_all | solution.py:294
  166.6 18.6 %all-to-all-start.6 = ((bf16[64,2,32,128]{3,2,1,0:T(8,128)(2,1)}), bf16[64,2,32,128]{3,2,1,0:T(8,128)(2,1)S(1)}, u32[]{:S(2)}, u32[]{:S(2)}) async-start(bf16[64,2,32,128]{3,2,1,0:T(8,128)(2,1)} %broadcast_in_dim.38), calls=%async_computation.6 | async-start | bytes 2097152 | tf_op jit(solution)/shard_map/all_to_all | solution.py:294
  188.5 18.5 %all-to-all-start.7 = ((bf16[64,2,32,128]{3,2,1,0:T(8,128)(2,1)}), bf16[64,2,32,128]{3,2,1,0:T(8,128)(2,1)S(1)}, u32[]{:S(2)}, u32[]{:S(2)}) async-start(bf16[64,2,32,128]{3,2,1,0:T(8,128)(2,1)} %broadcast_in_dim.39), calls=%async_computation.7 | async-start | bytes 2097152 | tf_op jit(solution)/shard_map/all_to_all | solution.py:294
  209.1 19.4 %all-to-all-start.8 = ((bf16[64,2,32,128]{3,2,1,0:T(8,128)(2,1)}), bf16[64,2,32,128]{3,2,1,0:T(8,128)(2,1)S(1)}, u32[]{:S(2)}, u32[]{:S(2)}) async-start(bf16[64,2,32,128]{3,2,1,0:T(8,128)(2,1)} %broadcast_in_dim.40), calls=%async_computation.8 | async-start | bytes 2097152 | tf_op jit(solution)/shard_map/all_to_all | solution.py:294
  232.4 18.2 %all-to-all-start.9 = ((bf16[64,2,32,128]{3,2,1,0:T(8,128)(2,1)}), bf16[64,2,32,128]{3,2,1,0:T(8,128)(2,1)S(1)}, u32[]{:S(2)}, u32[]{:S(2)}) async-start(bf16[64,2,32,128]{3,2,1,0:T(8,128)(2,1)} %broadcast_in_dim.41), calls=%async_computation.9 | async-start | bytes 2097152 | tf_op jit(solution)/shard_map/all_to_all | solution.py:294
  252.8 19.6 %all-to-all-start.10 = ((bf16[64,2,32,128]{3,2,1,0:T(8,128)(2,1)}), bf16[64,2,32,128]{3,2,1,0:T(8,128)(2,1)S(1)}, u32[]{:S(2)}, u32[]{:S(2)}) async-start(bf16[64,2,32,128]{3,2,1,0:T(8,128)(2,1)} %broadcast_in_dim.42), calls=%async_computation.10 | async-start | bytes 2097152 | tf_op jit(solution)/shard_map/all_to_all | solution.py:294
  275.9 18.2 %all-to-all-start.11 = ((bf16[64,2,32,128]{3,2,1,0:T(8,128)(2,1)}), bf16[64,2,32,128]{3,2,1,0:T(8,128)(2,1)S(1)}, u32[]{:S(2)}, u32[]{:S(2)}) async-start(bf16[64,2,32,128]{3,2,1,0:T(8,128)(2,1)} %broadcast_in_dim.43), calls=%async_computation.11 | async-start | bytes 2097152 | tf_op jit(solution)/shard_map/all_to_all | solution.py:294
  297.5 18.3 %all-to-all-start.12 = ((bf16[64,2,32,128]{3,2,1,0:T(8,128)(2,1)}), bf16[64,2,32,128]{3,2,1,0:T(8,128)(2,1)S(1)}, u32[]{:S(2)}, u32[]{:S(2)}) async-start(bf16[64,2,32,128]{3,2,1,0:T(8,128)(2,1)} %broadcast_in_dim.44), calls=%async_computation.12 | async-start | bytes 2097152 | tf_op jit(solution)/shard_map/all_to_all | solution.py:294
  319.5 18.2 %all-to-all-start.13 = ((bf16[64,2,32,128]{3,2,1,0:T(8,128)(2,1)}), bf16[64,2,32,128]{3,2,1,0:T(8,128)(2,1)S(1)}, u32[]{:S(2)}, u32[]{:S(2)}) async-start(bf16[64,2,32,128]{3,2,1,0:T(8,128)(2,1)} %broadcast_in_dim.45), calls=%async_computation.13 | async-start | bytes 2097152 | tf_op jit(solution)/shard_map/all_to_all | solution.py:294
  340.1 21.3 %all-to-all-start.14 = ((bf16[64,2,32,128]{3,2,1,0:T(8,128)(2,1)}), bf16[64,2,32,128]{3,2,1,0:T(8,128)(2,1)S(1)}, u32[]{:S(2)}, u32[]{:S(2)}) async-start(bf16[64,2,32,128]{3,2,1,0:T(8,128)(2,1)} %broadcast_in_dim.46), calls=%async_computation.14 | async-start | bytes 2097152 | tf_op jit(solution)/shard_map/all_to_all | solution.py:294
  366.4 21.6 %collective-permute-start.5 = (bf16[8,32,128]{2,1,0:T(8,128)(2,1)S(1)}, bf16[8,32,128]{2,1,0:T(8,128)(2,1)S(1)}, u32[]{:S(2)}, u32[]{:S(2)}) collective-permute-start(bf16[8,32,128]{2,1,0:T(8,128)(2,1)S(1)} %get-tuple-element.12), channel_id=1, source_target_pairs={{0,1},{1,0},{2,3},{3,2},{4,5},{5,4},{6,7},{7,6},{8,9},{9,8},{10,11... | collective-permute-start | bytes 196616 | tf_op jit(solution)/shard_map/ppermute | solution.py:220

commit v3 on v0

v3 whole, which is shorter than its diff:
```python
import functools

import jax
import jax.numpy as jnp
from jax import lax
from jax.experimental import pallas as pl
from jax.experimental.pallas import tpu as pltpu
from jax.sharding import Mesh
from jax.sharding import PartitionSpec as P

LEVELS = 16
ROWS = ("rows_0", "rows_1", "rows_2", "rows_3")
CHIPS = ("rows_0", "rows_1", "rows_2")
CORE = "rows_3"
SWAP = ((0, 1), (1, 0))
MEMBERS = 2
KEYS = LEVELS * 2 * MEMBERS
RING = 8
GROUP = 3
READY = 6
GRANT = 50 << 20


def smem():
    return pl.BlockSpec(memory_space=pltpu.SMEM)


def vmem():
    return pl.BlockSpec(memory_space=pltpu.VMEM)


def anywhere():
    return pl.BlockSpec(memory_space=pltpu.HBM)


def bucket(level, urgent, member):
    return (level * 2 + (0 if urgent else 1)) * MEMBERS + member


def times_transposed(rows, tile):
    return lax.dot_general(
        rows, tile, (((1,), (1,)), ((), ())), preferred_element_type=jnp.float32
    )


def device_of(member, owners_index):
    core = lax.axis_index(CORE)
    return owners_index + (1 - 2 * core) * member


def slot_of(member):
    core = lax.axis_index(CORE)
    return core if member == 0 else 1 - core


def find_row(levels, owners, member, rows, level):
    own = device_of(member, lax.axis_index(ROWS))
    pick = jnp.int32(-1)
    for s in range(rows):
        pick = jnp.where(levels[s * owners + own] == level, s, pick)
    return pick


def list_edges(owners, columns, counts, levels, edges, starts, fill):
    rows = counts.shape[0] // MEMBERS
    width_k = columns.shape[0] // counts.shape[0]

    def clear(key, unused):
        fill[key] = 0
        return unused

    lax.fori_loop(0, KEYS, clear, 0)

    def over_slots(visit):
        for member in range(MEMBERS):
            own = device_of(member, lax.axis_index(ROWS))

            def each_row(row, unused, member=member, own=own):
                next_level = levels[row * owners + own]
                at = member * rows + row

                def each_slot(slot, unused):
                    col = columns[at * width_k + slot]
                    level = levels[col]
                    late = jnp.where(next_level == level + 1, 0, 1)
                    visit(at * width_k + slot, col, (level * 2 + late) * MEMBERS + member)
                    return unused

                return lax.fori_loop(0, counts[at], each_slot, unused)

            lax.fori_loop(0, rows, each_row, 0)

    def count(slot, col, key):
        fill[key] = fill[key] + 1

    over_slots(count)

    def prefix(key, total):
        starts[key] = total
        here = fill[key]
        fill[key] = total
        return total + here

    starts[KEYS] = lax.fori_loop(0, KEYS, prefix, 0)

    def place(slot, col, key):
        at = fill[key]
        edges[at] = slot * owners + lax.rem(col, owners)
        fill[key] = at + 1

    over_slots(place)


def spread_piece(piece, spread):
    value = piece[...]
    for chip in range(spread.shape[0]):
        spread[chip] = value


def solve_first(rows, owners, levels, held, own_inverse, their_inverse, piece, spread, buf, sems):
    inverses = (own_inverse, their_inverse)
    picks = [find_row(levels, owners, member, rows, 0) for member in range(MEMBERS)]

    def copy(member):
        return pltpu.make_async_copy(
            inverses[member].at[jnp.maximum(picks[member], 0)], buf.at[member], sems.at[member]
        )

    for member in range(MEMBERS):
        copy(member).start()
    for member in range(MEMBERS):
        at = slot_of(member)
        copy(member).wait()
        row = held[member * rows + jnp.maximum(picks[member], 0)].astype(jnp.bfloat16)
        solved = times_transposed(row, buf[member])
        piece[at] = jnp.where(picks[member] >= 0, solved, 0.0).astype(jnp.bfloat16)
    spread_piece(piece, spread)


def prepare_level(level, rows, width_k, owners, levels, edges, starts, held_in, *refs):
    if level:
        store, *refs = refs
    tiles, inverses = refs[:MEMBERS], refs[MEMBERS : 2 * MEMBERS]
    held, totals, ready, info, buf, blocks, sems, block_sems, ready_sems = refs[2 * MEMBERS :]
    slots = 1 + READY
    picks = [find_row(levels, owners, member, rows, level + 1) for member in range(MEMBERS)]

    def tile_of(member, i):
        code = edges[i] // owners - member * rows * width_k
        return tiles[member].at[code // width_k, lax.rem(code, width_k)]

    def ready_copy(member, place, source):
        return pltpu.make_async_copy(
            source, ready.at[member, place], ready_sems.at[member * slots + place]
        )

    def late_copy(member, first, i):
        at = lax.rem(i, RING)
        return pltpu.make_async_copy(tile_of(member, first + i), buf.at[at], sems.at[at])

    def block_copy(first, i):
        at = lax.rem(i, RING)
        place = lax.rem(edges[first + i], owners)
        return pltpu.make_async_copy(store.at[level - 1, place], blocks.at[at], block_sems.at[at])

    late = []
    if level:
        for member in range(MEMBERS):
            key = bucket(level - 1, False, member)
            late.append((starts[key], starts[key + 1] - starts[key]))
        first, many = late[0]

        def begin(i, unused, first=first):
            late_copy(0, first, i).start()
            block_copy(first, i).start()
            return unused

        lax.fori_loop(0, jnp.minimum(many, RING), begin, 0)

    urgent = []
    for member in range(MEMBERS):
        key = bucket(level, True, member)
        first, many = starts[key], starts[key + 1] - starts[key]
        urgent.append(jnp.minimum(many, READY))
        info[member] = jnp.where(picks[member] >= 0, many, 0)
        ready_copy(member, 0, inverses[member].at[jnp.maximum(picks[member], 0)]).start()

        def fetch(i, unused, member=member, first=first):
            ready_copy(member, 1 + i, tile_of(member, first + i)).start()
            return unused

        lax.fori_loop(0, urgent[member], fetch, 0)

    held[...] = held_in[...]
    if level:
        for member in range(MEMBERS):
            first, many = late[member]
            if member:

                def begin(i, unused, member=member, first=first):
                    late_copy(member, first, i).start()
                    block_copy(first, i).start()
                    return unused

                lax.fori_loop(0, jnp.minimum(many, RING), begin, 0)

            def absorb(i, unused, member=member, first=first, many=many):
                late_copy(member, first, i).wait()
                block_copy(first, i).wait()
                row = edges[first + i] // (owners * width_k)
                at = lax.rem(i, RING)
                given = times_transposed(blocks[at], buf[at])
                held[row] = held[row] - given

                @pl.when(i + RING < many)
                def _():
                    late_copy(member, first, i + RING).start()
                    block_copy(first, i + RING).start()

                return unused

            lax.fori_loop(0, many, absorb, 0)

    for member in range(MEMBERS):
        totals[member] = held[member * rows + jnp.maximum(picks[member], 0)]
        ready_copy(member, 0, inverses[member].at[0]).wait()

        def settle(i, unused, member=member):
            ready_copy(member, 1 + i, tiles[member].at[0, 0]).wait()
            return unused

        lax.fori_loop(0, urgent[member], settle, 0)


def solve_level(level, width_k, owners, edges, starts, info, totals, ready, received, *refs):
    tiles, refs = refs[:MEMBERS], refs[MEMBERS:]
    last = level == LEVELS - 1
    if last:
        piece, buf, sems = refs
    else:
        piece, spread, store, buf, sems, keep_sem = refs[1 if level > 1 else 0 :]
        keep = pltpu.make_async_copy(received, store.at[level - 1], keep_sem.at[0])
        keep.start()
    extra = width_k - READY

    def extra_copy(member, i):
        code = edges[starts[bucket(level - 1, True, member)] + i] // owners
        code = code - member * tiles[member].shape[0] * width_k
        at = member * extra + i - READY
        return pltpu.make_async_copy(
            tiles[member].at[code // width_k, lax.rem(code, width_k)], buf.at[at], sems.at[at]
        )

    for member in range(MEMBERS):

        def begin(i, unused, member=member):
            extra_copy(member, i).start()
            return unused

        lax.fori_loop(READY, info[member], begin, 0)

    for member in range(MEMBERS):
        at = slot_of(member)
        many = info[member]

        @pl.when(many == 0)
        def _(at=at):
            piece[at] = jnp.zeros(piece.shape[1:], piece.dtype)

        @pl.when(many > 0)
        def _(member=member, at=at, many=many):
            first = starts[bucket(level - 1, True, member)]
            near = jnp.minimum(many, READY)

            def absorb(group, total):
                for u in range(GROUP):
                    i = group * GROUP + u
                    here = jnp.minimum(i, near - 1)
                    block = received[lax.rem(edges[first + here], owners)]
                    block = jnp.where(i < near, block, jnp.zeros_like(block))
                    total = total - times_transposed(block, ready[member, 1 + here])
                return total

            def absorb_extra(i, total):
                extra_copy(member, i).wait()
                block = received[lax.rem(edges[first + i], owners)]
                return total - times_transposed(block, buf[member * extra + i - READY])

            total = lax.fori_loop(0, (near + GROUP - 1) // GROUP, absorb, totals[member])
            total = lax.fori_loop(READY, many, absorb_extra, total)
            solved = times_transposed(total.astype(jnp.bfloat16), ready[member, 0])
            piece[at] = solved.astype(jnp.bfloat16)

    if not last:
        spread_piece(piece, spread)
        keep.wait()


def collect_rows(rows, owners, base, levels, *refs):
    pieces, outs = refs[:-MEMBERS], refs[-MEMBERS:]
    if base:
        befores, pieces = pieces[:MEMBERS], pieces[MEMBERS:]
    for member in range(MEMBERS):
        if base:
            outs[member][...] = befores[member][...]
        for i, piece in enumerate(pieces):
            row = find_row(levels, owners, member, rows, base + i)

            @pl.when(row >= 0)
            def _(piece=piece, member=member, row=row):
                outs[member][row] = piece[slot_of(member)]


def local(right_sides, lower_tiles, diag_inverse, tile_columns, tile_counts, level_sets):
    owners = lax.axis_size(ROWS)
    chips = lax.axis_size(CHIPS)
    core = lax.axis_index(CORE)
    rows, unused_one, width_k = tile_columns.shape
    part = right_sides.shape[3] // MEMBERS
    lanes = right_sides.shape[2]
    block = (part, lanes)
    tile = lower_tiles.shape[3:]

    def swapped(value):
        return lax.ppermute(value, CORE, SWAP)

    levels = level_sets.reshape(-1)
    rhs = jnp.swapaxes(right_sides[:, 0], 1, 2)
    rhs_mine = lax.dynamic_slice_in_dim(rhs, core * part, part, 1)
    rhs_theirs = swapped(lax.dynamic_slice_in_dim(rhs, (1 - core) * part, part, 1))
    held = jnp.concatenate([rhs_mine, rhs_theirs])
    inverses = (diag_inverse[:, 0], swapped(diag_inverse[:, 0]))

    def call(kernel, name, out_shape, out_specs, in_specs, scratch, operands, flops, moved):
        return pl.pallas_call(
            kernel,
            out_shape=out_shape,
            in_specs=in_specs,
            out_specs=out_specs,
            scratch_shapes=scratch,
            compiler_params=pltpu.CompilerParams(vmem_limit_bytes=GRANT),
            cost_estimate=pl.CostEstimate(flops=flops, bytes_accessed=moved, transcendentals=0),
            name=name,
        )(*operands)

    piece_shape = jax.ShapeDtypeStruct((MEMBERS, *block), jnp.bfloat16)
    spread_shape = jax.ShapeDtypeStruct((chips, MEMBERS, *block), jnp.bfloat16)

    store_shape = jax.ShapeDtypeStruct((LEVELS - 2, owners, *block), jnp.bfloat16)

    def exchanged(spread):
        return lax.all_to_all(spread, CHIPS, 0, 0, tiled=True).reshape(owners, *block)

    piece, spread = call(
        functools.partial(solve_first, rows, owners),
        "solve_0",
        (piece_shape, spread_shape),
        (vmem(), vmem()),
        [smem(), vmem(), anywhere(), anywhere()],
        [pltpu.VMEM((MEMBERS, *tile), jnp.bfloat16), pltpu.SemaphoreType.DMA((MEMBERS,))],
        (levels, held, *inverses),
        4 << 20,
        1 << 18,
    )
    pieces = [piece]
    arriving = exchanged(spread)

    own_tiles, columns_own, counts_own, unused_tie = lax.optimization_barrier(
        (lower_tiles[:, 0], tile_columns[:, 0], tile_counts[:, 0], piece)
    )
    tiles = (own_tiles, swapped(own_tiles))
    columns = jnp.concatenate([columns_own, swapped(columns_own)]).reshape(-1)
    counts = jnp.concatenate([counts_own, swapped(counts_own)])
    edges, starts = call(
        functools.partial(list_edges, owners),
        "list_edges",
        (
            jax.ShapeDtypeStruct((columns.size,), jnp.int32),
            jax.ShapeDtypeStruct((KEYS + 1,), jnp.int32),
        ),
        (smem(), smem()),
        [smem()] * 3,
        [pltpu.SMEM((KEYS,), jnp.int32)],
        (columns, counts, levels),
        8 << 20,
        1 << 20,
    )

    def prepare(level, store, held):
        return call(
            functools.partial(prepare_level, level, rows, width_k, owners),
            f"prepare_{level}",
            (
                jax.ShapeDtypeStruct(held.shape, held.dtype),
                jax.ShapeDtypeStruct((MEMBERS, *block), jnp.float32),
                jax.ShapeDtypeStruct((MEMBERS, 1 + READY, *tile), jnp.bfloat16),
                jax.ShapeDtypeStruct((MEMBERS,), jnp.int32),
            ),
            (vmem(), vmem(), vmem(), smem()),
            [smem()] * 3 + [vmem()] + [anywhere()] * (2 * MEMBERS + (1 if level else 0)),
            [
                pltpu.VMEM((RING, *tile), jnp.bfloat16),
                pltpu.VMEM((RING, *block), jnp.bfloat16),
                pltpu.SemaphoreType.DMA((RING,)),
                pltpu.SemaphoreType.DMA((RING,)),
                pltpu.SemaphoreType.DMA((MEMBERS * (1 + READY),)),
            ],
            (levels, edges, starts, held, *((store,) if level else ()), *tiles, *inverses),
            32 << 20,
            1 << 20,
        )

    def solve(level, received, store, totals, ready, info):
        last = level == LEVELS - 1
        held_store = (store,) if 1 < level and not last else ()
        operands = (edges, starts, info, totals, ready, received, *tiles, *held_store)
        extra = MEMBERS * (width_k - READY)
        return pl.pallas_call(
            functools.partial(solve_level, level, width_k, owners),
            out_shape=(piece_shape,) if last else (piece_shape, spread_shape, store_shape),
            in_specs=[smem()] * 3 + [vmem()] * 3 + [anywhere()] * (MEMBERS + len(held_store)),
            out_specs=(vmem(),) if last else (vmem(), vmem(), anywhere()),
            scratch_shapes=[
                pltpu.VMEM((extra, *tile), jnp.bfloat16),
                pltpu.SemaphoreType.DMA((extra,)),
            ]
            + ([] if last else [pltpu.SemaphoreType.DMA((1,))]),
            input_output_aliases={len(operands) - 1: 2} if held_store else {},
            compiler_params=pltpu.CompilerParams(vmem_limit_bytes=GRANT),
            cost_estimate=pl.CostEstimate(
                flops=4 << 20, bytes_accessed=1 << 18, transcendentals=0
            ),
            name=f"solve_{level}",
        )(*operands)

    def collect(base, befores, pieces):
        return call(
            functools.partial(collect_rows, rows, owners, base),
            "collect_rows",
            (jax.ShapeDtypeStruct((rows, *block), jnp.bfloat16),) * MEMBERS,
            (vmem(),) * MEMBERS,
            [smem()] + [vmem()] * (len(befores) + len(pieces)),
            [],
            (levels, *befores, *pieces),
            1 << 10,
            1 << 18,
        )

    store = None
    for level in range(1, LEVELS):
        held, totals, ready, info = prepare(level - 1, store, held)
        if level == LEVELS - 1:
            early = collect(0, (), pieces)
        piece, *more = solve(level, arriving, store, totals, ready, info)
        if more:
            spread, store = more
            pieces.append(piece)
            arriving = exchanged(spread)

    mine, theirs = collect(LEVELS - 1, early, (piece,))
    theirs = swapped(theirs)
    both = jnp.concatenate([mine, theirs], 1)
    crossed = jnp.concatenate([theirs, mine], 1)
    return jnp.swapaxes(jnp.where(core == 0, both, crossed), 1, 2)[:, None]


def solution(mesh):
    finer = Mesh(mesh.devices.reshape(4, 4, 4, 2), ROWS)
    return jax.shard_map(
        local,
        mesh=finer,
        in_specs=(
            P(None, ROWS, None, None),
            P(None, ROWS, None, None, None),
            P(None, ROWS, None, None),
            P(None, ROWS, None),
            P(None, ROWS),
            P(),
        ),
        out_specs=P(None, ROWS, None, None),
        check_vma=False,
    )
```

time: 660 us -> 371 us (0.56)
  waiting for transfers between devices: 266 us -> 154 us
  Pallas kernels: 0 us -> 108 us
  blocking collectives: 102 us -> 0 us
  matrix products: 91 us -> 0 us
  local copies, waits for them, and re-layouts: 66.8 us -> 4.34 us
  loops' own time: 26.4 us -> 0 us
  other arithmetic: 25.9 us -> 2.13 us
  starting transfers between devices: 77.1 us -> 98.6 us
    all_to_all x15, waiting for transfers between devices: 266 us -> 151 us  [exchanged(): lax.all_to_all(spread, CHIPS, 0, 0, tiled=True).reshape(owners, *block)]
    pallas_call x0 -> x34, Pallas kernels: none -> 108 us  [the longest x19 68.1 us: call(): pl.pallas_call(kernel, out_shape=out_shape, in_specs=in_specs, out_specs=...]
    all_to_all x15 -> x0, blocking collectives: 102 us -> none  [copy_for_each(): lax.all_to_all(jnp.broadcast_to(value[None], (length, *value.shape)), axi...]
    dot_general x31 -> x0, matrix products: 91 us -> none  [the longest x15 66.8 us: absorb(): jnp.einsum('skab,skbr->sar', tiles_local, fetched, preferred_element_type...]
    gather x17 -> x0, local copies, waits for them, and re-layouts: 33.6 us -> none  [the longest x15 32.5 us: select_blocks(): fetched = received[col_owner]]
    broadcast_in_dim x30 -> x0, local copies, waits for them, and re-layouts: 26.7 us -> none  [copy_for_each(): jnp.broadcast_to(value[None], (length, *value.shape))]
    another operation x1 -> x0, loops' own time: 26.4 us -> none  [local(): held, solution = lax.fori_loop(0, LEVELS - 1, advance, (store, solution))]
    ppermute x0 -> x6, starting transfers between devices: none -> 17.1 us  [swapped(): return lax.ppermute(value, CORE, SWAP)]
  transfers between devices with their start and end apart: 15 -> 21, of which waited for: 15 -> 18; matrix products, arithmetic and copies ran while one was open for 1% -> 1% of each run, Pallas kernels for 0% -> 18%
where the time goes in v3:
time: 371 us; the launch traced here: 367 us
  waiting for transfers between devices  154 us (42%)
  Pallas kernels  108 us (29%)
  starting transfers between devices  98.6 us (27%)
  local copies, waits for them, and re-layouts  4.34 us (1%)
    all_to_all x15, waiting for transfers between devices, exchanged(): lax.all_to_all(spread, CHIPS, 0, 0, tiled=True).reshape(owners, *block)  151 us
    all_to_all x15, starting transfers between devices, exchanged(): lax.all_to_all(spread, CHIPS, 0, 0, tiled=True).reshape(owners, *block)  81.5 us
    pallas_call x19, Pallas kernels, call(): pl.pallas_call(kernel, out_shape=out_shape, in_specs=in_specs, out_specs=...  68.1 us
    pallas_call x15, Pallas kernels, solve(): pl.pallas_call(functools.partial(solve_level, level, width_k, owners), ou...  39.6 us
    ppermute x6, starting transfers between devices, swapped(): return lax.ppermute(value, CORE, SWAP)  17.1 us
  transfers between devices with their start and end apart: 21, of which 18 were waited for; matrix products, arithmetic and copies ran while one was open for 1% of the time, Pallas kernels for 18%

profile of v3, /device:TPU:1, one launch (start us, length us, event | category | flops | bytes accessed | tf_op | source)
XLA Modules:
  0.0 367.2 jit_solution(5054048445895761263)
XLA Ops:
  7.9 11.2 %all-to-all-start = ((bf16[64,2,32,128]{3,2,1,0:T(8,128)(2,1)}), bf16[64,2,32,128]{3,2,1,0:T(8,128)(2,1)S(1)}, u32[]{:S(2)}, u32[]{:S(2)}) async-start(bf16[64,2,32,128]{3,2,1,0:T(8,128)(2,1)} %get-tuple-element.126), calls=%async_computation | async-start | bytes 2097152 | tf_op jit(solution)/shard_map/all_to_all | solution.py:352
  23.0 6.7 %list_edges.1 = (s32[256]{0:T(256)S(1)}, s32[65]{0:T(128)S(1)}) custom-call(s32[256]{0:T(256)S(1)} %reshape.60.columns, s32[16]{0:T(128)S(1)} %pad_add_fusion.1.counts, s32[1024]{0:T(1024)S(1)} %bitcast.67), custom_call_target="tpu_custom_call" | custom-call | flops 8388608 | bytes 1048576 | tf_op jit(solution)/shard_map/list_edges/pallas_call | solution.py:335
  33.1 4.2 %all-to-all-done = bf16[64,2,32,128]{3,2,1,0:T(8,128)(2,1)S(1)} async-done(((bf16[64,2,32,128]{3,2,1,0:T(8,128)(2,1)}), bf16[64,2,32,128]{3,2,1,0:T(8,128)(2,1)S(1)}, u32[]{:S(2)}, u32[]{:S(2)}) %all-to-all-start) | async-done | bytes 1048608 | tf_op jit(solution)/shard_map/all_to_all | solution.py:352
  37.3 2.7 solve_1.1
  40.0 7.5 %all-to-all-start.1 = ((bf16[64,2,32,128]{3,2,1,0:T(8,128)(2,1)}), bf16[64,2,32,128]{3,2,1,0:T(8,128)(2,1)S(1)}, u32[]{:S(2)}, u32[]{:S(2)}) async-start(bf16[64,2,32,128]{3,2,1,0:T(8,128)(2,1)} %get-tuple-element.133), calls=%async_computation.1 | async-start | bytes 2097152 | tf_op jit(solution)/shard_map/all_to_all | solution.py:352
  47.5 6.4 %prepare_1.1 = (f32[16,32,128]{2,1,0:T(8,128)S(1)}, f32[2,32,128]{2,1,0:T(8,128)S(1)}, bf16[2,7,128,128]{3,2,1,0:T(8,128)(2,1)S(1)}, s32[2]{0:T(128)S(1)}) custom-call(s32[1024]{0:T(1024)S(1)} %bitcast.69, s32[256]{0:T(256)S(1)} %get-tuple-element.120.edges, s32[65]{0:T(128)S(1)} %get-tuple-element.121.starts, ...), custom_call_target="tpu_custom_call" | custom-call | flops 33554432 | bytes 1048576 | tf_op jit(solution)/shard_map/prepare_1/pallas_call | solution.py:335
  54.0 10.9 %all-to-all-done.1 = bf16[64,2,32,128]{3,2,1,0:T(8,128)(2,1)S(1)} async-done(((bf16[64,2,32,128]{3,2,1,0:T(8,128)(2,1)}), bf16[64,2,32,128]{3,2,1,0:T(8,128)(2,1)S(1)}, u32[]{:S(2)}, u32[]{:S(2)}) %all-to-all-start.1) | async-done | bytes 1048608 | tf_op jit(solution)/shard_map/all_to_all | solution.py:352
  67.6 6.4 %all-to-all-start.2 = ((bf16[64,2,32,128]{3,2,1,0:T(8,128)(2,1)}), bf16[64,2,32,128]{3,2,1,0:T(8,128)(2,1)S(1)}, u32[]{:S(2)}, u32[]{:S(2)}) async-start(bf16[64,2,32,128]{3,2,1,0:T(8,128)(2,1)} %get-tuple-element.140), calls=%async_computation.2 | async-start | bytes 2097152 | tf_op jit(solution)/shard_map/all_to_all | solution.py:352
  74.0 5.5 %prepare_2.1 = (f32[16,32,128]{2,1,0:T(8,128)S(1)}, f32[2,32,128]{2,1,0:T(8,128)S(1)}, bf16[2,7,128,128]{3,2,1,0:T(8,128)(2,1)S(1)}, s32[2]{0:T(128)S(1)}) custom-call(s32[1024]{0:T(1024)S(1)} %bitcast.70, s32[256]{0:T(256)S(1)} %get-tuple-element.120.edges, s32[65]{0:T(128)S(1)} %get-tuple-element.121.starts, ...), custom_call_target="tpu_custom_call" | custom-call | flops 33554432 | bytes 1048576 | tf_op jit(solution)/shard_map/prepare_2/pallas_call | solution.py:335
  79.5 11.1 %all-to-all-done.2 = bf16[64,2,32,128]{3,2,1,0:T(8,128)(2,1)S(1)} async-done(((bf16[64,2,32,128]{3,2,1,0:T(8,128)(2,1)}), bf16[64,2,32,128]{3,2,1,0:T(8,128)(2,1)S(1)}, u32[]{:S(2)}, u32[]{:S(2)}) %all-to-all-start.2) | async-done | bytes 1048608 | tf_op jit(solution)/shard_map/all_to_all | solution.py:352
  90.6 2.8 solve_3.1
  93.4 4.9 %all-to-all-start.3 = ((bf16[64,2,32,128]{3,2,1,0:T(8,128)(2,1)}), bf16[64,2,32,128]{3,2,1,0:T(8,128)(2,1)S(1)}, u32[]{:S(2)}, u32[]{:S(2)}) async-start(bf16[64,2,32,128]{3,2,1,0:T(8,128)(2,1)} %get-tuple-element.147), calls=%async_computation.3 | async-start | bytes 2097152 | tf_op jit(solution)/shard_map/all_to_all | solution.py:352
  98.3 3.5 prepare_3.1
  101.8 12.4 %all-to-all-done.3 = bf16[64,2,32,128]{3,2,1,0:T(8,128)(2,1)S(1)} async-done(((bf16[64,2,32,128]{3,2,1,0:T(8,128)(2,1)}), bf16[64,2,32,128]{3,2,1,0:T(8,128)(2,1)S(1)}, u32[]{:S(2)}, u32[]{:S(2)}) %all-to-all-start.3) | async-done | bytes 1048608 | tf_op jit(solution)/shard_map/all_to_all | solution.py:352
  117.0 4.7 %all-to-all-start.4 = ((bf16[64,2,32,128]{3,2,1,0:T(8,128)(2,1)}), bf16[64,2,32,128]{3,2,1,0:T(8,128)(2,1)S(1)}, u32[]{:S(2)}, u32[]{:S(2)}) async-start(bf16[64,2,32,128]{3,2,1,0:T(8,128)(2,1)} %get-tuple-element.154), calls=%async_computation.4 | async-start | bytes 2097152 | tf_op jit(solution)/shard_map/all_to_all | solution.py:352
  121.6 5.1 %prepare_4.1 = (f32[16,32,128]{2,1,0:T(8,128)S(1)}, f32[2,32,128]{2,1,0:T(8,128)S(1)}, bf16[2,7,128,128]{3,2,1,0:T(8,128)(2,1)S(1)}, s32[2]{0:T(128)S(1)}) custom-call(s32[1024]{0:T(1024)S(1)} %bitcast.72, s32[256]{0:T(256)S(1)} %get-tuple-element.120.edges, s32[65]{0:T(128)S(1)} %get-tuple-element.121.starts, ...), custom_call_target="tpu_custom_call" | custom-call | flops 33554432 | bytes 1048576 | tf_op jit(solution)/shard_map/prepare_4/pallas_call | solution.py:335
  126.7 10.2 %all-to-all-done.4 = bf16[64,2,32,128]{3,2,1,0:T(8,128)(2,1)S(1)} async-done(((bf16[64,2,32,128]{3,2,1,0:T(8,128)(2,1)}), bf16[64,2,32,128]{3,2,1,0:T(8,128)(2,1)S(1)}, u32[]{:S(2)}, u32[]{:S(2)}) %all-to-all-start.4) | async-done | bytes 1048608 | tf_op jit(solution)/shard_map/all_to_all | solution.py:352
  139.7 4.7 %all-to-all-start.5 = ((bf16[64,2,32,128]{3,2,1,0:T(8,128)(2,1)}), bf16[64,2,32,128]{3,2,1,0:T(8,128)(2,1)S(1)}, u32[]{:S(2)}, u32[]{:S(2)}) async-start(bf16[64,2,32,128]{3,2,1,0:T(8,128)(2,1)} %get-tuple-element.161), calls=%async_computation.5 | async-start | bytes 2097152 | tf_op jit(solution)/shard_map/all_to_all | solution.py:352
  144.4 5.5 %prepare_5.1 = (f32[16,32,128]{2,1,0:T(8,128)S(1)}, f32[2,32,128]{2,1,0:T(8,128)S(1)}, bf16[2,7,128,128]{3,2,1,0:T(8,128)(2,1)S(1)}, s32[2]{0:T(128)S(1)}) custom-call(s32[1024]{0:T(1024)S(1)} %bitcast.73, s32[256]{0:T(256)S(1)} %get-tuple-element.120.edges, s32[65]{0:T(128)S(1)} %get-tuple-element.121.starts, ...), custom_call_target="tpu_custom_call" | custom-call | flops 33554432 | bytes 1048576 | tf_op jit(solution)/shard_map/prepare_5/pallas_call | solution.py:335
  149.9 9.2 %all-to-all-done.5 = bf16[64,2,32,128]{3,2,1,0:T(8,128)(2,1)S(1)} async-done(((bf16[64,2,32,128]{3,2,1,0:T(8,128)(2,1)}), bf16[64,2,32,128]{3,2,1,0:T(8,128)(2,1)S(1)}, u32[]{:S(2)}, u32[]{:S(2)}) %all-to-all-start.5) | async-done | bytes 1048608 | tf_op jit(solution)/shard_map/all_to_all | solution.py:352
  161.9 4.7 %all-to-all-start.6 = ((bf16[64,2,32,128]{3,2,1,0:T(8,128)(2,1)}), bf16[64,2,32,128]{3,2,1,0:T(8,128)(2,1)S(1)}, u32[]{:S(2)}, u32[]{:S(2)}) async-start(bf16[64,2,32,128]{3,2,1,0:T(8,128)(2,1)} %get-tuple-element.168), calls=%async_computation.6 | async-start | bytes 2097152 | tf_op jit(solution)/shard_map/all_to_all | solution.py:352
  166.5 4.5 %prepare_6.1 = (f32[16,32,128]{2,1,0:T(8,128)S(1)}, f32[2,32,128]{2,1,0:T(8,128)S(1)}, bf16[2,7,128,128]{3,2,1,0:T(8,128)(2,1)S(1)}, s32[2]{0:T(128)S(1)}) custom-call(s32[1024]{0:T(1024)S(1)} %bitcast.74, s32[256]{0:T(256)S(1)} %get-tuple-element.120.edges, s32[65]{0:T(128)S(1)} %get-tuple-element.121.starts, ...), custom_call_target="tpu_custom_call" | custom-call | flops 33554432 | bytes 1048576 | tf_op jit(solution)/shard_map/prepare_6/pallas_call | solution.py:335
  171.0 9.7 %all-to-all-done.6 = bf16[64,2,32,128]{3,2,1,0:T(8,128)(2,1)S(1)} async-done(((bf16[64,2,32,128]{3,2,1,0:T(8,128)(2,1)}), bf16[64,2,32,128]{3,2,1,0:T(8,128)(2,1)S(1)}, u32[]{:S(2)}, u32[]{:S(2)}) %all-to-all-start.6) | async-done | bytes 1048608 | tf_op jit(solution)/shard_map/all_to_all | solution.py:352
  180.7 2.8 solve_7.1
  183.4 4.7 %all-to-all-start.7 = ((bf16[64,2,32,128]{3,2,1,0:T(8,128)(2,1)}), bf16[64,2,32,128]{3,2,1,0:T(8,128)(2,1)S(1)}, u32[]{:S(2)}, u32[]{:S(2)}) async-start(bf16[64,2,32,128]{3,2,1,0:T(8,128)(2,1)} %get-tuple-element.175), calls=%async_computation.7 | async-start | bytes 2097152 | tf_op jit(solution)/shard_map/all_to_all | solution.py:352
  188.1 3.8 %prepare_7.1 = (f32[16,32,128]{2,1,0:T(8,128)S(1)}, f32[2,32,128]{2,1,0:T(8,128)S(1)}, bf16[2,7,128,128]{3,2,1,0:T(8,128)(2,1)S(1)}, s32[2]{0:T(128)S(1)}) custom-call(s32[1024]{0:T(1024)S(1)} %bitcast.75, s32[256]{0:T(256)S(1)} %get-tuple-element.120.edges, s32[65]{0:T(128)S(1)} %get-tuple-element.121.starts, ...), custom_call_target="tpu_custom_call" | custom-call | flops 33554432 | bytes 1048576 | tf_op jit(solution)/shard_map/prepare_7/pallas_call | solution.py:335
  192.0 10.0 %all-to-all-done.7 = bf16[64,2,32,128]{3,2,1,0:T(8,128)(2,1)S(1)} async-done(((bf16[64,2,32,128]{3,2,1,0:T(8,128)(2,1)}), bf16[64,2,32,128]{3,2,1,0:T(8,128)(2,1)S(1)}, u32[]{:S(2)}, u32[]{:S(2)}) %all-to-all-start.7) | async-done | bytes 1048608 | tf_op jit(solution)/shard_map/all_to_all | solution.py:352
  202.0 2.8 solve_8.1
  204.8 4.7 %all-to-all-start.8 = ((bf16[64,2,32,128]{3,2,1,0:T(8,128)(2,1)}), bf16[64,2,32,128]{3,2,1,0:T(8,128)(2,1)S(1)}, u32[]{:S(2)}, u32[]{:S(2)}) async-start(bf16[64,2,32,128]{3,2,1,0:T(8,128)(2,1)} %get-tuple-element.182), calls=%async_computation.8 | async-start | bytes 2097152 | tf_op jit(solution)/shard_map/all_to_all | solution.py:352
  209.5 4.5 %prepare_8.1 = (f32[16,32,128]{2,1,0:T(8,128)S(1)}, f32[2,32,128]{2,1,0:T(8,128)S(1)}, bf16[2,7,128,128]{3,2,1,0:T(8,128)(2,1)S(1)}, s32[2]{0:T(128)S(1)}) custom-call(s32[1024]{0:T(1024)S(1)} %bitcast.76, s32[256]{0:T(256)S(1)} %get-tuple-element.120.edges, s32[65]{0:T(128)S(1)} %get-tuple-element.121.starts, ...), custom_call_target="tpu_custom_call" | custom-call | flops 33554432 | bytes 1048576 | tf_op jit(solution)/shard_map/prepare_8/pallas_call | solution.py:335
  213.9 9.3 %all-to-all-done.8 = bf16[64,2,32,128]{3,2,1,0:T(8,128)(2,1)S(1)} async-done(((bf16[64,2,32,128]{3,2,1,0:T(8,128)(2,1)}), bf16[64,2,32,128]{3,2,1,0:T(8,128)(2,1)S(1)}, u32[]{:S(2)}, u32[]{:S(2)}) %all-to-all-start.8) | async-done | bytes 1048608 | tf_op jit(solution)/shard_map/all_to_all | solution.py:352
  226.0 4.7 %all-to-all-start.9 = ((bf16[64,2,32,128]{3,2,1,0:T(8,128)(2,1)}), bf16[64,2,32,128]{3,2,1,0:T(8,128)(2,1)S(1)}, u32[]{:S(2)}, u32[]{:S(2)}) async-start(bf16[64,2,32,128]{3,2,1,0:T(8,128)(2,1)} %get-tuple-element.189), calls=%async_computation.9 | async-start | bytes 2097152 | tf_op jit(solution)/shard_map/all_to_all | solution.py:352
  230.6 3.1 prepare_9.1
  233.7 10.6 %all-to-all-done.9 = bf16[64,2,32,128]{3,2,1,0:T(8,128)(2,1)S(1)} async-done(((bf16[64,2,32,128]{3,2,1,0:T(8,128)(2,1)}), bf16[64,2,32,128]{3,2,1,0:T(8,128)(2,1)S(1)}, u32[]{:S(2)}, u32[]{:S(2)}) %all-to-all-start.9) | async-done | bytes 1048608 | tf_op jit(solution)/shard_map/all_to_all | solution.py:352
  247.0 4.7 %all-to-all-start.10 = ((bf16[64,2,32,128]{3,2,1,0:T(8,128)(2,1)}), bf16[64,2,32,128]{3,2,1,0:T(8,128)(2,1)S(1)}, u32[]{:S(2)}, u32[]{:S(2)}) async-start(bf16[64,2,32,128]{3,2,1,0:T(8,128)(2,1)} %get-tuple-element.196), calls=%async_computation.10 | async-start | bytes 2097152 | tf_op jit(solution)/shard_map/all_to_all | solution.py:352
  251.7 2.9 prepare_10.1
  254.6 10.6 %all-to-all-done.10 = bf16[64,2,32,128]{3,2,1,0:T(8,128)(2,1)S(1)} async-done(((bf16[64,2,32,128]{3,2,1,0:T(8,128)(2,1)}), bf16[64,2,32,128]{3,2,1,0:T(8,128)(2,1)S(1)}, u32[]{:S(2)}, u32[]{:S(2)}) %all-to-all-start.10) | async-done | bytes 1048608 | tf_op jit(solution)/shard_map/all_to_all | solution.py:352
  268.0 4.7 %all-to-all-start.11 = ((bf16[64,2,32,128]{3,2,1,0:T(8,128)(2,1)}), bf16[64,2,32,128]{3,2,1,0:T(8,128)(2,1)S(1)}, u32[]{:S(2)}, u32[]{:S(2)}) async-start(bf16[64,2,32,128]{3,2,1,0:T(8,128)(2,1)} %get-tuple-element.203), calls=%async_computation.11 | async-start | bytes 2097152 | tf_op jit(solution)/shard_map/all_to_all | solution.py:352
  275.0 11.2 %all-to-all-done.11 = bf16[64,2,32,128]{3,2,1,0:T(8,128)(2,1)S(1)} async-done(((bf16[64,2,32,128]{3,2,1,0:T(8,128)(2,1)}), bf16[64,2,32,128]{3,2,1,0:T(8,128)(2,1)S(1)}, u32[]{:S(2)}, u32[]{:S(2)}) %all-to-all-start.11) | async-done | bytes 1048608 | tf_op jit(solution)/shard_map/all_to_all | solution.py:352
  286.2 2.8 solve_12.1
  289.0 4.9 %all-to-all-start.12 = ((bf16[64,2,32,128]{3,2,1,0:T(8,128)(2,1)}), bf16[64,2,32,128]{3,2,1,0:T(8,128)(2,1)S(1)}, u32[]{:S(2)}, u32[]{:S(2)}) async-start(bf16[64,2,32,128]{3,2,1,0:T(8,128)(2,1)} %get-tuple-element.210), calls=%async_computation.12 | async-start | bytes 2097152 | tf_op jit(solution)/shard_map/all_to_all | solution.py:352
  296.4 11.1 %all-to-all-done.12 = bf16[64,2,32,128]{3,2,1,0:T(8,128)(2,1)S(1)} async-done(((bf16[64,2,32,128]{3,2,1,0:T(8,128)(2,1)}), bf16[64,2,32,128]{3,2,1,0:T(8,128)(2,1)S(1)}, u32[]{:S(2)}, u32[]{:S(2)}) %all-to-all-start.12) | async-done | bytes 1048608 | tf_op jit(solution)/shard_map/all_to_all | solution.py:352
  310.2 4.7 %all-to-all-start.13 = ((bf16[64,2,32,128]{3,2,1,0:T(8,128)(2,1)}), bf16[64,2,32,128]{3,2,1,0:T(8,128)(2,1)S(1)}, u32[]{:S(2)}, u32[]{:S(2)}) async-start(bf16[64,2,32,128]{3,2,1,0:T(8,128)(2,1)} %get-tuple-element.217), calls=%async_computation.13 | async-start | bytes 2097152 | tf_op jit(solution)/shard_map/all_to_all | solution.py:352
  314.8 2.9 prepare_13.1
  317.8 10.6 %all-to-all-done.13 = bf16[64,2,32,128]{3,2,1,0:T(8,128)(2,1)S(1)} async-done(((bf16[64,2,32,128]{3,2,1,0:T(8,128)(2,1)}), bf16[64,2,32,128]{3,2,1,0:T(8,128)(2,1)S(1)}, u32[]{:S(2)}, u32[]{:S(2)}) %all-to-all-start.13) | async-done | bytes 1048608 | tf_op jit(solution)/shard_map/all_to_all | solution.py:352
  331.1 4.7 %all-to-all-start.14 = ((bf16[64,2,32,128]{3,2,1,0:T(8,128)(2,1)}), bf16[64,2,32,128]{3,2,1,0:T(8,128)(2,1)S(1)}, u32[]{:S(2)}, u32[]{:S(2)}) async-start(bf16[64,2,32,128]{3,2,1,0:T(8,128)(2,1)} %get-tuple-element.226), calls=%async_computation.14 | async-start | bytes 2097152 | tf_op jit(solution)/shard_map/all_to_all | solution.py:352
  339.4 9.9 %all-to-all-done.14 = bf16[64,2,32,128]{3,2,1,0:T(8,128)(2,1)S(1)} async-done(((bf16[64,2,32,128]{3,2,1,0:T(8,128)(2,1)}), bf16[64,2,32,128]{3,2,1,0:T(8,128)(2,1)S(1)}, u32[]{:S(2)}, u32[]{:S(2)}) %all-to-all-start.14) | async-done | bytes 1048608 | tf_op jit(solution)/shard_map/all_to_all | solution.py:352
  351.1 14.5 %collective-permute-start.5 = (bf16[8,32,128]{2,1,0:T(8,128)(2,1)S(1)}, bf16[8,32,128]{2,1,0:T(8,128)(2,1)S(1)}, u32[]{:S(2)}, u32[]{:S(2)}) collective-permute-start(bf16[8,32,128]{2,1,0:T(8,128)(2,1)S(1)} %get-tuple-element.228), channel_id=1, source_target_pairs={{0,1},{1,0},{2,3},{3,2},{4,5},{5,4},{6,7},{7,6},{8,9},{9,8},{10,11... | collective-permute-start | bytes 196616 | tf_op jit(solution)/shard_map/ppermute | solution.py:325
  (46 shorter events, 51.5 us)
Async XLA Ops:
  0.0 47.5 %copy-start.2 = (bf16[8,1,128,128]{3,2,1,0:T(8,128)(2,1)S(1)}, bf16[8,1,128,128]{3,2,1,0:T(8,128)(2,1)}, u32[]{:S(2)}) copy-start(bf16[8,1,128,128]{3,2,1,0:T(8,128)(2,1)} %param.8) | copy-start | bytes 786436
  0.0 47.5 %copy-start.5 = (s32[8,128]{1,0:T(8,128)S(1)}, s32[8,128]{1,0:T(8,128)}, u32[]{:S(2)}) copy-start(s32[8,128]{1,0:T(8,128)} %param.11) | copy-start | bytes 12292
  0.0 3.8 %collective-permute-start.1 = (bf16[8,128,128]{2,1,0:T(8,128)(2,1)}, bf16[8,128,128]{2,1,0:T(8,128)(2,1)S(1)}, u32[]{:S(2)}, u32[]{:S(2)}) collective-permute-start(bf16[8,128,128]{2,1,0:T(8,128)(2,1)} %bitcast.34), channel_id=1, source_target_pairs={{0,1},{1,0},{2,3},{3,2},{4,5},{5,4},{6,7},{7,6},{8,9},{9,8},{10,11... | collective-permute-start | bytes 786440 | tf_op jit(solution)/shard_map/ppermute | solution.py:325
  2.4 1.4 collective-permute-start
  3.8 1.0 copy-start
  4.8 0.7 copy-start.3
  7.7 22.0 %collective-permute-start.4 = (bf16[8,16,128,128]{3,2,1,0:T(8,128)(2,1)}, bf16[8,16,128,128]{3,2,1,0:T(8,128)(2,1)}, u32[]{:S(2)}, u32[]{:S(2)}) collective-permute-start(bf16[8,16,128,128]{3,2,1,0:T(8,128)(2,1)} %bitcast.85), channel_id=1, source_target_pairs={{0,1},{1,0},{2,3},{3,2},{4,5},{5,4},{6,7},{7,6},{8,9},{9,8},{10,11... | collective-permute-start | bytes 12582920 | tf_op jit(solution)/shard_map/ppermute | solution.py:325
  7.9 29.3 %all-to-all-start = ((bf16[64,2,32,128]{3,2,1,0:T(8,128)(2,1)}), bf16[64,2,32,128]{3,2,1,0:T(8,128)(2,1)S(1)}, u32[]{:S(2)}, u32[]{:S(2)}) async-start(bf16[64,2,32,128]{3,2,1,0:T(8,128)(2,1)} %get-tuple-element.126), calls=%async_computation | async-start | bytes 2097152 | tf_op jit(solution)/shard_map/all_to_all | solution.py:352
  19.2 1.7 collective-permute-start.3
  19.9 1.7 collective-permute-start.2
  22.3 0.7 copy-start.4
  29.7 1.0 copy-start.1
  40.0 24.8 %all-to-all-start.1 = ((bf16[64,2,32,128]{3,2,1,0:T(8,128)(2,1)}), bf16[64,2,32,128]{3,2,1,0:T(8,128)(2,1)S(1)}, u32[]{:S(2)}, u32[]{:S(2)}) async-start(bf16[64,2,32,128]{3,2,1,0:T(8,128)(2,1)} %get-tuple-element.133), calls=%async_computation.1 | async-start | bytes 2097152 | tf_op jit(solution)/shard_map/all_to_all | solution.py:352
  67.6 23.0 %all-to-all-start.2 = ((bf16[64,2,32,128]{3,2,1,0:T(8,128)(2,1)}), bf16[64,2,32,128]{3,2,1,0:T(8,128)(2,1)S(1)}, u32[]{:S(2)}, u32[]{:S(2)}) async-start(bf16[64,2,32,128]{3,2,1,0:T(8,128)(2,1)} %get-tuple-element.140), calls=%async_computation.2 | async-start | bytes 2097152 | tf_op jit(solution)/shard_map/all_to_all | solution.py:352
  93.4 20.9 %all-to-all-start.3 = ((bf16[64,2,32,128]{3,2,1,0:T(8,128)(2,1)}), bf16[64,2,32,128]{3,2,1,0:T(8,128)(2,1)S(1)}, u32[]{:S(2)}, u32[]{:S(2)}) async-start(bf16[64,2,32,128]{3,2,1,0:T(8,128)(2,1)} %get-tuple-element.147), calls=%async_computation.3 | async-start | bytes 2097152 | tf_op jit(solution)/shard_map/all_to_all | solution.py:352
  117.0 20.0 %all-to-all-start.4 = ((bf16[64,2,32,128]{3,2,1,0:T(8,128)(2,1)}), bf16[64,2,32,128]{3,2,1,0:T(8,128)(2,1)S(1)}, u32[]{:S(2)}, u32[]{:S(2)}) async-start(bf16[64,2,32,128]{3,2,1,0:T(8,128)(2,1)} %get-tuple-element.154), calls=%async_computation.4 | async-start | bytes 2097152 | tf_op jit(solution)/shard_map/all_to_all | solution.py:352
  139.7 19.4 %all-to-all-start.5 = ((bf16[64,2,32,128]{3,2,1,0:T(8,128)(2,1)}), bf16[64,2,32,128]{3,2,1,0:T(8,128)(2,1)S(1)}, u32[]{:S(2)}, u32[]{:S(2)}) async-start(bf16[64,2,32,128]{3,2,1,0:T(8,128)(2,1)} %get-tuple-element.161), calls=%async_computation.5 | async-start | bytes 2097152 | tf_op jit(solution)/shard_map/all_to_all | solution.py:352
  161.9 18.8 %all-to-all-start.6 = ((bf16[64,2,32,128]{3,2,1,0:T(8,128)(2,1)}), bf16[64,2,32,128]{3,2,1,0:T(8,128)(2,1)S(1)}, u32[]{:S(2)}, u32[]{:S(2)}) async-start(bf16[64,2,32,128]{3,2,1,0:T(8,128)(2,1)} %get-tuple-element.168), calls=%async_computation.6 | async-start | bytes 2097152 | tf_op jit(solution)/shard_map/all_to_all | solution.py:352
  183.4 18.5 %all-to-all-start.7 = ((bf16[64,2,32,128]{3,2,1,0:T(8,128)(2,1)}), bf16[64,2,32,128]{3,2,1,0:T(8,128)(2,1)S(1)}, u32[]{:S(2)}, u32[]{:S(2)}) async-start(bf16[64,2,32,128]{3,2,1,0:T(8,128)(2,1)} %get-tuple-element.175), calls=%async_computation.7 | async-start | bytes 2097152 | tf_op jit(solution)/shard_map/all_to_all | solution.py:352
  204.8 18.4 %all-to-all-start.8 = ((bf16[64,2,32,128]{3,2,1,0:T(8,128)(2,1)}), bf16[64,2,32,128]{3,2,1,0:T(8,128)(2,1)S(1)}, u32[]{:S(2)}, u32[]{:S(2)}) async-start(bf16[64,2,32,128]{3,2,1,0:T(8,128)(2,1)} %get-tuple-element.182), calls=%async_computation.8 | async-start | bytes 2097152 | tf_op jit(solution)/shard_map/all_to_all | solution.py:352
  226.0 18.3 %all-to-all-start.9 = ((bf16[64,2,32,128]{3,2,1,0:T(8,128)(2,1)}), bf16[64,2,32,128]{3,2,1,0:T(8,128)(2,1)S(1)}, u32[]{:S(2)}, u32[]{:S(2)}) async-start(bf16[64,2,32,128]{3,2,1,0:T(8,128)(2,1)} %get-tuple-element.189), calls=%async_computation.9 | async-start | bytes 2097152 | tf_op jit(solution)/shard_map/all_to_all | solution.py:352
  247.0 18.2 %all-to-all-start.10 = ((bf16[64,2,32,128]{3,2,1,0:T(8,128)(2,1)}), bf16[64,2,32,128]{3,2,1,0:T(8,128)(2,1)S(1)}, u32[]{:S(2)}, u32[]{:S(2)}) async-start(bf16[64,2,32,128]{3,2,1,0:T(8,128)(2,1)} %get-tuple-element.196), calls=%async_computation.10 | async-start | bytes 2097152 | tf_op jit(solution)/shard_map/all_to_all | solution.py:352
  268.0 18.2 %all-to-all-start.11 = ((bf16[64,2,32,128]{3,2,1,0:T(8,128)(2,1)}), bf16[64,2,32,128]{3,2,1,0:T(8,128)(2,1)S(1)}, u32[]{:S(2)}, u32[]{:S(2)}) async-start(bf16[64,2,32,128]{3,2,1,0:T(8,128)(2,1)} %get-tuple-element.203), calls=%async_computation.11 | async-start | bytes 2097152 | tf_op jit(solution)/shard_map/all_to_all | solution.py:352
  289.0 18.4 %all-to-all-start.12 = ((bf16[64,2,32,128]{3,2,1,0:T(8,128)(2,1)}), bf16[64,2,32,128]{3,2,1,0:T(8,128)(2,1)S(1)}, u32[]{:S(2)}, u32[]{:S(2)}) async-start(bf16[64,2,32,128]{3,2,1,0:T(8,128)(2,1)} %get-tuple-element.210), calls=%async_computation.12 | async-start | bytes 2097152 | tf_op jit(solution)/shard_map/all_to_all | solution.py:352
  310.2 18.2 %all-to-all-start.13 = ((bf16[64,2,32,128]{3,2,1,0:T(8,128)(2,1)}), bf16[64,2,32,128]{3,2,1,0:T(8,128)(2,1)S(1)}, u32[]{:S(2)}, u32[]{:S(2)}) async-start(bf16[64,2,32,128]{3,2,1,0:T(8,128)(2,1)} %get-tuple-element.217), calls=%async_computation.13 | async-start | bytes 2097152 | tf_op jit(solution)/shard_map/all_to_all | solution.py:352
  331.1 18.2 %all-to-all-start.14 = ((bf16[64,2,32,128]{3,2,1,0:T(8,128)(2,1)}), bf16[64,2,32,128]{3,2,1,0:T(8,128)(2,1)S(1)}, u32[]{:S(2)}, u32[]{:S(2)}) async-start(bf16[64,2,32,128]{3,2,1,0:T(8,128)(2,1)} %get-tuple-element.226), calls=%async_computation.14 | async-start | bytes 2097152 | tf_op jit(solution)/shard_map/all_to_all | solution.py:352
  351.1 15.4 %collective-permute-start.5 = (bf16[8,32,128]{2,1,0:T(8,128)(2,1)S(1)}, bf16[8,32,128]{2,1,0:T(8,128)(2,1)S(1)}, u32[]{:S(2)}, u32[]{:S(2)}) collective-permute-start(bf16[8,32,128]{2,1,0:T(8,128)(2,1)S(1)} %get-tuple-element.228), channel_id=1, source_target_pairs={{0,1},{1,0},{2,3},{3,2},{4,5},{5,4},{6,7},{7,6},{8,9},{9,8},{10,11... | collective-permute-start | bytes 196616 | tf_op jit(solution)/shard_map/ppermute | solution.py:325

commit v4 on v3

--- a/solution.py
+++ b/solution.py
@@ -10,14 +10,14 @@
 
 LEVELS = 16
 ROWS = ("rows_0", "rows_1", "rows_2", "rows_3")
-CHIPS = ("rows_0", "rows_1", "rows_2")
+CHIPS = ("rows_2", "rows_0", "rows_1")
 CORE = "rows_3"
 SWAP = ((0, 1), (1, 0))
 MEMBERS = 2
 KEYS = LEVELS * 2 * MEMBERS
 RING = 8
 GROUP = 3
-READY = 6
+READY = 3
 GRANT = 50 << 20
 
 
@@ -61,7 +61,7 @@
     return pick
 
 
-def list_edges(owners, columns, counts, levels, edges, starts, fill):
+def list_edges(owners, line, columns, counts, levels, edges, starts, fill):
     rows = counts.shape[0] // MEMBERS
     width_k = columns.shape[0] // counts.shape[0]
 
@@ -105,7 +105,9 @@
 
     def place(slot, col, key):
         at = fill[key]
-        edges[at] = slot * owners + lax.rem(col, owners)
+        chip = lax.rem(col, owners) // MEMBERS
+        turned = lax.rem(chip, line) * (owners // MEMBERS // line) + chip // line
+        edges[at] = slot * owners + turned * MEMBERS + lax.rem(col, MEMBERS)
         fill[key] = at + 1
 
     over_slots(place)
@@ -139,9 +141,9 @@
 
 def prepare_level(level, rows, width_k, owners, levels, edges, starts, held_in, *refs):
     if level:
-        store, *refs = refs
+        received, *refs = refs
     tiles, inverses = refs[:MEMBERS], refs[MEMBERS : 2 * MEMBERS]
-    held, totals, ready, info, buf, blocks, sems, block_sems, ready_sems = refs[2 * MEMBERS :]
+    held, totals, ready, info, buf, sems, ready_sems = refs[2 * MEMBERS :]
     slots = 1 + READY
     picks = [find_row(levels, owners, member, rows, level + 1) for member in range(MEMBERS)]
 
@@ -157,11 +159,6 @@
     def late_copy(member, first, i):
         at = lax.rem(i, RING)
         return pltpu.make_async_copy(tile_of(member, first + i), buf.at[at], sems.at[at])
-
-    def block_copy(first, i):
-        at = lax.rem(i, RING)
-        place = lax.rem(edges[first + i], owners)
-        return pltpu.make_async_copy(store.at[level - 1, place], blocks.at[at], block_sems.at[at])
 
     late = []
     if level:
@@ -172,7 +169,6 @@
 
         def begin(i, unused, first=first):
             late_copy(0, first, i).start()
-            block_copy(first, i).start()
             return unused
 
         lax.fori_loop(0, jnp.minimum(many, RING), begin, 0)
@@ -199,23 +195,20 @@
 
                 def begin(i, unused, member=member, first=first):
                     late_copy(member, first, i).start()
-                    block_copy(first, i).start()
                     return unused
 
                 lax.fori_loop(0, jnp.minimum(many, RING), begin, 0)
 
             def absorb(i, unused, member=member, first=first, many=many):
                 late_copy(member, first, i).wait()
-                block_copy(first, i).wait()
-                row = edges[first + i] // (owners * width_k)
-                at = lax.rem(i, RING)
-                given = times_transposed(blocks[at], buf[at])
+                code = edges[first + i]
+                row = code // (owners * width_k)
+                given = times_transposed(received[lax.rem(code, owners)], buf[lax.rem(i, RING)])
                 held[row] = held[row] - given
 
                 @pl.when(i + RING < many)
                 def _():
                     late_copy(member, first, i + RING).start()
-                    block_copy(first, i + RING).start()
 
                 return unused
 
@@ -233,14 +226,7 @@
 
 
 def solve_level(level, width_k, owners, edges, starts, info, totals, ready, received, *refs):
-    tiles, refs = refs[:MEMBERS], refs[MEMBERS:]
-    last = level == LEVELS - 1
-    if last:
-        piece, buf, sems = refs
-    else:
-        piece, spread, store, buf, sems, keep_sem = refs[1 if level > 1 else 0 :]
-        keep = pltpu.make_async_copy(received, store.at[level - 1], keep_sem.at[0])
-        keep.start()
+    tiles, (piece, *spread, buf, sems) = refs[:MEMBERS], refs[MEMBERS:]
     extra = width_k - READY
 
     def extra_copy(member, i):
@@ -291,9 +277,8 @@
             solved = times_transposed(total.astype(jnp.bfloat16), ready[member, 0])
             piece[at] = solved.astype(jnp.bfloat16)
 
-    if not last:
-        spread_piece(piece, spread)
-        keep.wait()
+    if spread:
+        spread_piece(piece, *spread)
 
 
 def collect_rows(rows, owners, base, levels, *refs):
@@ -345,8 +330,6 @@
 
     piece_shape = jax.ShapeDtypeStruct((MEMBERS, *block), jnp.bfloat16)
     spread_shape = jax.ShapeDtypeStruct((chips, MEMBERS, *block), jnp.bfloat16)
-
-    store_shape = jax.ShapeDtypeStruct((LEVELS - 2, owners, *block), jnp.bfloat16)
 
     def exchanged(spread):
         return lax.all_to_all(spread, CHIPS, 0, 0, tiled=True).reshape(owners, *block)
@@ -372,7 +355,7 @@
     columns = jnp.concatenate([columns_own, swapped(columns_own)]).reshape(-1)
     counts = jnp.concatenate([counts_own, swapped(counts_own)])
     edges, starts = call(
-        functools.partial(list_edges, owners),
+        functools.partial(list_edges, owners, lax.axis_size(CHIPS[0])),
         "list_edges",
         (
             jax.ShapeDtypeStruct((columns.size,), jnp.int32),
@@ -386,7 +369,7 @@
         1 << 20,
     )
 
-    def prepare(level, store, held):
+    def prepare(level, received, held):
         return call(
             functools.partial(prepare_level, level, rows, width_k, owners),
             f"prepare_{level}",
@@ -397,41 +380,33 @@
                 jax.ShapeDtypeStruct((MEMBERS,), jnp.int32),
             ),
             (vmem(), vmem(), vmem(), smem()),
-            [smem()] * 3 + [vmem()] + [anywhere()] * (2 * MEMBERS + (1 if level else 0)),
+            [smem()] * 3 + [vmem()] * (2 if level else 1) + [anywhere()] * (2 * MEMBERS),
             [
                 pltpu.VMEM((RING, *tile), jnp.bfloat16),
-                pltpu.VMEM((RING, *block), jnp.bfloat16),
-                pltpu.SemaphoreType.DMA((RING,)),
                 pltpu.SemaphoreType.DMA((RING,)),
                 pltpu.SemaphoreType.DMA((MEMBERS * (1 + READY),)),
             ],
-            (levels, edges, starts, held, *((store,) if level else ()), *tiles, *inverses),
+            (levels, edges, starts, held, *((received,) if level else ()), *tiles, *inverses),
             32 << 20,
             1 << 20,
         )
 
-    def solve(level, received, store, totals, ready, info):
+    def solve(level, received, totals, ready, info):
         last = level == LEVELS - 1
-        held_store = (store,) if 1 < level and not last else ()
-        operands = (edges, starts, info, totals, ready, received, *tiles, *held_store)
-        extra = MEMBERS * (width_k - READY)
-        return pl.pallas_call(
+        return call(
             functools.partial(solve_level, level, width_k, owners),
-            out_shape=(piece_shape,) if last else (piece_shape, spread_shape, store_shape),
-            in_specs=[smem()] * 3 + [vmem()] * 3 + [anywhere()] * (MEMBERS + len(held_store)),
-            out_specs=(vmem(),) if last else (vmem(), vmem(), anywhere()),
-            scratch_shapes=[
-                pltpu.VMEM((extra, *tile), jnp.bfloat16),
-                pltpu.SemaphoreType.DMA((extra,)),
-            ]
-            + ([] if last else [pltpu.SemaphoreType.DMA((1,))]),
-            input_output_aliases={len(operands) - 1: 2} if held_store else {},
-            compiler_params=pltpu.CompilerParams(vmem_limit_bytes=GRANT),
-            cost_estimate=pl.CostEstimate(
-                flops=4 << 20, bytes_accessed=1 << 18, transcendentals=0
-            ),
-            name=f"solve_{level}",
-        )(*operands)
+            f"solve_{level}",
+            (piece_shape,) if last else (piece_shape, spread_shape),
+            (vmem(),) if last else (vmem(), vmem()),
+            [smem()] * 3 + [vmem()] * 3 + [anywhere()] * MEMBERS,
+            [
+                pltpu.VMEM((MEMBERS * (width_k - READY), *tile), jnp.bfloat16),
+                pltpu.SemaphoreType.DMA((MEMBERS * (width_k - READY),)),
+            ],
+            (edges, starts, info, totals, ready, received, *tiles),
+            4 << 20,
+            1 << 18,
+        )
 
     def collect(base, befores, pieces):
         return call(
@@ -446,16 +421,16 @@
             1 << 18,
         )
 
-    store = None
+    received = None
     for level in range(1, LEVELS):
-        held, totals, ready, info = prepare(level - 1, store, held)
+        held, totals, ready, info = prepare(level - 1, received, held)
         if level == LEVELS - 1:
             early = collect(0, (), pieces)
-        piece, *more = solve(level, arriving, store, totals, ready, info)
-        if more:
-            spread, store = more
+        received = arriving
+        piece, *spread = solve(level, received, totals, ready, info)
+        if level < LEVELS - 1:
             pieces.append(piece)
-            arriving = exchanged(spread)
+            arriving = exchanged(*spread)
 
     mine, theirs = collect(LEVELS - 1, early, (piece,))
     theirs = swapped(theirs)

time: 371 us -> 371 us (level)
  Pallas kernels: 108 us -> 76.8 us
  local copies, waits for them, and re-layouts: 4.34 us -> 17.5 us
  waiting for transfers between devices: 154 us -> 166 us
  starting transfers between devices: 98.6 us -> 104 us
    pallas_call x15 -> x0, Pallas kernels: 39.6 us -> none  [solve(): pl.pallas_call(functools.partial(solve_level, level, width_k, owners), ou...]
    unnamed x12 -> x72, local copies, waits for them, and re-layouts: 3.27 us -> 16.5 us
    all_to_all x15, waiting for transfers between devices: 151 us -> 163 us  [exchanged(): lax.all_to_all(spread, CHIPS, 0, 0, tiled=True).reshape(owners, *block)]
    pallas_call x19 -> x34, Pallas kernels: 68.1 us -> 76.8 us  [call(): pl.pallas_call(kernel, out_shape=out_shape, in_specs=in_specs, out_specs=...]
    all_to_all x15, starting transfers between devices: 81.5 us -> 87 us  [exchanged(): lax.all_to_all(spread, CHIPS, 0, 0, tiled=True).reshape(owners, *block)]
  transfers between devices with their start and end apart: 21 -> 21, of which waited for: 18 -> 18; matrix products, arithmetic and copies ran while one was open for 1% -> 1% of each run, Pallas kernels for 18% -> 14%
where the time goes in v4:
time: 371 us; the launch traced here: 367 us
  waiting for transfers between devices  166 us (45%)
  starting transfers between devices  104 us (28%)
  Pallas kernels  76.8 us (21%)
  local copies, waits for them, and re-layouts  17.5 us (5%)
    all_to_all x15, waiting for transfers between devices, exchanged(): lax.all_to_all(spread, CHIPS, 0, 0, tiled=True).reshape(owners, *block)  163 us
    all_to_all x15, starting transfers between devices, exchanged(): lax.all_to_all(spread, CHIPS, 0, 0, tiled=True).reshape(owners, *block)  87 us
    pallas_call x34, Pallas kernels, call(): pl.pallas_call(kernel, out_shape=out_shape, in_specs=in_specs, out_specs=...  76.8 us
    ppermute x6, starting transfers between devices, swapped(): return lax.ppermute(value, CORE, SWAP)  16.8 us
    unnamed x72, local copies, waits for them, and re-layouts  16.5 us
  transfers between devices with their start and end apart: 21, of which 18 were waited for; matrix products, arithmetic and copies ran while one was open for 1% of the time, Pallas kernels for 14%

profile of v4, /device:TPU:1, one launch (start us, length us, event | category | flops | bytes accessed | tf_op | source)
XLA Modules:
  0.0 367.0 jit_solution(3828142851603418417)
XLA Ops:
  7.9 11.2 %all-to-all-start = ((bf16[64,2,32,128]{3,2,1,0:T(8,128)(2,1)}), bf16[64,2,32,128]{3,2,1,0:T(8,128)(2,1)S(1)}, u32[]{:S(2)}, u32[]{:S(2)}) async-start(bf16[64,2,32,128]{3,2,1,0:T(8,128)(2,1)} %get-tuple-element.112), calls=%async_computation | async-start | bytes 2097152 | tf_op jit(solution)/shard_map/all_to_all | solution.py:335
  23.4 5.4 %list_edges.1 = (s32[256]{0:T(256)S(1)}, s32[65]{0:T(128)S(1)}) custom-call(s32[256]{0:T(256)S(1)} %reshape.60.columns, s32[16]{0:T(128)S(1)} %pad_add_fusion.1.counts, s32[1024]{0:T(1024)S(1)} %bitcast.81), custom_call_target="tpu_custom_call" | custom-call | flops 8388608 | bytes 1048576 | tf_op jit(solution)/shard_map/list_edges/pallas_call | solution.py:320
  28.8 2.3 prepare_0.1
  31.1 5.1 %all-to-all-done = bf16[64,2,32,128]{3,2,1,0:T(8,128)(2,1)S(1)} async-done(((bf16[64,2,32,128]{3,2,1,0:T(8,128)(2,1)}), bf16[64,2,32,128]{3,2,1,0:T(8,128)(2,1)S(1)}, u32[]{:S(2)}, u32[]{:S(2)}) %all-to-all-start) | async-done | bytes 1048608 | tf_op jit(solution)/shard_map/all_to_all | solution.py:335
  36.2 2.4 solve_1.1
  39.7 7.8 %all-to-all-start.1 = ((bf16[64,2,32,128]{3,2,1,0:T(8,128)(2,1)}), bf16[64,2,32,128]{3,2,1,0:T(8,128)(2,1)S(1)}, u32[]{:S(2)}, u32[]{:S(2)}) async-start(bf16[64,2,32,128]{3,2,1,0:T(8,128)(2,1)} %copy-done.8), calls=%async_computation.1 | async-start | bytes 2097152 | tf_op jit(solution)/shard_map/all_to_all | solution.py:335
  47.5 4.6 %prepare_1.1 = (f32[16,32,128]{2,1,0:T(8,128)S(1)}, f32[2,32,128]{2,1,0:T(8,128)S(1)}, bf16[2,4,128,128]{3,2,1,0:T(8,128)(2,1)S(1)}, s32[2]{0:T(128)S(1)}) custom-call(s32[1024]{0:T(1024)S(1)} %bitcast.83, s32[256]{0:T(256)S(1)} %get-tuple-element.106.edges, s32[65]{0:T(128)S(1)} %get-tuple-element.107.starts, ...), custom_call_target="tpu_custom_call" | custom-call | flops 33554432 | bytes 1048576 | tf_op jit(solution)/shard_map/prepare_1/pallas_call | solution.py:320
  52.1 12.1 %all-to-all-done.1 = bf16[64,2,32,128]{3,2,1,0:T(8,128)(2,1)S(1)} async-done(((bf16[64,2,32,128]{3,2,1,0:T(8,128)(2,1)}), bf16[64,2,32,128]{3,2,1,0:T(8,128)(2,1)S(1)}, u32[]{:S(2)}, u32[]{:S(2)}) %all-to-all-start.1) | async-done | bytes 1048608 | tf_op jit(solution)/shard_map/all_to_all | solution.py:335
  67.0 6.3 %all-to-all-start.2 = ((bf16[64,2,32,128]{3,2,1,0:T(8,128)(2,1)}), bf16[64,2,32,128]{3,2,1,0:T(8,128)(2,1)S(1)}, u32[]{:S(2)}, u32[]{:S(2)}) async-start(bf16[64,2,32,128]{3,2,1,0:T(8,128)(2,1)} %copy-done.9), calls=%async_computation.2 | async-start | bytes 2097152 | tf_op jit(solution)/shard_map/all_to_all | solution.py:335
  73.3 2.9 prepare_2.1
  76.2 13.2 %all-to-all-done.2 = bf16[64,2,32,128]{3,2,1,0:T(8,128)(2,1)S(1)} async-done(((bf16[64,2,32,128]{3,2,1,0:T(8,128)(2,1)}), bf16[64,2,32,128]{3,2,1,0:T(8,128)(2,1)S(1)}, u32[]{:S(2)}, u32[]{:S(2)}) %all-to-all-start.2) | async-done | bytes 1048608 | tf_op jit(solution)/shard_map/all_to_all | solution.py:335
  92.2 5.9 %all-to-all-start.3 = ((bf16[64,2,32,128]{3,2,1,0:T(8,128)(2,1)}), bf16[64,2,32,128]{3,2,1,0:T(8,128)(2,1)S(1)}, u32[]{:S(2)}, u32[]{:S(2)}) async-start(bf16[64,2,32,128]{3,2,1,0:T(8,128)(2,1)} %copy-done.10), calls=%async_computation.3 | async-start | bytes 2097152 | tf_op jit(solution)/shard_map/all_to_all | solution.py:335
  98.1 3.8 %prepare_3.1 = (f32[16,32,128]{2,1,0:T(8,128)S(1)}, f32[2,32,128]{2,1,0:T(8,128)S(1)}, bf16[2,4,128,128]{3,2,1,0:T(8,128)(2,1)S(1)}, s32[2]{0:T(128)S(1)}) custom-call(s32[1024]{0:T(1024)S(1)} %bitcast.85, s32[256]{0:T(256)S(1)} %get-tuple-element.106.edges, s32[65]{0:T(128)S(1)} %get-tuple-element.107.starts, ...), custom_call_target="tpu_custom_call" | custom-call | flops 33554432 | bytes 1048576 | tf_op jit(solution)/shard_map/prepare_3/pallas_call | solution.py:320
  101.9 12.3 %all-to-all-done.3 = bf16[64,2,32,128]{3,2,1,0:T(8,128)(2,1)S(1)} async-done(((bf16[64,2,32,128]{3,2,1,0:T(8,128)(2,1)}), bf16[64,2,32,128]{3,2,1,0:T(8,128)(2,1)S(1)}, u32[]{:S(2)}, u32[]{:S(2)}) %all-to-all-start.3) | async-done | bytes 1048608 | tf_op jit(solution)/shard_map/all_to_all | solution.py:335
  116.7 6.0 %all-to-all-start.4 = ((bf16[64,2,32,128]{3,2,1,0:T(8,128)(2,1)}), bf16[64,2,32,128]{3,2,1,0:T(8,128)(2,1)S(1)}, u32[]{:S(2)}, u32[]{:S(2)}) async-start(bf16[64,2,32,128]{3,2,1,0:T(8,128)(2,1)} %copy-done.11), calls=%async_computation.4 | async-start | bytes 2097152 | tf_op jit(solution)/shard_map/all_to_all | solution.py:335
  122.7 4.0 %prepare_4.1 = (f32[16,32,128]{2,1,0:T(8,128)S(1)}, f32[2,32,128]{2,1,0:T(8,128)S(1)}, bf16[2,4,128,128]{3,2,1,0:T(8,128)(2,1)S(1)}, s32[2]{0:T(128)S(1)}) custom-call(s32[1024]{0:T(1024)S(1)} %bitcast.86, s32[256]{0:T(256)S(1)} %get-tuple-element.106.edges, s32[65]{0:T(128)S(1)} %get-tuple-element.107.starts, ...), custom_call_target="tpu_custom_call" | custom-call | flops 33554432 | bytes 1048576 | tf_op jit(solution)/shard_map/prepare_4/pallas_call | solution.py:320
  126.7 12.0 %all-to-all-done.4 = bf16[64,2,32,128]{3,2,1,0:T(8,128)(2,1)S(1)} async-done(((bf16[64,2,32,128]{3,2,1,0:T(8,128)(2,1)}), bf16[64,2,32,128]{3,2,1,0:T(8,128)(2,1)S(1)}, u32[]{:S(2)}, u32[]{:S(2)}) %all-to-all-start.4) | async-done | bytes 1048608 | tf_op jit(solution)/shard_map/all_to_all | solution.py:335
  140.8 6.1 %all-to-all-start.5 = ((bf16[64,2,32,128]{3,2,1,0:T(8,128)(2,1)}), bf16[64,2,32,128]{3,2,1,0:T(8,128)(2,1)S(1)}, u32[]{:S(2)}, u32[]{:S(2)}) async-start(bf16[64,2,32,128]{3,2,1,0:T(8,128)(2,1)} %copy-done.12), calls=%async_computation.5 | async-start | bytes 2097152 | tf_op jit(solution)/shard_map/all_to_all | solution.py:335
  146.9 2.8 prepare_5.1
  149.7 12.4 %all-to-all-done.5 = bf16[64,2,32,128]{3,2,1,0:T(8,128)(2,1)S(1)} async-done(((bf16[64,2,32,128]{3,2,1,0:T(8,128)(2,1)}), bf16[64,2,32,128]{3,2,1,0:T(8,128)(2,1)S(1)}, u32[]{:S(2)}, u32[]{:S(2)}) %all-to-all-start.5) | async-done | bytes 1048608 | tf_op jit(solution)/shard_map/all_to_all | solution.py:335
  164.5 4.9 %all-to-all-start.6 = ((bf16[64,2,32,128]{3,2,1,0:T(8,128)(2,1)}), bf16[64,2,32,128]{3,2,1,0:T(8,128)(2,1)S(1)}, u32[]{:S(2)}, u32[]{:S(2)}) async-start(bf16[64,2,32,128]{3,2,1,0:T(8,128)(2,1)} %copy-done.13), calls=%async_computation.6 | async-start | bytes 2097152 | tf_op jit(solution)/shard_map/all_to_all | solution.py:335
  169.5 2.5 prepare_6.1
  172.0 11.6 %all-to-all-done.6 = bf16[64,2,32,128]{3,2,1,0:T(8,128)(2,1)S(1)} async-done(((bf16[64,2,32,128]{3,2,1,0:T(8,128)(2,1)}), bf16[64,2,32,128]{3,2,1,0:T(8,128)(2,1)S(1)}, u32[]{:S(2)}, u32[]{:S(2)}) %all-to-all-start.6) | async-done | bytes 1048608 | tf_op jit(solution)/shard_map/all_to_all | solution.py:335
  186.0 4.9 %all-to-all-start.7 = ((bf16[64,2,32,128]{3,2,1,0:T(8,128)(2,1)}), bf16[64,2,32,128]{3,2,1,0:T(8,128)(2,1)S(1)}, u32[]{:S(2)}, u32[]{:S(2)}) async-start(bf16[64,2,32,128]{3,2,1,0:T(8,128)(2,1)} %copy-done.14), calls=%async_computation.7 | async-start | bytes 2097152 | tf_op jit(solution)/shard_map/all_to_all | solution.py:335
  190.9 3.2 prepare_7.1
  194.2 10.7 %all-to-all-done.7 = bf16[64,2,32,128]{3,2,1,0:T(8,128)(2,1)S(1)} async-done(((bf16[64,2,32,128]{3,2,1,0:T(8,128)(2,1)}), bf16[64,2,32,128]{3,2,1,0:T(8,128)(2,1)S(1)}, u32[]{:S(2)}, u32[]{:S(2)}) %all-to-all-start.7) | async-done | bytes 1048608 | tf_op jit(solution)/shard_map/all_to_all | solution.py:335
  206.9 5.0 %all-to-all-start.8 = ((bf16[64,2,32,128]{3,2,1,0:T(8,128)(2,1)}), bf16[64,2,32,128]{3,2,1,0:T(8,128)(2,1)S(1)}, u32[]{:S(2)}, u32[]{:S(2)}) async-start(bf16[64,2,32,128]{3,2,1,0:T(8,128)(2,1)} %copy-done.15), calls=%async_computation.8 | async-start | bytes 2097152 | tf_op jit(solution)/shard_map/all_to_all | solution.py:335
  212.0 2.8 prepare_8.1
  214.8 11.4 %all-to-all-done.8 = bf16[64,2,32,128]{3,2,1,0:T(8,128)(2,1)S(1)} async-done(((bf16[64,2,32,128]{3,2,1,0:T(8,128)(2,1)}), bf16[64,2,32,128]{3,2,1,0:T(8,128)(2,1)S(1)}, u32[]{:S(2)}, u32[]{:S(2)}) %all-to-all-start.8) | async-done | bytes 1048608 | tf_op jit(solution)/shard_map/all_to_all | solution.py:335
  228.2 4.7 %all-to-all-start.9 = ((bf16[64,2,32,128]{3,2,1,0:T(8,128)(2,1)}), bf16[64,2,32,128]{3,2,1,0:T(8,128)(2,1)S(1)}, u32[]{:S(2)}, u32[]{:S(2)}) async-start(bf16[64,2,32,128]{3,2,1,0:T(8,128)(2,1)} %copy-done.16), calls=%async_computation.9 | async-start | bytes 2097152 | tf_op jit(solution)/shard_map/all_to_all | solution.py:335
  232.9 3.3 prepare_9.1
  236.2 10.4 %all-to-all-done.9 = bf16[64,2,32,128]{3,2,1,0:T(8,128)(2,1)S(1)} async-done(((bf16[64,2,32,128]{3,2,1,0:T(8,128)(2,1)}), bf16[64,2,32,128]{3,2,1,0:T(8,128)(2,1)S(1)}, u32[]{:S(2)}, u32[]{:S(2)}) %all-to-all-start.9) | async-done | bytes 1048608 | tf_op jit(solution)/shard_map/all_to_all | solution.py:335
  249.0 4.7 %all-to-all-start.10 = ((bf16[64,2,32,128]{3,2,1,0:T(8,128)(2,1)}), bf16[64,2,32,128]{3,2,1,0:T(8,128)(2,1)S(1)}, u32[]{:S(2)}, u32[]{:S(2)}) async-start(bf16[64,2,32,128]{3,2,1,0:T(8,128)(2,1)} %copy-done.17), calls=%async_computation.10 | async-start | bytes 2097152 | tf_op jit(solution)/shard_map/all_to_all | solution.py:335
  253.7 2.6 prepare_10.1
  256.3 10.6 %all-to-all-done.10 = bf16[64,2,32,128]{3,2,1,0:T(8,128)(2,1)S(1)} async-done(((bf16[64,2,32,128]{3,2,1,0:T(8,128)(2,1)}), bf16[64,2,32,128]{3,2,1,0:T(8,128)(2,1)S(1)}, u32[]{:S(2)}, u32[]{:S(2)}) %all-to-all-start.10) | async-done | bytes 1048608 | tf_op jit(solution)/shard_map/all_to_all | solution.py:335
  269.1 5.2 %all-to-all-start.11 = ((bf16[64,2,32,128]{3,2,1,0:T(8,128)(2,1)}), bf16[64,2,32,128]{3,2,1,0:T(8,128)(2,1)S(1)}, u32[]{:S(2)}, u32[]{:S(2)}) async-start(bf16[64,2,32,128]{3,2,1,0:T(8,128)(2,1)} %copy-done.18), calls=%async_computation.11 | async-start | bytes 2097152 | tf_op jit(solution)/shard_map/all_to_all | solution.py:335
  274.2 2.4 prepare_11.1
  276.6 10.9 %all-to-all-done.11 = bf16[64,2,32,128]{3,2,1,0:T(8,128)(2,1)S(1)} async-done(((bf16[64,2,32,128]{3,2,1,0:T(8,128)(2,1)}), bf16[64,2,32,128]{3,2,1,0:T(8,128)(2,1)S(1)}, u32[]{:S(2)}, u32[]{:S(2)}) %all-to-all-start.11) | async-done | bytes 1048608 | tf_op jit(solution)/shard_map/all_to_all | solution.py:335
  290.3 4.9 %all-to-all-start.12 = ((bf16[64,2,32,128]{3,2,1,0:T(8,128)(2,1)}), bf16[64,2,32,128]{3,2,1,0:T(8,128)(2,1)S(1)}, u32[]{:S(2)}, u32[]{:S(2)}) async-start(bf16[64,2,32,128]{3,2,1,0:T(8,128)(2,1)} %copy-done.19), calls=%async_computation.12 | async-start | bytes 2097152 | tf_op jit(solution)/shard_map/all_to_all | solution.py:335
  295.2 3.4 prepare_12.1
  298.6 9.8 %all-to-all-done.12 = bf16[64,2,32,128]{3,2,1,0:T(8,128)(2,1)S(1)} async-done(((bf16[64,2,32,128]{3,2,1,0:T(8,128)(2,1)}), bf16[64,2,32,128]{3,2,1,0:T(8,128)(2,1)S(1)}, u32[]{:S(2)}, u32[]{:S(2)}) %all-to-all-start.12) | async-done | bytes 1048608 | tf_op jit(solution)/shard_map/all_to_all | solution.py:335
  308.4 2.8 solve_13.1
  311.2 4.7 %all-to-all-start.13 = ((bf16[64,2,32,128]{3,2,1,0:T(8,128)(2,1)}), bf16[64,2,32,128]{3,2,1,0:T(8,128)(2,1)S(1)}, u32[]{:S(2)}, u32[]{:S(2)}) async-start(bf16[64,2,32,128]{3,2,1,0:T(8,128)(2,1)} %get-tuple-element.190), calls=%async_computation.13 | async-start | bytes 2097152 | tf_op jit(solution)/shard_map/all_to_all | solution.py:335
  317.1 2.2 prepare_13.1
  319.3 9.7 %all-to-all-done.13 = bf16[64,2,32,128]{3,2,1,0:T(8,128)(2,1)S(1)} async-done(((bf16[64,2,32,128]{3,2,1,0:T(8,128)(2,1)}), bf16[64,2,32,128]{3,2,1,0:T(8,128)(2,1)S(1)}, u32[]{:S(2)}, u32[]{:S(2)}) %all-to-all-start.13) | async-done | bytes 1048608 | tf_op jit(solution)/shard_map/all_to_all | solution.py:335
  331.5 4.9 %all-to-all-start.14 = ((bf16[64,2,32,128]{3,2,1,0:T(8,128)(2,1)}), bf16[64,2,32,128]{3,2,1,0:T(8,128)(2,1)S(1)}, u32[]{:S(2)}, u32[]{:S(2)}) async-start(bf16[64,2,32,128]{3,2,1,0:T(8,128)(2,1)} %copy-done.7), calls=%async_computation.14 | async-start | bytes 2097152 | tf_op jit(solution)/shard_map/all_to_all | solution.py:335
  339.3 10.3 %all-to-all-done.14 = bf16[64,2,32,128]{3,2,1,0:T(8,128)(2,1)S(1)} async-done(((bf16[64,2,32,128]{3,2,1,0:T(8,128)(2,1)}), bf16[64,2,32,128]{3,2,1,0:T(8,128)(2,1)S(1)}, u32[]{:S(2)}, u32[]{:S(2)}) %all-to-all-start.14) | async-done | bytes 1048608 | tf_op jit(solution)/shard_map/all_to_all | solution.py:335
  351.1 14.3 %collective-permute-start.5 = (bf16[8,32,128]{2,1,0:T(8,128)(2,1)S(1)}, bf16[8,32,128]{2,1,0:T(8,128)(2,1)S(1)}, u32[]{:S(2)}, u32[]{:S(2)}) collective-permute-start(bf16[8,32,128]{2,1,0:T(8,128)(2,1)S(1)} %get-tuple-element.200), channel_id=1, source_target_pairs={{0,1},{1,0},{2,3},{3,2},{4,5},{5,4},{6,7},{7,6},{8,9},{9,8},{10,11... | collective-permute-start | bytes 196616 | tf_op jit(solution)/shard_map/ppermute | solution.py:310
  (106 shorter events, 48.9 us)
Async XLA Ops:
  0.0 28.8 %copy-start.1 = (bf16[8,1,128,128]{3,2,1,0:T(8,128)(2,1)S(1)}, bf16[8,1,128,128]{3,2,1,0:T(8,128)(2,1)}, u32[]{:S(2)}) copy-start(bf16[8,1,128,128]{3,2,1,0:T(8,128)(2,1)} %param.8) | copy-start | bytes 786436
  0.0 3.8 %collective-permute-start.1 = (bf16[8,128,128]{2,1,0:T(8,128)(2,1)}, bf16[8,128,128]{2,1,0:T(8,128)(2,1)S(1)}, u32[]{:S(2)}, u32[]{:S(2)}) collective-permute-start(bf16[8,128,128]{2,1,0:T(8,128)(2,1)} %bitcast.34), channel_id=1, source_target_pairs={{0,1},{1,0},{2,3},{3,2},{4,5},{5,4},{6,7},{7,6},{8,9},{9,8},{10,11... | collective-permute-start | bytes 786440 | tf_op jit(solution)/shard_map/ppermute | solution.py:310
  2.4 1.4 collective-permute-start
  7.7 21.2 %collective-permute-start.4 = (bf16[8,16,128,128]{3,2,1,0:T(8,128)(2,1)}, bf16[8,16,128,128]{3,2,1,0:T(8,128)(2,1)}, u32[]{:S(2)}, u32[]{:S(2)}) collective-permute-start(bf16[8,16,128,128]{3,2,1,0:T(8,128)(2,1)} %bitcast.99), channel_id=1, source_target_pairs={{0,1},{1,0},{2,3},{3,2},{4,5},{5,4},{6,7},{7,6},{8,9},{9,8},{10,11... | collective-permute-start | bytes 12582920 | tf_op jit(solution)/shard_map/ppermute | solution.py:310
  7.9 28.3 %all-to-all-start = ((bf16[64,2,32,128]{3,2,1,0:T(8,128)(2,1)}), bf16[64,2,32,128]{3,2,1,0:T(8,128)(2,1)S(1)}, u32[]{:S(2)}, u32[]{:S(2)}) async-start(bf16[64,2,32,128]{3,2,1,0:T(8,128)(2,1)} %get-tuple-element.112), calls=%async_computation | async-start | bytes 2097152 | tf_op jit(solution)/shard_map/all_to_all | solution.py:335
  19.2 2.8 collective-permute-start.2
  19.9 1.3 collective-permute-start.3
  36.2 11.3 %copy-start.6 = (s32[8,128]{1,0:T(8,128)S(1)}, s32[8,128]{1,0:T(8,128)}, u32[]{:S(2)}) copy-start(s32[8,128]{1,0:T(8,128)} %param.11) | copy-start | bytes 12292
  39.7 24.5 %all-to-all-start.1 = ((bf16[64,2,32,128]{3,2,1,0:T(8,128)(2,1)}), bf16[64,2,32,128]{3,2,1,0:T(8,128)(2,1)S(1)}, u32[]{:S(2)}, u32[]{:S(2)}) async-start(bf16[64,2,32,128]{3,2,1,0:T(8,128)(2,1)} %copy-done.8), calls=%async_computation.1 | async-start | bytes 2097152 | tf_op jit(solution)/shard_map/all_to_all | solution.py:335
  66.0 1.0 copy-start.9
  67.0 22.5 %all-to-all-start.2 = ((bf16[64,2,32,128]{3,2,1,0:T(8,128)(2,1)}), bf16[64,2,32,128]{3,2,1,0:T(8,128)(2,1)S(1)}, u32[]{:S(2)}, u32[]{:S(2)}) async-start(bf16[64,2,32,128]{3,2,1,0:T(8,128)(2,1)} %copy-done.9), calls=%async_computation.2 | async-start | bytes 2097152 | tf_op jit(solution)/shard_map/all_to_all | solution.py:335
  92.2 22.0 %all-to-all-start.3 = ((bf16[64,2,32,128]{3,2,1,0:T(8,128)(2,1)}), bf16[64,2,32,128]{3,2,1,0:T(8,128)(2,1)S(1)}, u32[]{:S(2)}, u32[]{:S(2)}) async-start(bf16[64,2,32,128]{3,2,1,0:T(8,128)(2,1)} %copy-done.10), calls=%async_computation.3 | async-start | bytes 2097152 | tf_op jit(solution)/shard_map/all_to_all | solution.py:335
  115.7 1.0 copy-start.11
  116.7 22.0 %all-to-all-start.4 = ((bf16[64,2,32,128]{3,2,1,0:T(8,128)(2,1)}), bf16[64,2,32,128]{3,2,1,0:T(8,128)(2,1)S(1)}, u32[]{:S(2)}, u32[]{:S(2)}) async-start(bf16[64,2,32,128]{3,2,1,0:T(8,128)(2,1)} %copy-done.11), calls=%async_computation.4 | async-start | bytes 2097152 | tf_op jit(solution)/shard_map/all_to_all | solution.py:335
  140.8 21.3 %all-to-all-start.5 = ((bf16[64,2,32,128]{3,2,1,0:T(8,128)(2,1)}), bf16[64,2,32,128]{3,2,1,0:T(8,128)(2,1)S(1)}, u32[]{:S(2)}, u32[]{:S(2)}) async-start(bf16[64,2,32,128]{3,2,1,0:T(8,128)(2,1)} %copy-done.12), calls=%async_computation.5 | async-start | bytes 2097152 | tf_op jit(solution)/shard_map/all_to_all | solution.py:335
  163.5 1.0 copy-start.13
  164.5 4.9 %copy-start.20 = (bf16[2,32,128]{2,1,0:T(8,128)(2,1)}, bf16[2,32,128]{2,1,0:T(8,128)(2,1)S(1)}, u32[]{:S(2)}) copy-start(bf16[2,32,128]{2,1,0:T(8,128)(2,1)S(1)} %get-tuple-element.143.refs_6_) | copy-start | bytes 49156
  164.5 19.1 %all-to-all-start.6 = ((bf16[64,2,32,128]{3,2,1,0:T(8,128)(2,1)}), bf16[64,2,32,128]{3,2,1,0:T(8,128)(2,1)S(1)}, u32[]{:S(2)}, u32[]{:S(2)}) async-start(bf16[64,2,32,128]{3,2,1,0:T(8,128)(2,1)} %copy-done.13), calls=%async_computation.6 | async-start | bytes 2097152 | tf_op jit(solution)/shard_map/all_to_all | solution.py:335
  185.0 1.0 copy-start.14
  186.0 4.9 %copy-start.22 = (bf16[2,32,128]{2,1,0:T(8,128)(2,1)}, bf16[2,32,128]{2,1,0:T(8,128)(2,1)S(1)}, u32[]{:S(2)}) copy-start(bf16[2,32,128]{2,1,0:T(8,128)(2,1)S(1)} %get-tuple-element.149.refs_7_) | copy-start | bytes 49156
  186.0 18.8 %all-to-all-start.7 = ((bf16[64,2,32,128]{3,2,1,0:T(8,128)(2,1)}), bf16[64,2,32,128]{3,2,1,0:T(8,128)(2,1)S(1)}, u32[]{:S(2)}, u32[]{:S(2)}) async-start(bf16[64,2,32,128]{3,2,1,0:T(8,128)(2,1)} %copy-done.14), calls=%async_computation.7 | async-start | bytes 2097152 | tf_op jit(solution)/shard_map/all_to_all | solution.py:335
  205.9 1.0 copy-start.15
  206.9 5.0 %copy-start.24 = (bf16[2,32,128]{2,1,0:T(8,128)(2,1)}, bf16[2,32,128]{2,1,0:T(8,128)(2,1)S(1)}, u32[]{:S(2)}) copy-start(bf16[2,32,128]{2,1,0:T(8,128)(2,1)S(1)} %get-tuple-element.155.refs_8_) | copy-start | bytes 49156
  206.9 19.2 %all-to-all-start.8 = ((bf16[64,2,32,128]{3,2,1,0:T(8,128)(2,1)}), bf16[64,2,32,128]{3,2,1,0:T(8,128)(2,1)S(1)}, u32[]{:S(2)}, u32[]{:S(2)}) async-start(bf16[64,2,32,128]{3,2,1,0:T(8,128)(2,1)} %copy-done.15), calls=%async_computation.8 | async-start | bytes 2097152 | tf_op jit(solution)/shard_map/all_to_all | solution.py:335
  227.2 1.0 copy-start.16
  228.2 4.7 %copy-start.26 = (bf16[2,32,128]{2,1,0:T(8,128)(2,1)}, bf16[2,32,128]{2,1,0:T(8,128)(2,1)S(1)}, u32[]{:S(2)}) copy-start(bf16[2,32,128]{2,1,0:T(8,128)(2,1)S(1)} %get-tuple-element.161.refs_9_) | copy-start | bytes 49156
  228.2 18.3 %all-to-all-start.9 = ((bf16[64,2,32,128]{3,2,1,0:T(8,128)(2,1)}), bf16[64,2,32,128]{3,2,1,0:T(8,128)(2,1)S(1)}, u32[]{:S(2)}, u32[]{:S(2)}) async-start(bf16[64,2,32,128]{3,2,1,0:T(8,128)(2,1)} %copy-done.16), calls=%async_computation.9 | async-start | bytes 2097152 | tf_op jit(solution)/shard_map/all_to_all | solution.py:335
  248.0 1.0 copy-start.17
  249.0 4.7 %copy-start.28 = (bf16[2,32,128]{2,1,0:T(8,128)(2,1)}, bf16[2,32,128]{2,1,0:T(8,128)(2,1)S(1)}, u32[]{:S(2)}) copy-start(bf16[2,32,128]{2,1,0:T(8,128)(2,1)S(1)} %get-tuple-element.167.refs_10_) | copy-start | bytes 49156
  249.0 17.9 %all-to-all-start.10 = ((bf16[64,2,32,128]{3,2,1,0:T(8,128)(2,1)}), bf16[64,2,32,128]{3,2,1,0:T(8,128)(2,1)S(1)}, u32[]{:S(2)}, u32[]{:S(2)}) async-start(bf16[64,2,32,128]{3,2,1,0:T(8,128)(2,1)} %copy-done.17), calls=%async_computation.10 | async-start | bytes 2097152 | tf_op jit(solution)/shard_map/all_to_all | solution.py:335
  269.1 5.2 %copy-start.30 = (bf16[2,32,128]{2,1,0:T(8,128)(2,1)}, bf16[2,32,128]{2,1,0:T(8,128)(2,1)S(1)}, u32[]{:S(2)}) copy-start(bf16[2,32,128]{2,1,0:T(8,128)(2,1)S(1)} %get-tuple-element.173.refs_11_) | copy-start | bytes 49156
  269.1 18.4 %all-to-all-start.11 = ((bf16[64,2,32,128]{3,2,1,0:T(8,128)(2,1)}), bf16[64,2,32,128]{3,2,1,0:T(8,128)(2,1)S(1)}, u32[]{:S(2)}, u32[]{:S(2)}) async-start(bf16[64,2,32,128]{3,2,1,0:T(8,128)(2,1)} %copy-done.18), calls=%async_computation.11 | async-start | bytes 2097152 | tf_op jit(solution)/shard_map/all_to_all | solution.py:335
  290.3 4.9 %copy-start.32 = (bf16[2,32,128]{2,1,0:T(8,128)(2,1)}, bf16[2,32,128]{2,1,0:T(8,128)(2,1)S(1)}, u32[]{:S(2)}) copy-start(bf16[2,32,128]{2,1,0:T(8,128)(2,1)S(1)} %get-tuple-element.179.refs_12_) | copy-start | bytes 49156
  290.3 18.1 %all-to-all-start.12 = ((bf16[64,2,32,128]{3,2,1,0:T(8,128)(2,1)}), bf16[64,2,32,128]{3,2,1,0:T(8,128)(2,1)S(1)}, u32[]{:S(2)}, u32[]{:S(2)}) async-start(bf16[64,2,32,128]{3,2,1,0:T(8,128)(2,1)} %copy-done.19), calls=%async_computation.12 | async-start | bytes 2097152 | tf_op jit(solution)/shard_map/all_to_all | solution.py:335
  308.4 2.8 copy-start.2
  311.1 4.7 %copy-start.34 = (bf16[2,32,128]{2,1,0:T(8,128)(2,1)}, bf16[2,32,128]{2,1,0:T(8,128)(2,1)S(1)}, u32[]{:S(2)}) copy-start(bf16[2,32,128]{2,1,0:T(8,128)(2,1)S(1)} %get-tuple-element.185.refs_13_) | copy-start | bytes 49156
  311.2 17.9 %all-to-all-start.13 = ((bf16[64,2,32,128]{3,2,1,0:T(8,128)(2,1)}), bf16[64,2,32,128]{3,2,1,0:T(8,128)(2,1)S(1)}, u32[]{:S(2)}, u32[]{:S(2)}) async-start(bf16[64,2,32,128]{3,2,1,0:T(8,128)(2,1)} %get-tuple-element.190), calls=%async_computation.13 | async-start | bytes 2097152 | tf_op jit(solution)/shard_map/all_to_all | solution.py:335
  315.8 1.2 copy-start.3
  329.0 7.4 %copy-start.21 = (bf16[2,32,128]{2,1,0:T(8,128)(2,1)S(1)}, bf16[2,32,128]{2,1,0:T(8,128)(2,1)}, u32[]{:S(2)}) copy-start(bf16[2,32,128]{2,1,0:T(8,128)(2,1)} %copy-done.20) | copy-start | bytes 49156
  329.0 7.4 %copy-start.23 = (bf16[2,32,128]{2,1,0:T(8,128)(2,1)S(1)}, bf16[2,32,128]{2,1,0:T(8,128)(2,1)}, u32[]{:S(2)}) copy-start(bf16[2,32,128]{2,1,0:T(8,128)(2,1)} %copy-done.22) | copy-start | bytes 49156
  329.0 7.4 %copy-start.25 = (bf16[2,32,128]{2,1,0:T(8,128)(2,1)S(1)}, bf16[2,32,128]{2,1,0:T(8,128)(2,1)}, u32[]{:S(2)}) copy-start(bf16[2,32,128]{2,1,0:T(8,128)(2,1)} %copy-done.24) | copy-start | bytes 49156
  329.0 7.4 %copy-start.27 = (bf16[2,32,128]{2,1,0:T(8,128)(2,1)S(1)}, bf16[2,32,128]{2,1,0:T(8,128)(2,1)}, u32[]{:S(2)}) copy-start(bf16[2,32,128]{2,1,0:T(8,128)(2,1)} %copy-done.26) | copy-start | bytes 49156
  329.0 7.4 %copy-start.29 = (bf16[2,32,128]{2,1,0:T(8,128)(2,1)S(1)}, bf16[2,32,128]{2,1,0:T(8,128)(2,1)}, u32[]{:S(2)}) copy-start(bf16[2,32,128]{2,1,0:T(8,128)(2,1)} %copy-done.28) | copy-start | bytes 49156
  329.0 7.4 %copy-start.31 = (bf16[2,32,128]{2,1,0:T(8,128)(2,1)S(1)}, bf16[2,32,128]{2,1,0:T(8,128)(2,1)}, u32[]{:S(2)}) copy-start(bf16[2,32,128]{2,1,0:T(8,128)(2,1)} %copy-done.30) | copy-start | bytes 49156
  329.0 7.4 %copy-start.33 = (bf16[2,32,128]{2,1,0:T(8,128)(2,1)S(1)}, bf16[2,32,128]{2,1,0:T(8,128)(2,1)}, u32[]{:S(2)}) copy-start(bf16[2,32,128]{2,1,0:T(8,128)(2,1)} %copy-done.32) | copy-start | bytes 49156
  329.1 7.4 %copy-start.35 = (bf16[2,32,128]{2,1,0:T(8,128)(2,1)S(1)}, bf16[2,32,128]{2,1,0:T(8,128)(2,1)}, u32[]{:S(2)}) copy-start(bf16[2,32,128]{2,1,0:T(8,128)(2,1)} %copy-done.34) | copy-start | bytes 49156
  331.5 18.1 %all-to-all-start.14 = ((bf16[64,2,32,128]{3,2,1,0:T(8,128)(2,1)}), bf16[64,2,32,128]{3,2,1,0:T(8,128)(2,1)S(1)}, u32[]{:S(2)}, u32[]{:S(2)}) async-start(bf16[64,2,32,128]{3,2,1,0:T(8,128)(2,1)} %copy-done.7), calls=%async_computation.14 | async-start | bytes 2097152 | tf_op jit(solution)/shard_map/all_to_all | solution.py:335
  351.1 15.2 %collective-permute-start.5 = (bf16[8,32,128]{2,1,0:T(8,128)(2,1)S(1)}, bf16[8,32,128]{2,1,0:T(8,128)(2,1)S(1)}, u32[]{:S(2)}, u32[]{:S(2)}) collective-permute-start(bf16[8,32,128]{2,1,0:T(8,128)(2,1)S(1)} %get-tuple-element.200), channel_id=1, source_target_pairs={{0,1},{1,0},{2,3},{3,2},{4,5},{5,4},{6,7},{7,6},{8,9},{9,8},{10,11... | collective-permute-start | bytes 196616 | tf_op jit(solution)/shard_map/ppermute | solution.py:310
  (9 other events, 8.3 us)

commit v5 on v3

--- a/solution.py
+++ b/solution.py
@@ -16,6 +16,7 @@
 MEMBERS = 2
 KEYS = LEVELS * 2 * MEMBERS
 RING = 8
+FAN = 8
 GROUP = 3
 READY = 6
 GRANT = 50 << 20
@@ -111,13 +112,23 @@
     over_slots(place)
 
 
-def spread_piece(piece, spread):
-    value = piece[...]
-    for chip in range(spread.shape[0]):
-        spread[chip] = value
-
-
-def solve_first(rows, owners, levels, held, own_inverse, their_inverse, piece, spread, buf, sems):
+def spread_slot(member, piece, spread, fan, sems):
+    at = slot_of(member)
+    value = piece[at]
+    for i in range(FAN):
+        fan[member, i] = value
+    copies = [
+        pltpu.make_async_copy(
+            fan.at[member], spread.at[pl.ds(i * FAN, FAN), at], sems.at[member, i]
+        )
+        for i in range(spread.shape[0] // FAN)
+    ]
+    for copy in copies:
+        copy.start()
+    return copies
+
+
+def solve_first(rows, owners, levels, held, own_inverse, their_inverse, piece, spread, buf, sems, fan, fan_sems):
     inverses = (own_inverse, their_inverse)
     picks = [find_row(levels, owners, member, rows, 0) for member in range(MEMBERS)]
 
@@ -126,6 +137,7 @@
             inverses[member].at[jnp.maximum(picks[member], 0)], buf.at[member], sems.at[member]
         )
 
+    copies = []
     for member in range(MEMBERS):
         copy(member).start()
     for member in range(MEMBERS):
@@ -134,7 +146,9 @@
         row = held[member * rows + jnp.maximum(picks[member], 0)].astype(jnp.bfloat16)
         solved = times_transposed(row, buf[member])
         piece[at] = jnp.where(picks[member] >= 0, solved, 0.0).astype(jnp.bfloat16)
-    spread_piece(piece, spread)
+        copies += spread_slot(member, piece, spread, fan, fan_sems)
+    for spreading in copies:
+        spreading.wait()
 
 
 def prepare_level(level, rows, width_k, owners, levels, edges, starts, held_in, *refs):
@@ -238,9 +252,10 @@
     if last:
         piece, buf, sems = refs
     else:
-        piece, spread, store, buf, sems, keep_sem = refs[1 if level > 1 else 0 :]
+        piece, spread, store, buf, sems, keep_sem, *fan = refs[1 if level > 1 else 0 :]
         keep = pltpu.make_async_copy(received, store.at[level - 1], keep_sem.at[0])
         keep.start()
+    copies = []
     extra = width_k - READY
 
     def extra_copy(member, i):
@@ -291,9 +306,13 @@
             solved = times_transposed(total.astype(jnp.bfloat16), ready[member, 0])
             piece[at] = solved.astype(jnp.bfloat16)
 
+        if not last:
+            copies += spread_slot(member, piece, spread, *fan)
+
     if not last:
-        spread_piece(piece, spread)
         keep.wait()
+        for copy in copies:
+            copy.wait()
 
 
 def collect_rows(rows, owners, base, levels, *refs):
@@ -348,6 +367,11 @@
 
     store_shape = jax.ShapeDtypeStruct((LEVELS - 2, owners, *block), jnp.bfloat16)
 
+    fan = [
+        pltpu.VMEM((MEMBERS, FAN, *block), jnp.bfloat16),
+        pltpu.SemaphoreType.DMA((MEMBERS, chips // FAN)),
+    ]
+
     def exchanged(spread):
         return lax.all_to_all(spread, CHIPS, 0, 0, tiled=True).reshape(owners, *block)
 
@@ -355,9 +379,9 @@
         functools.partial(solve_first, rows, owners),
         "solve_0",
         (piece_shape, spread_shape),
-        (vmem(), vmem()),
+        (vmem(), anywhere()),
         [smem(), vmem(), anywhere(), anywhere()],
-        [pltpu.VMEM((MEMBERS, *tile), jnp.bfloat16), pltpu.SemaphoreType.DMA((MEMBERS,))],
+        [pltpu.VMEM((MEMBERS, *tile), jnp.bfloat16), pltpu.SemaphoreType.DMA((MEMBERS,)), *fan],
         (levels, held, *inverses),
         4 << 20,
         1 << 18,
@@ -419,12 +443,12 @@
             functools.partial(solve_level, level, width_k, owners),
             out_shape=(piece_shape,) if last else (piece_shape, spread_shape, store_shape),
             in_specs=[smem()] * 3 + [vmem()] * 3 + [anywhere()] * (MEMBERS + len(held_store)),
-            out_specs=(vmem(),) if last else (vmem(), vmem(), anywhere()),
+            out_specs=(vmem(),) if last else (vmem(), anywhere(), anywhere()),
             scratch_shapes=[
                 pltpu.VMEM((extra, *tile), jnp.bfloat16),
                 pltpu.SemaphoreType.DMA((extra,)),
             ]
-            + ([] if last else [pltpu.SemaphoreType.DMA((1,))]),
+            + ([] if last else [pltpu.SemaphoreType.DMA((1,)), *fan]),
             input_output_aliases={len(operands) - 1: 2} if held_store else {},
             compiler_params=pltpu.CompilerParams(vmem_limit_bytes=GRANT),
             cost_estimate=pl.CostEstimate(

time: 371 us -> 367 us (0.989)
  Pallas kernels: 108 us -> 93.7 us
  waiting for transfers between devices: 154 us -> 167 us
    all_to_all x15, waiting for transfers between devices: 151 us -> 163 us  [exchanged(): lax.all_to_all(spread, CHIPS, 0, 0, tiled=True).reshape(owners, *block)]
    pallas_call x19, Pallas kernels: 68.1 us -> 57.8 us  [call(): pl.pallas_call(kernel, out_shape=out_shape, in_specs=in_specs, out_specs=...]
    pallas_call x15, Pallas kernels: 39.6 us -> 35.9 us  [solve(): pl.pallas_call(functools.partial(solve_level, level, width_k, owners), ou...]
  transfers between devices with their start and end apart: 21 -> 21, of which waited for: 18 -> 18; matrix products, arithmetic and copies ran while one was open for 1% -> 1% of each run, Pallas kernels for 18% -> 15%
where the time goes in v5:
time: 367 us; the launch traced here: 364 us
  waiting for transfers between devices  167 us (46%)
  starting transfers between devices  96.9 us (26%)
  Pallas kernels  93.7 us (26%)
  local copies, waits for them, and re-layouts  4.34 us (1%)
    all_to_all x15, waiting for transfers between devices, exchanged(): lax.all_to_all(spread, CHIPS, 0, 0, tiled=True).reshape(owners, *block)  163 us
    all_to_all x15, starting transfers between devices, exchanged(): lax.all_to_all(spread, CHIPS, 0, 0, tiled=True).reshape(owners, *block)  79.3 us
    pallas_call x19, Pallas kernels, call(): pl.pallas_call(kernel, out_shape=out_shape, in_specs=in_specs, out_specs=...  57.8 us
    pallas_call x15, Pallas kernels, solve(): pl.pallas_call(functools.partial(solve_level, level, width_k, owners), ou...  35.9 us
    ppermute x6, starting transfers between devices, swapped(): return lax.ppermute(value, CORE, SWAP)  17.7 us
  transfers between devices with their start and end apart: 21, of which 18 were waited for; matrix products, arithmetic and copies ran while one was open for 1% of the time, Pallas kernels for 15%

profile of v5, /device:TPU:1, one launch (start us, length us, event | category | flops | bytes accessed | tf_op | source)
XLA Modules:
  0.0 364.1 jit_solution(14480550585541583533)
XLA Ops:
  7.8 11.2 %all-to-all-start = ((bf16[64,2,32,128]{3,2,1,0:T(8,128)(2,1)}), bf16[64,2,32,128]{3,2,1,0:T(8,128)(2,1)S(1)}, u32[]{:S(2)}, u32[]{:S(2)}) async-start(bf16[64,2,32,128]{3,2,1,0:T(8,128)(2,1)} %get-tuple-element.126), calls=%async_computation | async-start | bytes 2097152 | tf_op jit(solution)/shard_map/all_to_all | solution.py:376
  22.9 5.8 %list_edges.1 = (s32[256]{0:T(256)S(1)}, s32[65]{0:T(128)S(1)}) custom-call(s32[256]{0:T(256)S(1)} %reshape.60.columns, s32[16]{0:T(128)S(1)} %pad_add_fusion.1.counts, s32[1024]{0:T(1024)S(1)} %bitcast.67), custom_call_target="tpu_custom_call" | custom-call | flops 8388608 | bytes 1048576 | tf_op jit(solution)/shard_map/list_edges/pallas_call | solution.py:354
  32.1 5.0 %all-to-all-done = bf16[64,2,32,128]{3,2,1,0:T(8,128)(2,1)S(1)} async-done(((bf16[64,2,32,128]{3,2,1,0:T(8,128)(2,1)}), bf16[64,2,32,128]{3,2,1,0:T(8,128)(2,1)S(1)}, u32[]{:S(2)}, u32[]{:S(2)}) %all-to-all-start) | async-done | bytes 1048608 | tf_op jit(solution)/shard_map/all_to_all | solution.py:376
  37.1 3.9 %solve_1.1 = (bf16[2,32,128]{2,1,0:T(8,128)(2,1)S(1)}, bf16[64,2,32,128]{3,2,1,0:T(8,128)(2,1)}, bf16[14,128,32,128]{3,2,1,0:T(8,128)(2,1)}) custom-call(s32[256]{0:T(256)S(1)} %get-tuple-element.120.edges, s32[65]{0:T(128)S(1)} %get-tuple-element.121.starts, s32[2]{0:T(128)S(1)} %get-tuple-element.123.info, f32[2,32,128]{2,1,0:T(8,128)S(1)} %get-tuple-element.124.totals, ...), custom_call_target="tpu_custom_call" | custom-call | flops 4194304 | bytes 262144 | tf_op jit(solution)/shard_map/solve_1/pallas_call | solution.py:442
  41.0 6.1 %all-to-all-start.1 = ((bf16[64,2,32,128]{3,2,1,0:T(8,128)(2,1)}), bf16[64,2,32,128]{3,2,1,0:T(8,128)(2,1)S(1)}, u32[]{:S(2)}, u32[]{:S(2)}) async-start(bf16[64,2,32,128]{3,2,1,0:T(8,128)(2,1)} %get-tuple-element.133), calls=%async_computation.1 | async-start | bytes 2097152 | tf_op jit(solution)/shard_map/all_to_all | solution.py:376
  47.2 5.2 %prepare_1.1 = (f32[16,32,128]{2,1,0:T(8,128)S(1)}, f32[2,32,128]{2,1,0:T(8,128)S(1)}, bf16[2,7,128,128]{3,2,1,0:T(8,128)(2,1)S(1)}, s32[2]{0:T(128)S(1)}) custom-call(s32[1024]{0:T(1024)S(1)} %bitcast.69, s32[256]{0:T(256)S(1)} %get-tuple-element.120.edges, s32[65]{0:T(128)S(1)} %get-tuple-element.121.starts, ...), custom_call_target="tpu_custom_call" | custom-call | flops 33554432 | bytes 1048576 | tf_op jit(solution)/shard_map/prepare_1/pallas_call | solution.py:354
  52.4 12.9 %all-to-all-done.1 = bf16[64,2,32,128]{3,2,1,0:T(8,128)(2,1)S(1)} async-done(((bf16[64,2,32,128]{3,2,1,0:T(8,128)(2,1)}), bf16[64,2,32,128]{3,2,1,0:T(8,128)(2,1)S(1)}, u32[]{:S(2)}, u32[]{:S(2)}) %all-to-all-start.1) | async-done | bytes 1048608 | tf_op jit(solution)/shard_map/all_to_all | solution.py:376
  67.5 5.7 %all-to-all-start.2 = ((bf16[64,2,32,128]{3,2,1,0:T(8,128)(2,1)}), bf16[64,2,32,128]{3,2,1,0:T(8,128)(2,1)S(1)}, u32[]{:S(2)}, u32[]{:S(2)}) async-start(bf16[64,2,32,128]{3,2,1,0:T(8,128)(2,1)} %get-tuple-element.140), calls=%async_computation.2 | async-start | bytes 2097152 | tf_op jit(solution)/shard_map/all_to_all | solution.py:376
  73.2 4.6 %prepare_2.1 = (f32[16,32,128]{2,1,0:T(8,128)S(1)}, f32[2,32,128]{2,1,0:T(8,128)S(1)}, bf16[2,7,128,128]{3,2,1,0:T(8,128)(2,1)S(1)}, s32[2]{0:T(128)S(1)}) custom-call(s32[1024]{0:T(1024)S(1)} %bitcast.70, s32[256]{0:T(256)S(1)} %get-tuple-element.120.edges, s32[65]{0:T(128)S(1)} %get-tuple-element.121.starts, ...), custom_call_target="tpu_custom_call" | custom-call | flops 33554432 | bytes 1048576 | tf_op jit(solution)/shard_map/prepare_2/pallas_call | solution.py:354
  77.8 13.1 %all-to-all-done.2 = bf16[64,2,32,128]{3,2,1,0:T(8,128)(2,1)S(1)} async-done(((bf16[64,2,32,128]{3,2,1,0:T(8,128)(2,1)}), bf16[64,2,32,128]{3,2,1,0:T(8,128)(2,1)S(1)}, u32[]{:S(2)}, u32[]{:S(2)}) %all-to-all-start.2) | async-done | bytes 1048608 | tf_op jit(solution)/shard_map/all_to_all | solution.py:376
  90.9 2.8 solve_3.1
  93.7 4.7 %all-to-all-start.3 = ((bf16[64,2,32,128]{3,2,1,0:T(8,128)(2,1)}), bf16[64,2,32,128]{3,2,1,0:T(8,128)(2,1)S(1)}, u32[]{:S(2)}, u32[]{:S(2)}) async-start(bf16[64,2,32,128]{3,2,1,0:T(8,128)(2,1)} %get-tuple-element.147), calls=%async_computation.3 | async-start | bytes 2097152 | tf_op jit(solution)/shard_map/all_to_all | solution.py:376
  98.4 4.5 %prepare_3.1 = (f32[16,32,128]{2,1,0:T(8,128)S(1)}, f32[2,32,128]{2,1,0:T(8,128)S(1)}, bf16[2,7,128,128]{3,2,1,0:T(8,128)(2,1)S(1)}, s32[2]{0:T(128)S(1)}) custom-call(s32[1024]{0:T(1024)S(1)} %bitcast.71, s32[256]{0:T(256)S(1)} %get-tuple-element.120.edges, s32[65]{0:T(128)S(1)} %get-tuple-element.121.starts, ...), custom_call_target="tpu_custom_call" | custom-call | flops 33554432 | bytes 1048576 | tf_op jit(solution)/shard_map/prepare_3/pallas_call | solution.py:354
  102.9 11.7 %all-to-all-done.3 = bf16[64,2,32,128]{3,2,1,0:T(8,128)(2,1)S(1)} async-done(((bf16[64,2,32,128]{3,2,1,0:T(8,128)(2,1)}), bf16[64,2,32,128]{3,2,1,0:T(8,128)(2,1)S(1)}, u32[]{:S(2)}, u32[]{:S(2)}) %all-to-all-start.3) | async-done | bytes 1048608 | tf_op jit(solution)/shard_map/all_to_all | solution.py:376
  114.6 2.8 solve_4.1
  117.4 4.7 %all-to-all-start.4 = ((bf16[64,2,32,128]{3,2,1,0:T(8,128)(2,1)}), bf16[64,2,32,128]{3,2,1,0:T(8,128)(2,1)S(1)}, u32[]{:S(2)}, u32[]{:S(2)}) async-start(bf16[64,2,32,128]{3,2,1,0:T(8,128)(2,1)} %get-tuple-element.154), calls=%async_computation.4 | async-start | bytes 2097152 | tf_op jit(solution)/shard_map/all_to_all | solution.py:376
  122.1 4.3 %prepare_4.1 = (f32[16,32,128]{2,1,0:T(8,128)S(1)}, f32[2,32,128]{2,1,0:T(8,128)S(1)}, bf16[2,7,128,128]{3,2,1,0:T(8,128)(2,1)S(1)}, s32[2]{0:T(128)S(1)}) custom-call(s32[1024]{0:T(1024)S(1)} %bitcast.72, s32[256]{0:T(256)S(1)} %get-tuple-element.120.edges, s32[65]{0:T(128)S(1)} %get-tuple-element.121.starts, ...), custom_call_target="tpu_custom_call" | custom-call | flops 33554432 | bytes 1048576 | tf_op jit(solution)/shard_map/prepare_4/pallas_call | solution.py:354
  126.4 11.2 %all-to-all-done.4 = bf16[64,2,32,128]{3,2,1,0:T(8,128)(2,1)S(1)} async-done(((bf16[64,2,32,128]{3,2,1,0:T(8,128)(2,1)}), bf16[64,2,32,128]{3,2,1,0:T(8,128)(2,1)S(1)}, u32[]{:S(2)}, u32[]{:S(2)}) %all-to-all-start.4) | async-done | bytes 1048608 | tf_op jit(solution)/shard_map/all_to_all | solution.py:376
  137.6 2.5 solve_5.1
  140.1 4.7 %all-to-all-start.5 = ((bf16[64,2,32,128]{3,2,1,0:T(8,128)(2,1)}), bf16[64,2,32,128]{3,2,1,0:T(8,128)(2,1)S(1)}, u32[]{:S(2)}, u32[]{:S(2)}) async-start(bf16[64,2,32,128]{3,2,1,0:T(8,128)(2,1)} %get-tuple-element.161), calls=%async_computation.5 | async-start | bytes 2097152 | tf_op jit(solution)/shard_map/all_to_all | solution.py:376
  144.8 3.7 %prepare_5.1 = (f32[16,32,128]{2,1,0:T(8,128)S(1)}, f32[2,32,128]{2,1,0:T(8,128)S(1)}, bf16[2,7,128,128]{3,2,1,0:T(8,128)(2,1)S(1)}, s32[2]{0:T(128)S(1)}) custom-call(s32[1024]{0:T(1024)S(1)} %bitcast.73, s32[256]{0:T(256)S(1)} %get-tuple-element.120.edges, s32[65]{0:T(128)S(1)} %get-tuple-element.121.starts, ...), custom_call_target="tpu_custom_call" | custom-call | flops 33554432 | bytes 1048576 | tf_op jit(solution)/shard_map/prepare_5/pallas_call | solution.py:354
  148.5 11.0 %all-to-all-done.5 = bf16[64,2,32,128]{3,2,1,0:T(8,128)(2,1)S(1)} async-done(((bf16[64,2,32,128]{3,2,1,0:T(8,128)(2,1)}), bf16[64,2,32,128]{3,2,1,0:T(8,128)(2,1)S(1)}, u32[]{:S(2)}, u32[]{:S(2)}) %all-to-all-start.5) | async-done | bytes 1048608 | tf_op jit(solution)/shard_map/all_to_all | solution.py:376
  161.8 4.8 %all-to-all-start.6 = ((bf16[64,2,32,128]{3,2,1,0:T(8,128)(2,1)}), bf16[64,2,32,128]{3,2,1,0:T(8,128)(2,1)S(1)}, u32[]{:S(2)}, u32[]{:S(2)}) async-start(bf16[64,2,32,128]{3,2,1,0:T(8,128)(2,1)} %get-tuple-element.168), calls=%async_computation.6 | async-start | bytes 2097152 | tf_op jit(solution)/shard_map/all_to_all | solution.py:376
  166.7 3.4 prepare_6.1
  170.1 10.7 %all-to-all-done.6 = bf16[64,2,32,128]{3,2,1,0:T(8,128)(2,1)S(1)} async-done(((bf16[64,2,32,128]{3,2,1,0:T(8,128)(2,1)}), bf16[64,2,32,128]{3,2,1,0:T(8,128)(2,1)S(1)}, u32[]{:S(2)}, u32[]{:S(2)}) %all-to-all-start.6) | async-done | bytes 1048608 | tf_op jit(solution)/shard_map/all_to_all | solution.py:376
  183.0 4.7 %all-to-all-start.7 = ((bf16[64,2,32,128]{3,2,1,0:T(8,128)(2,1)}), bf16[64,2,32,128]{3,2,1,0:T(8,128)(2,1)S(1)}, u32[]{:S(2)}, u32[]{:S(2)}) async-start(bf16[64,2,32,128]{3,2,1,0:T(8,128)(2,1)} %get-tuple-element.175), calls=%async_computation.7 | async-start | bytes 2097152 | tf_op jit(solution)/shard_map/all_to_all | solution.py:376
  187.7 3.0 prepare_7.1
  190.8 10.8 %all-to-all-done.7 = bf16[64,2,32,128]{3,2,1,0:T(8,128)(2,1)S(1)} async-done(((bf16[64,2,32,128]{3,2,1,0:T(8,128)(2,1)}), bf16[64,2,32,128]{3,2,1,0:T(8,128)(2,1)S(1)}, u32[]{:S(2)}, u32[]{:S(2)}) %all-to-all-start.7) | async-done | bytes 1048608 | tf_op jit(solution)/shard_map/all_to_all | solution.py:376
  203.9 4.7 %all-to-all-start.8 = ((bf16[64,2,32,128]{3,2,1,0:T(8,128)(2,1)}), bf16[64,2,32,128]{3,2,1,0:T(8,128)(2,1)S(1)}, u32[]{:S(2)}, u32[]{:S(2)}) async-start(bf16[64,2,32,128]{3,2,1,0:T(8,128)(2,1)} %get-tuple-element.182), calls=%async_computation.8 | async-start | bytes 2097152 | tf_op jit(solution)/shard_map/all_to_all | solution.py:376
  208.6 3.4 prepare_8.1
  212.0 10.4 %all-to-all-done.8 = bf16[64,2,32,128]{3,2,1,0:T(8,128)(2,1)S(1)} async-done(((bf16[64,2,32,128]{3,2,1,0:T(8,128)(2,1)}), bf16[64,2,32,128]{3,2,1,0:T(8,128)(2,1)S(1)}, u32[]{:S(2)}, u32[]{:S(2)}) %all-to-all-start.8) | async-done | bytes 1048608 | tf_op jit(solution)/shard_map/all_to_all | solution.py:376
  224.7 4.7 %all-to-all-start.9 = ((bf16[64,2,32,128]{3,2,1,0:T(8,128)(2,1)}), bf16[64,2,32,128]{3,2,1,0:T(8,128)(2,1)S(1)}, u32[]{:S(2)}, u32[]{:S(2)}) async-start(bf16[64,2,32,128]{3,2,1,0:T(8,128)(2,1)} %get-tuple-element.189), calls=%async_computation.9 | async-start | bytes 2097152 | tf_op jit(solution)/shard_map/all_to_all | solution.py:376
  229.4 3.2 prepare_9.1
  232.5 10.5 %all-to-all-done.9 = bf16[64,2,32,128]{3,2,1,0:T(8,128)(2,1)S(1)} async-done(((bf16[64,2,32,128]{3,2,1,0:T(8,128)(2,1)}), bf16[64,2,32,128]{3,2,1,0:T(8,128)(2,1)S(1)}, u32[]{:S(2)}, u32[]{:S(2)}) %all-to-all-start.9) | async-done | bytes 1048608 | tf_op jit(solution)/shard_map/all_to_all | solution.py:376
  243.0 2.5 solve_10.1
  245.5 4.7 %all-to-all-start.10 = ((bf16[64,2,32,128]{3,2,1,0:T(8,128)(2,1)}), bf16[64,2,32,128]{3,2,1,0:T(8,128)(2,1)S(1)}, u32[]{:S(2)}, u32[]{:S(2)}) async-start(bf16[64,2,32,128]{3,2,1,0:T(8,128)(2,1)} %get-tuple-element.196), calls=%async_computation.10 | async-start | bytes 2097152 | tf_op jit(solution)/shard_map/all_to_all | solution.py:376
  250.2 2.9 prepare_10.1
  253.1 10.7 %all-to-all-done.10 = bf16[64,2,32,128]{3,2,1,0:T(8,128)(2,1)S(1)} async-done(((bf16[64,2,32,128]{3,2,1,0:T(8,128)(2,1)}), bf16[64,2,32,128]{3,2,1,0:T(8,128)(2,1)S(1)}, u32[]{:S(2)}, u32[]{:S(2)}) %all-to-all-start.10) | async-done | bytes 1048608 | tf_op jit(solution)/shard_map/all_to_all | solution.py:376
  266.0 4.7 %all-to-all-start.11 = ((bf16[64,2,32,128]{3,2,1,0:T(8,128)(2,1)}), bf16[64,2,32,128]{3,2,1,0:T(8,128)(2,1)S(1)}, u32[]{:S(2)}, u32[]{:S(2)}) async-start(bf16[64,2,32,128]{3,2,1,0:T(8,128)(2,1)} %get-tuple-element.203), calls=%async_computation.11 | async-start | bytes 2097152 | tf_op jit(solution)/shard_map/all_to_all | solution.py:376
  273.1 11.1 %all-to-all-done.11 = bf16[64,2,32,128]{3,2,1,0:T(8,128)(2,1)S(1)} async-done(((bf16[64,2,32,128]{3,2,1,0:T(8,128)(2,1)}), bf16[64,2,32,128]{3,2,1,0:T(8,128)(2,1)S(1)}, u32[]{:S(2)}, u32[]{:S(2)}) %all-to-all-start.11) | async-done | bytes 1048608 | tf_op jit(solution)/shard_map/all_to_all | solution.py:376
  284.2 2.5 solve_12.1
  286.7 4.7 %all-to-all-start.12 = ((bf16[64,2,32,128]{3,2,1,0:T(8,128)(2,1)}), bf16[64,2,32,128]{3,2,1,0:T(8,128)(2,1)S(1)}, u32[]{:S(2)}, u32[]{:S(2)}) async-start(bf16[64,2,32,128]{3,2,1,0:T(8,128)(2,1)} %get-tuple-element.210), calls=%async_computation.12 | async-start | bytes 2097152 | tf_op jit(solution)/shard_map/all_to_all | solution.py:376
  293.0 11.8 %all-to-all-done.12 = bf16[64,2,32,128]{3,2,1,0:T(8,128)(2,1)S(1)} async-done(((bf16[64,2,32,128]{3,2,1,0:T(8,128)(2,1)}), bf16[64,2,32,128]{3,2,1,0:T(8,128)(2,1)S(1)}, u32[]{:S(2)}, u32[]{:S(2)}) %all-to-all-start.12) | async-done | bytes 1048608 | tf_op jit(solution)/shard_map/all_to_all | solution.py:376
  307.1 4.8 %all-to-all-start.13 = ((bf16[64,2,32,128]{3,2,1,0:T(8,128)(2,1)}), bf16[64,2,32,128]{3,2,1,0:T(8,128)(2,1)S(1)}, u32[]{:S(2)}, u32[]{:S(2)}) async-start(bf16[64,2,32,128]{3,2,1,0:T(8,128)(2,1)} %get-tuple-element.217), calls=%async_computation.13 | async-start | bytes 2097152 | tf_op jit(solution)/shard_map/all_to_all | solution.py:376
  313.6 11.8 %all-to-all-done.13 = bf16[64,2,32,128]{3,2,1,0:T(8,128)(2,1)S(1)} async-done(((bf16[64,2,32,128]{3,2,1,0:T(8,128)(2,1)}), bf16[64,2,32,128]{3,2,1,0:T(8,128)(2,1)S(1)}, u32[]{:S(2)}, u32[]{:S(2)}) %all-to-all-start.13) | async-done | bytes 1048608 | tf_op jit(solution)/shard_map/all_to_all | solution.py:376
  327.7 4.7 %all-to-all-start.14 = ((bf16[64,2,32,128]{3,2,1,0:T(8,128)(2,1)}), bf16[64,2,32,128]{3,2,1,0:T(8,128)(2,1)S(1)}, u32[]{:S(2)}, u32[]{:S(2)}) async-start(bf16[64,2,32,128]{3,2,1,0:T(8,128)(2,1)} %get-tuple-element.226), calls=%async_computation.14 | async-start | bytes 2097152 | tf_op jit(solution)/shard_map/all_to_all | solution.py:376
  335.3 10.6 %all-to-all-done.14 = bf16[64,2,32,128]{3,2,1,0:T(8,128)(2,1)S(1)} async-done(((bf16[64,2,32,128]{3,2,1,0:T(8,128)(2,1)}), bf16[64,2,32,128]{3,2,1,0:T(8,128)(2,1)S(1)}, u32[]{:S(2)}, u32[]{:S(2)}) %all-to-all-start.14) | async-done | bytes 1048608 | tf_op jit(solution)/shard_map/all_to_all | solution.py:376
  347.4 15.1 %collective-permute-start.5 = (bf16[8,32,128]{2,1,0:T(8,128)(2,1)S(1)}, bf16[8,32,128]{2,1,0:T(8,128)(2,1)S(1)}, u32[]{:S(2)}, u32[]{:S(2)}) collective-permute-start(bf16[8,32,128]{2,1,0:T(8,128)(2,1)S(1)} %get-tuple-element.228), channel_id=1, source_target_pairs={{0,1},{1,0},{2,3},{3,2},{4,5},{5,4},{6,7},{7,6},{8,9},{9,8},{10,11... | collective-permute-start | bytes 196616 | tf_op jit(solution)/shard_map/ppermute | solution.py:344
  (46 shorter events, 44.8 us)
Async XLA Ops:
  0.0 47.2 %copy-start.2 = (bf16[8,1,128,128]{3,2,1,0:T(8,128)(2,1)S(1)}, bf16[8,1,128,128]{3,2,1,0:T(8,128)(2,1)}, u32[]{:S(2)}) copy-start(bf16[8,1,128,128]{3,2,1,0:T(8,128)(2,1)} %param.8) | copy-start | bytes 786436
  0.0 47.2 %copy-start.5 = (s32[8,128]{1,0:T(8,128)S(1)}, s32[8,128]{1,0:T(8,128)}, u32[]{:S(2)}) copy-start(s32[8,128]{1,0:T(8,128)} %param.11) | copy-start | bytes 12292
  0.0 3.8 %collective-permute-start.1 = (bf16[8,128,128]{2,1,0:T(8,128)(2,1)}, bf16[8,128,128]{2,1,0:T(8,128)(2,1)S(1)}, u32[]{:S(2)}, u32[]{:S(2)}) collective-permute-start(bf16[8,128,128]{2,1,0:T(8,128)(2,1)} %bitcast.34), channel_id=1, source_target_pairs={{0,1},{1,0},{2,3},{3,2},{4,5},{5,4},{6,7},{7,6},{8,9},{9,8},{10,11... | collective-permute-start | bytes 786440 | tf_op jit(solution)/shard_map/ppermute | solution.py:344
  2.4 1.4 collective-permute-start
  3.8 1.0 copy-start
  4.8 0.7 copy-start.3
  7.5 21.2 %collective-permute-start.4 = (bf16[8,16,128,128]{3,2,1,0:T(8,128)(2,1)}, bf16[8,16,128,128]{3,2,1,0:T(8,128)(2,1)}, u32[]{:S(2)}, u32[]{:S(2)}) collective-permute-start(bf16[8,16,128,128]{3,2,1,0:T(8,128)(2,1)} %bitcast.85), channel_id=1, source_target_pairs={{0,1},{1,0},{2,3},{3,2},{4,5},{5,4},{6,7},{7,6},{8,9},{9,8},{10,11... | collective-permute-start | bytes 12582920 | tf_op jit(solution)/shard_map/ppermute | solution.py:344
  7.8 29.3 %all-to-all-start = ((bf16[64,2,32,128]{3,2,1,0:T(8,128)(2,1)}), bf16[64,2,32,128]{3,2,1,0:T(8,128)(2,1)S(1)}, u32[]{:S(2)}, u32[]{:S(2)}) async-start(bf16[64,2,32,128]{3,2,1,0:T(8,128)(2,1)} %get-tuple-element.126), calls=%async_computation | async-start | bytes 2097152 | tf_op jit(solution)/shard_map/all_to_all | solution.py:376
  19.0 1.7 collective-permute-start.3
  19.7 1.7 collective-permute-start.2
  22.2 0.7 copy-start.4
  28.7 1.0 copy-start.1
  41.0 24.2 %all-to-all-start.1 = ((bf16[64,2,32,128]{3,2,1,0:T(8,128)(2,1)}), bf16[64,2,32,128]{3,2,1,0:T(8,128)(2,1)S(1)}, u32[]{:S(2)}, u32[]{:S(2)}) async-start(bf16[64,2,32,128]{3,2,1,0:T(8,128)(2,1)} %get-tuple-element.133), calls=%async_computation.1 | async-start | bytes 2097152 | tf_op jit(solution)/shard_map/all_to_all | solution.py:376
  67.5 23.4 %all-to-all-start.2 = ((bf16[64,2,32,128]{3,2,1,0:T(8,128)(2,1)}), bf16[64,2,32,128]{3,2,1,0:T(8,128)(2,1)S(1)}, u32[]{:S(2)}, u32[]{:S(2)}) async-start(bf16[64,2,32,128]{3,2,1,0:T(8,128)(2,1)} %get-tuple-element.140), calls=%async_computation.2 | async-start | bytes 2097152 | tf_op jit(solution)/shard_map/all_to_all | solution.py:376
  93.7 20.8 %all-to-all-start.3 = ((bf16[64,2,32,128]{3,2,1,0:T(8,128)(2,1)}), bf16[64,2,32,128]{3,2,1,0:T(8,128)(2,1)S(1)}, u32[]{:S(2)}, u32[]{:S(2)}) async-start(bf16[64,2,32,128]{3,2,1,0:T(8,128)(2,1)} %get-tuple-element.147), calls=%async_computation.3 | async-start | bytes 2097152 | tf_op jit(solution)/shard_map/all_to_all | solution.py:376
  117.4 20.2 %all-to-all-start.4 = ((bf16[64,2,32,128]{3,2,1,0:T(8,128)(2,1)}), bf16[64,2,32,128]{3,2,1,0:T(8,128)(2,1)S(1)}, u32[]{:S(2)}, u32[]{:S(2)}) async-start(bf16[64,2,32,128]{3,2,1,0:T(8,128)(2,1)} %get-tuple-element.154), calls=%async_computation.4 | async-start | bytes 2097152 | tf_op jit(solution)/shard_map/all_to_all | solution.py:376
  140.1 19.4 %all-to-all-start.5 = ((bf16[64,2,32,128]{3,2,1,0:T(8,128)(2,1)}), bf16[64,2,32,128]{3,2,1,0:T(8,128)(2,1)S(1)}, u32[]{:S(2)}, u32[]{:S(2)}) async-start(bf16[64,2,32,128]{3,2,1,0:T(8,128)(2,1)} %get-tuple-element.161), calls=%async_computation.5 | async-start | bytes 2097152 | tf_op jit(solution)/shard_map/all_to_all | solution.py:376
  161.8 18.9 %all-to-all-start.6 = ((bf16[64,2,32,128]{3,2,1,0:T(8,128)(2,1)}), bf16[64,2,32,128]{3,2,1,0:T(8,128)(2,1)S(1)}, u32[]{:S(2)}, u32[]{:S(2)}) async-start(bf16[64,2,32,128]{3,2,1,0:T(8,128)(2,1)} %get-tuple-element.168), calls=%async_computation.6 | async-start | bytes 2097152 | tf_op jit(solution)/shard_map/all_to_all | solution.py:376
  183.0 18.5 %all-to-all-start.7 = ((bf16[64,2,32,128]{3,2,1,0:T(8,128)(2,1)}), bf16[64,2,32,128]{3,2,1,0:T(8,128)(2,1)S(1)}, u32[]{:S(2)}, u32[]{:S(2)}) async-start(bf16[64,2,32,128]{3,2,1,0:T(8,128)(2,1)} %get-tuple-element.175), calls=%async_computation.7 | async-start | bytes 2097152 | tf_op jit(solution)/shard_map/all_to_all | solution.py:376
  203.9 18.4 %all-to-all-start.8 = ((bf16[64,2,32,128]{3,2,1,0:T(8,128)(2,1)}), bf16[64,2,32,128]{3,2,1,0:T(8,128)(2,1)S(1)}, u32[]{:S(2)}, u32[]{:S(2)}) async-start(bf16[64,2,32,128]{3,2,1,0:T(8,128)(2,1)} %get-tuple-element.182), calls=%async_computation.8 | async-start | bytes 2097152 | tf_op jit(solution)/shard_map/all_to_all | solution.py:376
  224.7 18.3 %all-to-all-start.9 = ((bf16[64,2,32,128]{3,2,1,0:T(8,128)(2,1)}), bf16[64,2,32,128]{3,2,1,0:T(8,128)(2,1)S(1)}, u32[]{:S(2)}, u32[]{:S(2)}) async-start(bf16[64,2,32,128]{3,2,1,0:T(8,128)(2,1)} %get-tuple-element.189), calls=%async_computation.9 | async-start | bytes 2097152 | tf_op jit(solution)/shard_map/all_to_all | solution.py:376
  245.5 18.3 %all-to-all-start.10 = ((bf16[64,2,32,128]{3,2,1,0:T(8,128)(2,1)}), bf16[64,2,32,128]{3,2,1,0:T(8,128)(2,1)S(1)}, u32[]{:S(2)}, u32[]{:S(2)}) async-start(bf16[64,2,32,128]{3,2,1,0:T(8,128)(2,1)} %get-tuple-element.196), calls=%async_computation.10 | async-start | bytes 2097152 | tf_op jit(solution)/shard_map/all_to_all | solution.py:376
  266.0 18.2 %all-to-all-start.11 = ((bf16[64,2,32,128]{3,2,1,0:T(8,128)(2,1)}), bf16[64,2,32,128]{3,2,1,0:T(8,128)(2,1)S(1)}, u32[]{:S(2)}, u32[]{:S(2)}) async-start(bf16[64,2,32,128]{3,2,1,0:T(8,128)(2,1)} %get-tuple-element.203), calls=%async_computation.11 | async-start | bytes 2097152 | tf_op jit(solution)/shard_map/all_to_all | solution.py:376
  286.7 18.2 %all-to-all-start.12 = ((bf16[64,2,32,128]{3,2,1,0:T(8,128)(2,1)}), bf16[64,2,32,128]{3,2,1,0:T(8,128)(2,1)S(1)}, u32[]{:S(2)}, u32[]{:S(2)}) async-start(bf16[64,2,32,128]{3,2,1,0:T(8,128)(2,1)} %get-tuple-element.210), calls=%async_computation.12 | async-start | bytes 2097152 | tf_op jit(solution)/shard_map/all_to_all | solution.py:376
  307.1 18.3 %all-to-all-start.13 = ((bf16[64,2,32,128]{3,2,1,0:T(8,128)(2,1)}), bf16[64,2,32,128]{3,2,1,0:T(8,128)(2,1)S(1)}, u32[]{:S(2)}, u32[]{:S(2)}) async-start(bf16[64,2,32,128]{3,2,1,0:T(8,128)(2,1)} %get-tuple-element.217), calls=%async_computation.13 | async-start | bytes 2097152 | tf_op jit(solution)/shard_map/all_to_all | solution.py:376
  327.7 18.2 %all-to-all-start.14 = ((bf16[64,2,32,128]{3,2,1,0:T(8,128)(2,1)}), bf16[64,2,32,128]{3,2,1,0:T(8,128)(2,1)S(1)}, u32[]{:S(2)}, u32[]{:S(2)}) async-start(bf16[64,2,32,128]{3,2,1,0:T(8,128)(2,1)} %get-tuple-element.226), calls=%async_computation.14 | async-start | bytes 2097152 | tf_op jit(solution)/shard_map/all_to_all | solution.py:376
  347.4 16.0 %collective-permute-start.5 = (bf16[8,32,128]{2,1,0:T(8,128)(2,1)S(1)}, bf16[8,32,128]{2,1,0:T(8,128)(2,1)S(1)}, u32[]{:S(2)}, u32[]{:S(2)}) collective-permute-start(bf16[8,32,128]{2,1,0:T(8,128)(2,1)S(1)} %get-tuple-element.228), channel_id=1, source_target_pairs={{0,1},{1,0},{2,3},{3,2},{4,5},{5,4},{6,7},{7,6},{8,9},{9,8},{10,11... | collective-permute-start | bytes 196616 | tf_op jit(solution)/shard_map/ppermute | solution.py:344

commit v6 on v5

--- a/solution.py
+++ b/solution.py
@@ -17,6 +17,7 @@
 KEYS = LEVELS * 2 * MEMBERS
 RING = 8
 FAN = 8
+KEPT = 16
 GROUP = 3
 READY = 6
 GRANT = 50 << 20
@@ -174,8 +175,9 @@
 
     def block_copy(first, i):
         at = lax.rem(i, RING)
-        place = lax.rem(edges[first + i], owners)
-        return pltpu.make_async_copy(store.at[level - 1, place], blocks.at[at], block_sems.at[at])
+        return pltpu.make_async_copy(
+            store.at[(level - 1) // 2, first + i], blocks.at[at], block_sems.at[at]
+        )
 
     late = []
     if level:
@@ -253,8 +255,14 @@
         piece, buf, sems = refs
     else:
         piece, spread, store, buf, sems, keep_sem, *fan = refs[1 if level > 1 else 0 :]
-        keep = pltpu.make_async_copy(received, store.at[level - 1], keep_sem.at[0])
-        keep.start()
+
+        def keep_copy(edge):
+            return pltpu.make_async_copy(
+                received.at[lax.rem(edges[edge], owners)],
+                store.at[(level - 1) // 2, edge],
+                keep_sem.at[lax.rem(edge, KEPT)],
+            )
+
     copies = []
     extra = width_k - READY
 
@@ -310,7 +318,23 @@
             copies += spread_slot(member, piece, spread, *fan)
 
     if not last:
-        keep.wait()
+        first_kept = starts[bucket(level - 1, False, 0)]
+        end_kept = starts[bucket(level - 1, False, MEMBERS - 1) + 1]
+
+        def keep(edge, unused):
+            @pl.when(edge - KEPT >= first_kept)
+            def _():
+                keep_copy(edge - KEPT).wait()
+
+            keep_copy(edge).start()
+            return unused
+
+        def kept(edge, unused):
+            keep_copy(edge).wait()
+            return unused
+
+        lax.fori_loop(first_kept, end_kept, keep, 0)
+        lax.fori_loop(jnp.maximum(first_kept, end_kept - KEPT), end_kept, kept, 0)
         for copy in copies:
             copy.wait()
 
@@ -365,7 +389,9 @@
     piece_shape = jax.ShapeDtypeStruct((MEMBERS, *block), jnp.bfloat16)
     spread_shape = jax.ShapeDtypeStruct((chips, MEMBERS, *block), jnp.bfloat16)
 
-    store_shape = jax.ShapeDtypeStruct((LEVELS - 2, owners, *block), jnp.bfloat16)
+    store_shape = jax.ShapeDtypeStruct(
+        ((LEVELS - 1) // 2, MEMBERS * rows * width_k, *block), jnp.bfloat16
+    )
 
     fan = [
         pltpu.VMEM((MEMBERS, FAN, *block), jnp.bfloat16),
@@ -448,7 +474,7 @@
                 pltpu.VMEM((extra, *tile), jnp.bfloat16),
                 pltpu.SemaphoreType.DMA((extra,)),
             ]
-            + ([] if last else [pltpu.SemaphoreType.DMA((1,)), *fan]),
+            + ([] if last else [pltpu.SemaphoreType.DMA((KEPT,)), *fan]),
             input_output_aliases={len(operands) - 1: 2} if held_store else {},
             compiler_params=pltpu.CompilerParams(vmem_limit_bytes=GRANT),
             cost_estimate=pl.CostEstimate(

time: 367 us -> 367 us (level)
  waiting for transfers between devices: 167 us -> 158 us
  Pallas kernels: 93.7 us -> 99.5 us
    all_to_all x15, waiting for transfers between devices: 163 us -> 155 us  [exchanged(): lax.all_to_all(spread, CHIPS, 0, 0, tiled=True).reshape(owners, *block)]
  transfers between devices with their start and end apart: 21 -> 21, of which waited for: 18 -> 18; matrix products, arithmetic and copies ran while one was open for 1% -> 1% of each run, Pallas kernels for 15% -> 16%
where the time goes in v6:
time: 367 us; the launch traced here: 363 us
  waiting for transfers between devices  158 us (43%)
  Pallas kernels  99.5 us (27%)
  starting transfers between devices  98.5 us (27%)
  local copies, waits for them, and re-layouts  4.34 us (1%)
    all_to_all x15, waiting for transfers between devices, exchanged(): lax.all_to_all(spread, CHIPS, 0, 0, tiled=True).reshape(owners, *block)  155 us
    all_to_all x15, starting transfers between devices, exchanged(): lax.all_to_all(spread, CHIPS, 0, 0, tiled=True).reshape(owners, *block)  79.6 us
    pallas_call x19, Pallas kernels, call(): pl.pallas_call(kernel, out_shape=out_shape, in_specs=in_specs, out_specs=...  60.8 us
    pallas_call x15, Pallas kernels, solve(): pl.pallas_call(functools.partial(solve_level, level, width_k, owners), ou...  38.7 us
    ppermute x6, starting transfers between devices, swapped(): return lax.ppermute(value, CORE, SWAP)  19 us
  transfers between devices with their start and end apart: 21, of which 18 were waited for; matrix products, arithmetic and copies ran while one was open for 1% of the time, Pallas kernels for 16%

profile of v6, /device:TPU:1, one launch (start us, length us, event | category | flops | bytes accessed | tf_op | source)
XLA Modules:
  0.0 363.0 jit_solution(7677895443984722769)
XLA Ops:
  7.8 11.2 %all-to-all-start = ((bf16[64,2,32,128]{3,2,1,0:T(8,128)(2,1)}), bf16[64,2,32,128]{3,2,1,0:T(8,128)(2,1)S(1)}, u32[]{:S(2)}, u32[]{:S(2)}) async-start(bf16[64,2,32,128]{3,2,1,0:T(8,128)(2,1)} %get-tuple-element.126), calls=%async_computation | async-start | bytes 2097152 | tf_op jit(solution)/shard_map/all_to_all | solution.py:402
  22.9 6.3 %list_edges.1 = (s32[256]{0:T(256)S(1)}, s32[65]{0:T(128)S(1)}) custom-call(s32[256]{0:T(256)S(1)} %reshape.60.columns, s32[16]{0:T(128)S(1)} %pad_add_fusion.1.counts, s32[1024]{0:T(1024)S(1)} %bitcast.67), custom_call_target="tpu_custom_call" | custom-call | flops 8388608 | bytes 1048576 | tf_op jit(solution)/shard_map/list_edges/pallas_call | solution.py:378
  32.8 4.3 %all-to-all-done = bf16[64,2,32,128]{3,2,1,0:T(8,128)(2,1)S(1)} async-done(((bf16[64,2,32,128]{3,2,1,0:T(8,128)(2,1)}), bf16[64,2,32,128]{3,2,1,0:T(8,128)(2,1)S(1)}, u32[]{:S(2)}, u32[]{:S(2)}) %all-to-all-start) | async-done | bytes 1048608 | tf_op jit(solution)/shard_map/all_to_all | solution.py:402
  37.1 6.5 %solve_1.1 = (bf16[2,32,128]{2,1,0:T(8,128)(2,1)S(1)}, bf16[64,2,32,128]{3,2,1,0:T(8,128)(2,1)}, bf16[7,256,32,128]{3,2,1,0:T(8,128)(2,1)}) custom-call(s32[256]{0:T(256)S(1)} %get-tuple-element.120.edges, s32[65]{0:T(128)S(1)} %get-tuple-element.121.starts, s32[2]{0:T(128)S(1)} %get-tuple-element.123.info, f32[2,32,128]{2,1,0:T(8,128)S(1)} %get-tuple-element.124.totals, ...), custom_call_target="tpu_custom_call" | custom-call | flops 4194304 | bytes 262144 | tf_op jit(solution)/shard_map/solve_1/pallas_call | solution.py:468
  43.6 4.7 %all-to-all-start.1 = ((bf16[64,2,32,128]{3,2,1,0:T(8,128)(2,1)}), bf16[64,2,32,128]{3,2,1,0:T(8,128)(2,1)S(1)}, u32[]{:S(2)}, u32[]{:S(2)}) async-start(bf16[64,2,32,128]{3,2,1,0:T(8,128)(2,1)} %get-tuple-element.133), calls=%async_computation.1 | async-start | bytes 2097152 | tf_op jit(solution)/shard_map/all_to_all | solution.py:402
  48.3 5.8 %prepare_1.1 = (f32[16,32,128]{2,1,0:T(8,128)S(1)}, f32[2,32,128]{2,1,0:T(8,128)S(1)}, bf16[2,7,128,128]{3,2,1,0:T(8,128)(2,1)S(1)}, s32[2]{0:T(128)S(1)}) custom-call(s32[1024]{0:T(1024)S(1)} %bitcast.69, s32[256]{0:T(256)S(1)} %get-tuple-element.120.edges, s32[65]{0:T(128)S(1)} %get-tuple-element.121.starts, ...), custom_call_target="tpu_custom_call" | custom-call | flops 33554432 | bytes 1048576 | tf_op jit(solution)/shard_map/prepare_1/pallas_call | solution.py:378
  54.1 11.2 %all-to-all-done.1 = bf16[64,2,32,128]{3,2,1,0:T(8,128)(2,1)S(1)} async-done(((bf16[64,2,32,128]{3,2,1,0:T(8,128)(2,1)}), bf16[64,2,32,128]{3,2,1,0:T(8,128)(2,1)S(1)}, u32[]{:S(2)}, u32[]{:S(2)}) %all-to-all-start.1) | async-done | bytes 1048608 | tf_op jit(solution)/shard_map/all_to_all | solution.py:402
  65.3 3.2 solve_2.1
  68.4 5.2 %all-to-all-start.2 = ((bf16[64,2,32,128]{3,2,1,0:T(8,128)(2,1)}), bf16[64,2,32,128]{3,2,1,0:T(8,128)(2,1)S(1)}, u32[]{:S(2)}, u32[]{:S(2)}) async-start(bf16[64,2,32,128]{3,2,1,0:T(8,128)(2,1)} %get-tuple-element.140), calls=%async_computation.2 | async-start | bytes 2097152 | tf_op jit(solution)/shard_map/all_to_all | solution.py:402
  73.6 3.7 %prepare_2.1 = (f32[16,32,128]{2,1,0:T(8,128)S(1)}, f32[2,32,128]{2,1,0:T(8,128)S(1)}, bf16[2,7,128,128]{3,2,1,0:T(8,128)(2,1)S(1)}, s32[2]{0:T(128)S(1)}) custom-call(s32[1024]{0:T(1024)S(1)} %bitcast.70, s32[256]{0:T(256)S(1)} %get-tuple-element.120.edges, s32[65]{0:T(128)S(1)} %get-tuple-element.121.starts, ...), custom_call_target="tpu_custom_call" | custom-call | flops 33554432 | bytes 1048576 | tf_op jit(solution)/shard_map/prepare_2/pallas_call | solution.py:378
  77.3 12.2 %all-to-all-done.2 = bf16[64,2,32,128]{3,2,1,0:T(8,128)(2,1)S(1)} async-done(((bf16[64,2,32,128]{3,2,1,0:T(8,128)(2,1)}), bf16[64,2,32,128]{3,2,1,0:T(8,128)(2,1)S(1)}, u32[]{:S(2)}, u32[]{:S(2)}) %all-to-all-start.2) | async-done | bytes 1048608 | tf_op jit(solution)/shard_map/all_to_all | solution.py:402
  91.6 5.6 %all-to-all-start.3 = ((bf16[64,2,32,128]{3,2,1,0:T(8,128)(2,1)}), bf16[64,2,32,128]{3,2,1,0:T(8,128)(2,1)S(1)}, u32[]{:S(2)}, u32[]{:S(2)}) async-start(bf16[64,2,32,128]{3,2,1,0:T(8,128)(2,1)} %get-tuple-element.147), calls=%async_computation.3 | async-start | bytes 2097152 | tf_op jit(solution)/shard_map/all_to_all | solution.py:402
  97.2 3.7 %prepare_3.1 = (f32[16,32,128]{2,1,0:T(8,128)S(1)}, f32[2,32,128]{2,1,0:T(8,128)S(1)}, bf16[2,7,128,128]{3,2,1,0:T(8,128)(2,1)S(1)}, s32[2]{0:T(128)S(1)}) custom-call(s32[1024]{0:T(1024)S(1)} %bitcast.71, s32[256]{0:T(256)S(1)} %get-tuple-element.120.edges, s32[65]{0:T(128)S(1)} %get-tuple-element.121.starts, ...), custom_call_target="tpu_custom_call" | custom-call | flops 33554432 | bytes 1048576 | tf_op jit(solution)/shard_map/prepare_3/pallas_call | solution.py:378
  100.9 11.9 %all-to-all-done.3 = bf16[64,2,32,128]{3,2,1,0:T(8,128)(2,1)S(1)} async-done(((bf16[64,2,32,128]{3,2,1,0:T(8,128)(2,1)}), bf16[64,2,32,128]{3,2,1,0:T(8,128)(2,1)S(1)}, u32[]{:S(2)}, u32[]{:S(2)}) %all-to-all-start.3) | async-done | bytes 1048608 | tf_op jit(solution)/shard_map/all_to_all | solution.py:402
  114.9 5.1 %all-to-all-start.4 = ((bf16[64,2,32,128]{3,2,1,0:T(8,128)(2,1)}), bf16[64,2,32,128]{3,2,1,0:T(8,128)(2,1)S(1)}, u32[]{:S(2)}, u32[]{:S(2)}) async-start(bf16[64,2,32,128]{3,2,1,0:T(8,128)(2,1)} %get-tuple-element.154), calls=%async_computation.4 | async-start | bytes 2097152 | tf_op jit(solution)/shard_map/all_to_all | solution.py:402
  120.0 4.3 %prepare_4.1 = (f32[16,32,128]{2,1,0:T(8,128)S(1)}, f32[2,32,128]{2,1,0:T(8,128)S(1)}, bf16[2,7,128,128]{3,2,1,0:T(8,128)(2,1)S(1)}, s32[2]{0:T(128)S(1)}) custom-call(s32[1024]{0:T(1024)S(1)} %bitcast.72, s32[256]{0:T(256)S(1)} %get-tuple-element.120.edges, s32[65]{0:T(128)S(1)} %get-tuple-element.121.starts, ...), custom_call_target="tpu_custom_call" | custom-call | flops 33554432 | bytes 1048576 | tf_op jit(solution)/shard_map/prepare_4/pallas_call | solution.py:378
  124.3 10.5 %all-to-all-done.4 = bf16[64,2,32,128]{3,2,1,0:T(8,128)(2,1)S(1)} async-done(((bf16[64,2,32,128]{3,2,1,0:T(8,128)(2,1)}), bf16[64,2,32,128]{3,2,1,0:T(8,128)(2,1)S(1)}, u32[]{:S(2)}, u32[]{:S(2)}) %all-to-all-start.4) | async-done | bytes 1048608 | tf_op jit(solution)/shard_map/all_to_all | solution.py:402
  137.0 5.4 %all-to-all-start.5 = ((bf16[64,2,32,128]{3,2,1,0:T(8,128)(2,1)}), bf16[64,2,32,128]{3,2,1,0:T(8,128)(2,1)S(1)}, u32[]{:S(2)}, u32[]{:S(2)}) async-start(bf16[64,2,32,128]{3,2,1,0:T(8,128)(2,1)} %get-tuple-element.161), calls=%async_computation.5 | async-start | bytes 2097152 | tf_op jit(solution)/shard_map/all_to_all | solution.py:402
  142.4 4.4 %prepare_5.1 = (f32[16,32,128]{2,1,0:T(8,128)S(1)}, f32[2,32,128]{2,1,0:T(8,128)S(1)}, bf16[2,7,128,128]{3,2,1,0:T(8,128)(2,1)S(1)}, s32[2]{0:T(128)S(1)}) custom-call(s32[1024]{0:T(1024)S(1)} %bitcast.73, s32[256]{0:T(256)S(1)} %get-tuple-element.120.edges, s32[65]{0:T(128)S(1)} %get-tuple-element.121.starts, ...), custom_call_target="tpu_custom_call" | custom-call | flops 33554432 | bytes 1048576 | tf_op jit(solution)/shard_map/prepare_5/pallas_call | solution.py:378
  146.8 9.8 %all-to-all-done.5 = bf16[64,2,32,128]{3,2,1,0:T(8,128)(2,1)S(1)} async-done(((bf16[64,2,32,128]{3,2,1,0:T(8,128)(2,1)}), bf16[64,2,32,128]{3,2,1,0:T(8,128)(2,1)S(1)}, u32[]{:S(2)}, u32[]{:S(2)}) %all-to-all-start.5) | async-done | bytes 1048608 | tf_op jit(solution)/shard_map/all_to_all | solution.py:402
  156.5 2.6 solve_6.1
  159.2 4.7 %all-to-all-start.6 = ((bf16[64,2,32,128]{3,2,1,0:T(8,128)(2,1)}), bf16[64,2,32,128]{3,2,1,0:T(8,128)(2,1)S(1)}, u32[]{:S(2)}, u32[]{:S(2)}) async-start(bf16[64,2,32,128]{3,2,1,0:T(8,128)(2,1)} %get-tuple-element.168), calls=%async_computation.6 | async-start | bytes 2097152 | tf_op jit(solution)/shard_map/all_to_all | solution.py:402
  163.8 3.5 prepare_6.1
  167.4 10.3 %all-to-all-done.6 = bf16[64,2,32,128]{3,2,1,0:T(8,128)(2,1)S(1)} async-done(((bf16[64,2,32,128]{3,2,1,0:T(8,128)(2,1)}), bf16[64,2,32,128]{3,2,1,0:T(8,128)(2,1)S(1)}, u32[]{:S(2)}, u32[]{:S(2)}) %all-to-all-start.6) | async-done | bytes 1048608 | tf_op jit(solution)/shard_map/all_to_all | solution.py:402
  179.8 4.7 %all-to-all-start.7 = ((bf16[64,2,32,128]{3,2,1,0:T(8,128)(2,1)}), bf16[64,2,32,128]{3,2,1,0:T(8,128)(2,1)S(1)}, u32[]{:S(2)}, u32[]{:S(2)}) async-start(bf16[64,2,32,128]{3,2,1,0:T(8,128)(2,1)} %get-tuple-element.175), calls=%async_computation.7 | async-start | bytes 2097152 | tf_op jit(solution)/shard_map/all_to_all | solution.py:402
  184.5 4.2 %prepare_7.1 = (f32[16,32,128]{2,1,0:T(8,128)S(1)}, f32[2,32,128]{2,1,0:T(8,128)S(1)}, bf16[2,7,128,128]{3,2,1,0:T(8,128)(2,1)S(1)}, s32[2]{0:T(128)S(1)}) custom-call(s32[1024]{0:T(1024)S(1)} %bitcast.75, s32[256]{0:T(256)S(1)} %get-tuple-element.120.edges, s32[65]{0:T(128)S(1)} %get-tuple-element.121.starts, ...), custom_call_target="tpu_custom_call" | custom-call | flops 33554432 | bytes 1048576 | tf_op jit(solution)/shard_map/prepare_7/pallas_call | solution.py:378
  188.6 9.6 %all-to-all-done.7 = bf16[64,2,32,128]{3,2,1,0:T(8,128)(2,1)S(1)} async-done(((bf16[64,2,32,128]{3,2,1,0:T(8,128)(2,1)}), bf16[64,2,32,128]{3,2,1,0:T(8,128)(2,1)S(1)}, u32[]{:S(2)}, u32[]{:S(2)}) %all-to-all-start.7) | async-done | bytes 1048608 | tf_op jit(solution)/shard_map/all_to_all | solution.py:402
  198.2 2.6 solve_8.1
  200.8 4.7 %all-to-all-start.8 = ((bf16[64,2,32,128]{3,2,1,0:T(8,128)(2,1)}), bf16[64,2,32,128]{3,2,1,0:T(8,128)(2,1)S(1)}, u32[]{:S(2)}, u32[]{:S(2)}) async-start(bf16[64,2,32,128]{3,2,1,0:T(8,128)(2,1)} %get-tuple-element.182), calls=%async_computation.8 | async-start | bytes 2097152 | tf_op jit(solution)/shard_map/all_to_all | solution.py:402
  205.5 4.0 %prepare_8.1 = (f32[16,32,128]{2,1,0:T(8,128)S(1)}, f32[2,32,128]{2,1,0:T(8,128)S(1)}, bf16[2,7,128,128]{3,2,1,0:T(8,128)(2,1)S(1)}, s32[2]{0:T(128)S(1)}) custom-call(s32[1024]{0:T(1024)S(1)} %bitcast.76, s32[256]{0:T(256)S(1)} %get-tuple-element.120.edges, s32[65]{0:T(128)S(1)} %get-tuple-element.121.starts, ...), custom_call_target="tpu_custom_call" | custom-call | flops 33554432 | bytes 1048576 | tf_op jit(solution)/shard_map/prepare_8/pallas_call | solution.py:378
  209.6 9.6 %all-to-all-done.8 = bf16[64,2,32,128]{3,2,1,0:T(8,128)(2,1)S(1)} async-done(((bf16[64,2,32,128]{3,2,1,0:T(8,128)(2,1)}), bf16[64,2,32,128]{3,2,1,0:T(8,128)(2,1)S(1)}, u32[]{:S(2)}, u32[]{:S(2)}) %all-to-all-start.8) | async-done | bytes 1048608 | tf_op jit(solution)/shard_map/all_to_all | solution.py:402
  219.1 2.8 solve_9.1
  221.9 4.7 %all-to-all-start.9 = ((bf16[64,2,32,128]{3,2,1,0:T(8,128)(2,1)}), bf16[64,2,32,128]{3,2,1,0:T(8,128)(2,1)S(1)}, u32[]{:S(2)}, u32[]{:S(2)}) async-start(bf16[64,2,32,128]{3,2,1,0:T(8,128)(2,1)} %get-tuple-element.189), calls=%async_computation.9 | async-start | bytes 2097152 | tf_op jit(solution)/shard_map/all_to_all | solution.py:402
  226.6 2.6 prepare_9.1
  229.2 11.0 %all-to-all-done.9 = bf16[64,2,32,128]{3,2,1,0:T(8,128)(2,1)S(1)} async-done(((bf16[64,2,32,128]{3,2,1,0:T(8,128)(2,1)}), bf16[64,2,32,128]{3,2,1,0:T(8,128)(2,1)S(1)}, u32[]{:S(2)}, u32[]{:S(2)}) %all-to-all-start.9) | async-done | bytes 1048608 | tf_op jit(solution)/shard_map/all_to_all | solution.py:402
  242.6 4.7 %all-to-all-start.10 = ((bf16[64,2,32,128]{3,2,1,0:T(8,128)(2,1)}), bf16[64,2,32,128]{3,2,1,0:T(8,128)(2,1)S(1)}, u32[]{:S(2)}, u32[]{:S(2)}) async-start(bf16[64,2,32,128]{3,2,1,0:T(8,128)(2,1)} %get-tuple-element.196), calls=%async_computation.10 | async-start | bytes 2097152 | tf_op jit(solution)/shard_map/all_to_all | solution.py:402
  249.7 11.1 %all-to-all-done.10 = bf16[64,2,32,128]{3,2,1,0:T(8,128)(2,1)S(1)} async-done(((bf16[64,2,32,128]{3,2,1,0:T(8,128)(2,1)}), bf16[64,2,32,128]{3,2,1,0:T(8,128)(2,1)S(1)}, u32[]{:S(2)}, u32[]{:S(2)}) %all-to-all-start.10) | async-done | bytes 1048608 | tf_op jit(solution)/shard_map/all_to_all | solution.py:402
  260.8 2.7 solve_11.1
  263.5 4.7 %all-to-all-start.11 = ((bf16[64,2,32,128]{3,2,1,0:T(8,128)(2,1)}), bf16[64,2,32,128]{3,2,1,0:T(8,128)(2,1)S(1)}, u32[]{:S(2)}, u32[]{:S(2)}) async-start(bf16[64,2,32,128]{3,2,1,0:T(8,128)(2,1)} %get-tuple-element.203), calls=%async_computation.11 | async-start | bytes 2097152 | tf_op jit(solution)/shard_map/all_to_all | solution.py:402
  268.2 2.8 prepare_11.1
  271.0 10.8 %all-to-all-done.11 = bf16[64,2,32,128]{3,2,1,0:T(8,128)(2,1)S(1)} async-done(((bf16[64,2,32,128]{3,2,1,0:T(8,128)(2,1)}), bf16[64,2,32,128]{3,2,1,0:T(8,128)(2,1)S(1)}, u32[]{:S(2)}, u32[]{:S(2)}) %all-to-all-start.11) | async-done | bytes 1048608 | tf_op jit(solution)/shard_map/all_to_all | solution.py:402
  283.8 4.9 %all-to-all-start.12 = ((bf16[64,2,32,128]{3,2,1,0:T(8,128)(2,1)}), bf16[64,2,32,128]{3,2,1,0:T(8,128)(2,1)S(1)}, u32[]{:S(2)}, u32[]{:S(2)}) async-start(bf16[64,2,32,128]{3,2,1,0:T(8,128)(2,1)} %get-tuple-element.210), calls=%async_computation.12 | async-start | bytes 2097152 | tf_op jit(solution)/shard_map/all_to_all | solution.py:402
  291.2 11.1 %all-to-all-done.12 = bf16[64,2,32,128]{3,2,1,0:T(8,128)(2,1)S(1)} async-done(((bf16[64,2,32,128]{3,2,1,0:T(8,128)(2,1)}), bf16[64,2,32,128]{3,2,1,0:T(8,128)(2,1)S(1)}, u32[]{:S(2)}, u32[]{:S(2)}) %all-to-all-start.12) | async-done | bytes 1048608 | tf_op jit(solution)/shard_map/all_to_all | solution.py:402
  304.3 4.9 %all-to-all-start.13 = ((bf16[64,2,32,128]{3,2,1,0:T(8,128)(2,1)}), bf16[64,2,32,128]{3,2,1,0:T(8,128)(2,1)S(1)}, u32[]{:S(2)}, u32[]{:S(2)}) async-start(bf16[64,2,32,128]{3,2,1,0:T(8,128)(2,1)} %get-tuple-element.217), calls=%async_computation.13 | async-start | bytes 2097152 | tf_op jit(solution)/shard_map/all_to_all | solution.py:402
  311.6 11.1 %all-to-all-done.13 = bf16[64,2,32,128]{3,2,1,0:T(8,128)(2,1)S(1)} async-done(((bf16[64,2,32,128]{3,2,1,0:T(8,128)(2,1)}), bf16[64,2,32,128]{3,2,1,0:T(8,128)(2,1)S(1)}, u32[]{:S(2)}, u32[]{:S(2)}) %all-to-all-start.13) | async-done | bytes 1048608 | tf_op jit(solution)/shard_map/all_to_all | solution.py:402
  325.3 4.7 %all-to-all-start.14 = ((bf16[64,2,32,128]{3,2,1,0:T(8,128)(2,1)}), bf16[64,2,32,128]{3,2,1,0:T(8,128)(2,1)S(1)}, u32[]{:S(2)}, u32[]{:S(2)}) async-start(bf16[64,2,32,128]{3,2,1,0:T(8,128)(2,1)} %get-tuple-element.226), calls=%async_computation.14 | async-start | bytes 2097152 | tf_op jit(solution)/shard_map/all_to_all | solution.py:402
  332.9 10.6 %all-to-all-done.14 = bf16[64,2,32,128]{3,2,1,0:T(8,128)(2,1)S(1)} async-done(((bf16[64,2,32,128]{3,2,1,0:T(8,128)(2,1)}), bf16[64,2,32,128]{3,2,1,0:T(8,128)(2,1)S(1)}, u32[]{:S(2)}, u32[]{:S(2)}) %all-to-all-start.14) | async-done | bytes 1048608 | tf_op jit(solution)/shard_map/all_to_all | solution.py:402
  345.0 16.4 %collective-permute-start.5 = (bf16[8,32,128]{2,1,0:T(8,128)(2,1)S(1)}, bf16[8,32,128]{2,1,0:T(8,128)(2,1)S(1)}, u32[]{:S(2)}, u32[]{:S(2)}) collective-permute-start(bf16[8,32,128]{2,1,0:T(8,128)(2,1)S(1)} %get-tuple-element.228), channel_id=1, source_target_pairs={{0,1},{1,0},{2,3},{3,2},{4,5},{5,4},{6,7},{7,6},{8,9},{9,8},{10,11... | collective-permute-start | bytes 196616 | tf_op jit(solution)/shard_map/ppermute | solution.py:368
  (46 shorter events, 45.9 us)
Async XLA Ops:
  0.0 48.3 %copy-start.2 = (bf16[8,1,128,128]{3,2,1,0:T(8,128)(2,1)S(1)}, bf16[8,1,128,128]{3,2,1,0:T(8,128)(2,1)}, u32[]{:S(2)}) copy-start(bf16[8,1,128,128]{3,2,1,0:T(8,128)(2,1)} %param.8) | copy-start | bytes 786436
  0.0 48.3 %copy-start.5 = (s32[8,128]{1,0:T(8,128)S(1)}, s32[8,128]{1,0:T(8,128)}, u32[]{:S(2)}) copy-start(s32[8,128]{1,0:T(8,128)} %param.11) | copy-start | bytes 12292
  0.0 3.8 %collective-permute-start.1 = (bf16[8,128,128]{2,1,0:T(8,128)(2,1)}, bf16[8,128,128]{2,1,0:T(8,128)(2,1)S(1)}, u32[]{:S(2)}, u32[]{:S(2)}) collective-permute-start(bf16[8,128,128]{2,1,0:T(8,128)(2,1)} %bitcast.34), channel_id=1, source_target_pairs={{0,1},{1,0},{2,3},{3,2},{4,5},{5,4},{6,7},{7,6},{8,9},{9,8},{10,11... | collective-permute-start | bytes 786440 | tf_op jit(solution)/shard_map/ppermute | solution.py:368
  2.4 1.4 collective-permute-start
  3.8 1.0 copy-start
  4.8 0.7 copy-start.3
  7.5 21.7 %collective-permute-start.4 = (bf16[8,16,128,128]{3,2,1,0:T(8,128)(2,1)}, bf16[8,16,128,128]{3,2,1,0:T(8,128)(2,1)}, u32[]{:S(2)}, u32[]{:S(2)}) collective-permute-start(bf16[8,16,128,128]{3,2,1,0:T(8,128)(2,1)} %bitcast.85), channel_id=1, source_target_pairs={{0,1},{1,0},{2,3},{3,2},{4,5},{5,4},{6,7},{7,6},{8,9},{9,8},{10,11... | collective-permute-start | bytes 12582920 | tf_op jit(solution)/shard_map/ppermute | solution.py:368
  7.8 29.3 %all-to-all-start = ((bf16[64,2,32,128]{3,2,1,0:T(8,128)(2,1)}), bf16[64,2,32,128]{3,2,1,0:T(8,128)(2,1)S(1)}, u32[]{:S(2)}, u32[]{:S(2)}) async-start(bf16[64,2,32,128]{3,2,1,0:T(8,128)(2,1)} %get-tuple-element.126), calls=%async_computation | async-start | bytes 2097152 | tf_op jit(solution)/shard_map/all_to_all | solution.py:402
  19.0 1.7 collective-permute-start.3
  19.7 1.7 collective-permute-start.2
  22.2 0.7 copy-start.4
  29.2 1.0 copy-start.1
  43.6 21.6 %all-to-all-start.1 = ((bf16[64,2,32,128]{3,2,1,0:T(8,128)(2,1)}), bf16[64,2,32,128]{3,2,1,0:T(8,128)(2,1)S(1)}, u32[]{:S(2)}, u32[]{:S(2)}) async-start(bf16[64,2,32,128]{3,2,1,0:T(8,128)(2,1)} %get-tuple-element.133), calls=%async_computation.1 | async-start | bytes 2097152 | tf_op jit(solution)/shard_map/all_to_all | solution.py:402
  68.4 21.1 %all-to-all-start.2 = ((bf16[64,2,32,128]{3,2,1,0:T(8,128)(2,1)}), bf16[64,2,32,128]{3,2,1,0:T(8,128)(2,1)S(1)}, u32[]{:S(2)}, u32[]{:S(2)}) async-start(bf16[64,2,32,128]{3,2,1,0:T(8,128)(2,1)} %get-tuple-element.140), calls=%async_computation.2 | async-start | bytes 2097152 | tf_op jit(solution)/shard_map/all_to_all | solution.py:402
  91.6 21.1 %all-to-all-start.3 = ((bf16[64,2,32,128]{3,2,1,0:T(8,128)(2,1)}), bf16[64,2,32,128]{3,2,1,0:T(8,128)(2,1)S(1)}, u32[]{:S(2)}, u32[]{:S(2)}) async-start(bf16[64,2,32,128]{3,2,1,0:T(8,128)(2,1)} %get-tuple-element.147), calls=%async_computation.3 | async-start | bytes 2097152 | tf_op jit(solution)/shard_map/all_to_all | solution.py:402
  114.9 20.0 %all-to-all-start.4 = ((bf16[64,2,32,128]{3,2,1,0:T(8,128)(2,1)}), bf16[64,2,32,128]{3,2,1,0:T(8,128)(2,1)S(1)}, u32[]{:S(2)}, u32[]{:S(2)}) async-start(bf16[64,2,32,128]{3,2,1,0:T(8,128)(2,1)} %get-tuple-element.154), calls=%async_computation.4 | async-start | bytes 2097152 | tf_op jit(solution)/shard_map/all_to_all | solution.py:402
  137.0 19.5 %all-to-all-start.5 = ((bf16[64,2,32,128]{3,2,1,0:T(8,128)(2,1)}), bf16[64,2,32,128]{3,2,1,0:T(8,128)(2,1)S(1)}, u32[]{:S(2)}, u32[]{:S(2)}) async-start(bf16[64,2,32,128]{3,2,1,0:T(8,128)(2,1)} %get-tuple-element.161), calls=%async_computation.5 | async-start | bytes 2097152 | tf_op jit(solution)/shard_map/all_to_all | solution.py:402
  159.2 18.5 %all-to-all-start.6 = ((bf16[64,2,32,128]{3,2,1,0:T(8,128)(2,1)}), bf16[64,2,32,128]{3,2,1,0:T(8,128)(2,1)S(1)}, u32[]{:S(2)}, u32[]{:S(2)}) async-start(bf16[64,2,32,128]{3,2,1,0:T(8,128)(2,1)} %get-tuple-element.168), calls=%async_computation.6 | async-start | bytes 2097152 | tf_op jit(solution)/shard_map/all_to_all | solution.py:402
  179.8 18.4 %all-to-all-start.7 = ((bf16[64,2,32,128]{3,2,1,0:T(8,128)(2,1)}), bf16[64,2,32,128]{3,2,1,0:T(8,128)(2,1)S(1)}, u32[]{:S(2)}, u32[]{:S(2)}) async-start(bf16[64,2,32,128]{3,2,1,0:T(8,128)(2,1)} %get-tuple-element.175), calls=%async_computation.7 | async-start | bytes 2097152 | tf_op jit(solution)/shard_map/all_to_all | solution.py:402
  200.8 18.3 %all-to-all-start.8 = ((bf16[64,2,32,128]{3,2,1,0:T(8,128)(2,1)}), bf16[64,2,32,128]{3,2,1,0:T(8,128)(2,1)S(1)}, u32[]{:S(2)}, u32[]{:S(2)}) async-start(bf16[64,2,32,128]{3,2,1,0:T(8,128)(2,1)} %get-tuple-element.182), calls=%async_computation.8 | async-start | bytes 2097152 | tf_op jit(solution)/shard_map/all_to_all | solution.py:402
  221.9 18.3 %all-to-all-start.9 = ((bf16[64,2,32,128]{3,2,1,0:T(8,128)(2,1)}), bf16[64,2,32,128]{3,2,1,0:T(8,128)(2,1)S(1)}, u32[]{:S(2)}, u32[]{:S(2)}) async-start(bf16[64,2,32,128]{3,2,1,0:T(8,128)(2,1)} %get-tuple-element.189), calls=%async_computation.9 | async-start | bytes 2097152 | tf_op jit(solution)/shard_map/all_to_all | solution.py:402
  242.6 18.2 %all-to-all-start.10 = ((bf16[64,2,32,128]{3,2,1,0:T(8,128)(2,1)}), bf16[64,2,32,128]{3,2,1,0:T(8,128)(2,1)S(1)}, u32[]{:S(2)}, u32[]{:S(2)}) async-start(bf16[64,2,32,128]{3,2,1,0:T(8,128)(2,1)} %get-tuple-element.196), calls=%async_computation.10 | async-start | bytes 2097152 | tf_op jit(solution)/shard_map/all_to_all | solution.py:402
  263.5 18.2 %all-to-all-start.11 = ((bf16[64,2,32,128]{3,2,1,0:T(8,128)(2,1)}), bf16[64,2,32,128]{3,2,1,0:T(8,128)(2,1)S(1)}, u32[]{:S(2)}, u32[]{:S(2)}) async-start(bf16[64,2,32,128]{3,2,1,0:T(8,128)(2,1)} %get-tuple-element.203), calls=%async_computation.11 | async-start | bytes 2097152 | tf_op jit(solution)/shard_map/all_to_all | solution.py:402
  283.8 18.4 %all-to-all-start.12 = ((bf16[64,2,32,128]{3,2,1,0:T(8,128)(2,1)}), bf16[64,2,32,128]{3,2,1,0:T(8,128)(2,1)S(1)}, u32[]{:S(2)}, u32[]{:S(2)}) async-start(bf16[64,2,32,128]{3,2,1,0:T(8,128)(2,1)} %get-tuple-element.210), calls=%async_computation.12 | async-start | bytes 2097152 | tf_op jit(solution)/shard_map/all_to_all | solution.py:402
  304.3 18.4 %all-to-all-start.13 = ((bf16[64,2,32,128]{3,2,1,0:T(8,128)(2,1)}), bf16[64,2,32,128]{3,2,1,0:T(8,128)(2,1)S(1)}, u32[]{:S(2)}, u32[]{:S(2)}) async-start(bf16[64,2,32,128]{3,2,1,0:T(8,128)(2,1)} %get-tuple-element.217), calls=%async_computation.13 | async-start | bytes 2097152 | tf_op jit(solution)/shard_map/all_to_all | solution.py:402
  325.3 18.2 %all-to-all-start.14 = ((bf16[64,2,32,128]{3,2,1,0:T(8,128)(2,1)}), bf16[64,2,32,128]{3,2,1,0:T(8,128)(2,1)S(1)}, u32[]{:S(2)}, u32[]{:S(2)}) async-start(bf16[64,2,32,128]{3,2,1,0:T(8,128)(2,1)} %get-tuple-element.226), calls=%async_computation.14 | async-start | bytes 2097152 | tf_op jit(solution)/shard_map/all_to_all | solution.py:402
  345.0 17.3 %collective-permute-start.5 = (bf16[8,32,128]{2,1,0:T(8,128)(2,1)S(1)}, bf16[8,32,128]{2,1,0:T(8,128)(2,1)S(1)}, u32[]{:S(2)}, u32[]{:S(2)}) collective-permute-start(bf16[8,32,128]{2,1,0:T(8,128)(2,1)S(1)} %get-tuple-element.228), channel_id=1, source_target_pairs={{0,1},{1,0},{2,3},{3,2},{4,5},{5,4},{6,7},{7,6},{8,9},{9,8},{10,11... | collective-permute-start | bytes 196616 | tf_op jit(solution)/shard_map/ppermute | solution.py:368
